TPU v7x, 32 devices: a whole 2x2x4 slice. The times are simulated.
32 devices in a mesh: ctx: 8 (over z, core), ch: 4 (over y, x).
Axes of the slice: x: 2, y: 2, z: 4, core: 2. Of those that a mesh axis runs over, the one named last changes fastest.
Arguments:
- features: bfloat16 [3, 2048, 8192], P(None, 'ctx', 'ch'), may hold values from -6 to 6
- short_filter: float32 [3, 7, 8192], P(None, None, 'ch'), may hold values from -4 to 4
- long_filter: float32 [512, 128], P('ch'), may hold values from -0.5 to 0.5
- cotangent: bfloat16 [2048, 8192], P('ctx', 'ch'), may hold values from -15 to 15
Outputs:
- grad_features: bfloat16 [3, 2048, 8192], P(None, 'ctx', 'ch')
- grad_short: float32 [3, 7, 8192], P(None, None, 'ch')
- grad_long: float32 [512, 128], P('ch')
All inputs are finite; a program needn't handle non-finite values.
Results may differ from a plain program's by a relative error of at most 0.0057.
Values may be sent and summed in bfloat16 or wider, within the bound.
No kernel may reach another device: no remote copies, remote signals or barrier semaphores. Data moves between devices by JAX's collectives and lax.ppermute only.
A program may use at most 128 MiB of HBM per device.

v0:
```python
import jax
import jax.numpy as jnp
from jax import lax
from jax.sharding import PartitionSpec as P

D = 8192
G = 512


def from_behind(block, axis, distance):
    devices = range(lax.axis_size(axis))
    route = [(i - distance, i) for i in devices if i - distance in devices]
    return lax.ppermute(block, axis, route)


def short_conv(extended, filt, count):
    taps = filt.shape[0]
    total = jnp.zeros((count, extended.shape[1]), jnp.float32)
    for tap in range(taps):
        start = taps - 1 - tap
        total = total + filt[tap] * extended[start : start + count].astype(jnp.float32)
    return total


def short_adjoint(grad, filt):
    taps = filt.shape[0]
    count = grad.shape[0]
    edge = jnp.zeros((taps - 1, grad.shape[1]), jnp.float32)
    padded = jnp.concatenate([edge, grad, edge], 0)
    total = jnp.zeros((count + taps - 1, grad.shape[1]), jnp.float32)
    for tap in range(taps):
        total = total + filt[tap] * padded[tap : tap + count + taps - 1]
    return total


def filter_grad(grad, extended, taps):
    count = grad.shape[0]
    pieces = []
    for tap in range(taps):
        start = taps - 1 - tap
        pieces.append(jnp.sum(grad * extended[start : start + count].astype(jnp.float32), 0))
    return jnp.stack(pieces)


def toeplitz(long_filter):
    groups, span = long_filter.shape
    rounded = long_filter.astype(jnp.bfloat16)
    line = jnp.concatenate(
        [
            jnp.zeros((groups, 1), jnp.bfloat16),
            rounded[:, ::-1],
            jnp.zeros((groups, 2 * span - 1), jnp.bfloat16),
        ],
        1,
    )
    flat = jnp.tile(line, (1, span))[:, : span * (3 * span - 1)]
    return flat.reshape(groups, span, 3 * span - 1)[:, :, : 2 * span]


def time_last(values, groups, span):
    count = values.shape[0] // span
    width = values.shape[1]
    turned = jnp.transpose(values.reshape(count, span, width), (0, 2, 1))
    return turned.reshape(count, groups, width // groups, span)


def time_first(blocked):
    count, groups, members, span = blocked.shape
    turned = jnp.transpose(blocked.reshape(count, groups * members, span), (0, 2, 1))
    return turned.reshape(count * span, groups * members)


def long_forward(z_pad, matrix, groups, span):
    blocks = time_last(z_pad, groups, span)
    lower = jnp.einsum(
        "bgcs,gts->bgct", blocks[:-1], matrix[:, :, :span], preferred_element_type=jnp.float32
    )
    upper = jnp.einsum(
        "bgcs,gts->bgct", blocks[1:], matrix[:, :, span:], preferred_element_type=jnp.float32
    )
    return time_first(lower + upper)


def long_adjoint(grad_y, matrix, groups, span):
    blocks = time_last(grad_y, groups, span)
    lower = jnp.einsum(
        "bgct,gts->bgcs", blocks, matrix[:, :, :span], preferred_element_type=jnp.float32
    )
    upper = jnp.einsum(
        "bgct,gts->bgcs", blocks, matrix[:, :, span:], preferred_element_type=jnp.float32
    )
    zero = jnp.zeros((1,) + lower.shape[1:], jnp.float32)
    total = jnp.concatenate([lower, zero], 0) + jnp.concatenate([zero, upper], 0)
    return time_first(total)


def long_filter_grad(grad_y, z_pad, groups, span):
    blocks = time_last(grad_y, groups, span)
    z_blocks = time_last(z_pad, groups, span)
    lower = jnp.einsum("bgct,bgcs->gts", blocks, z_blocks[:-1], preferred_element_type=jnp.float32)
    upper = jnp.einsum("bgct,bgcs->gts", blocks, z_blocks[1:], preferred_element_type=jnp.float32)
    inner = jnp.concatenate([lower, upper], 2)
    flat = jnp.concatenate(
        [inner.reshape(groups, span * 2 * span), jnp.zeros((groups, span), jnp.float32)], 1
    )
    skewed = flat.reshape(groups, span, 2 * span + 1)
    columns = jnp.sum(skewed, 1)
    return columns[:, 1 : span + 1][:, ::-1]


def add_tail(own, later):
    cut = own.shape[0] - later.shape[0]
    return jnp.concatenate([own[:cut], own[cut:] + later], 0)


def on_device(features, short_filter, long_filter, cotangent):
    rows = features.shape[1]
    width = features.shape[2]
    taps = short_filter.shape[1]
    groups, span = long_filter.shape
    reach = span + taps - 2
    earlier = from_behind(features[:, rows - reach :], "ctx", 1)
    q_prior = earlier[0, reach - (taps - 1) :]
    kv_prior = earlier[1:]
    q_ext = jnp.concatenate([q_prior, features[0]], 0)
    k_ext = jnp.concatenate([kv_prior[0], features[1]], 0)
    v_ext = jnp.concatenate([kv_prior[1], features[2]], 0)
    q_short = short_conv(q_ext, short_filter[0], rows)
    k_short = short_conv(k_ext, short_filter[1], rows + span - 1)
    v_short = short_conv(v_ext, short_filter[2], rows + span - 1)
    gated = (k_short * v_short).astype(jnp.bfloat16)
    z_pad = jnp.concatenate([jnp.zeros((1, width), jnp.bfloat16), gated], 0)
    matrix = toeplitz(long_filter)
    y_long = long_forward(z_pad, matrix, groups, span)
    cot = cotangent.astype(jnp.float32)
    grad_y = (cot * q_short).astype(jnp.bfloat16)
    grad_q_short = cot * y_long
    raw_long = long_filter_grad(grad_y, z_pad, groups, span)
    raw_q = filter_grad(grad_q_short, q_ext, taps)
    grad_z = long_adjoint(grad_y, matrix, groups, span)[1:]
    grad_k_short = grad_z * v_short
    grad_v_short = grad_z * k_short
    k_part = short_adjoint(grad_k_short, short_filter[1])
    v_part = short_adjoint(grad_v_short, short_filter[2])
    q_part = short_adjoint(grad_q_short, short_filter[0])
    raw_k = filter_grad(grad_k_short, k_ext, taps)
    raw_v = filter_grad(grad_v_short, v_ext, taps)
    later_kv, later_q = (
        from_behind(
            jnp.stack([k_part[:reach], v_part[:reach]]).astype(jnp.bfloat16), "ctx", -1
        ).astype(jnp.float32),
        from_behind(q_part[: taps - 1].astype(jnp.bfloat16), "ctx", -1).astype(jnp.float32),
    )
    grad_q = add_tail(q_part[taps - 1 :], later_q)
    grad_k = add_tail(k_part[reach:], later_kv[0])
    grad_v = add_tail(v_part[reach:], later_kv[1])
    raw_short = jnp.stack([raw_q, raw_k, raw_v])
    raw_short, raw_long = lax.psum((raw_short, raw_long), "ctx")
    local_square = jnp.sum(raw_short * raw_short) + jnp.sum(raw_long * raw_long)
    total_square = lax.psum(local_square, "ch")
    mean_square = total_square / (3 * taps * D + span * G)
    factor = lax.rsqrt(mean_square + 1e-06)
    grads = jnp.stack([grad_q, grad_k, grad_v]).astype(jnp.bfloat16)
    return (grads, raw_short * factor, raw_long * factor)


def solution(mesh):
    in_specs = (P(None, "ctx", "ch"), P(None, None, "ch"), P("ch", None), P("ctx", "ch"))
    out_specs = (P(None, "ctx", "ch"), P(None, None, "ch"), P("ch", None))
    return jax.shard_map(
        on_device, mesh=mesh, in_specs=in_specs, out_specs=out_specs, check_vma=False
    )
```

profile of v0, /device:TPU:0, one launch (start us, length us, event | category | flops | bytes accessed | tf_op | source)
XLA Modules:
  0.0 306.2 jit_solution(170825385856445952)
XLA Ops:
  7.2 3.1 %slice.379 = bf16[3,133,2048]{2,1,0:T(8,128)(2,1)} slice(bf16[3,256,2048]{2,1,0:T(8,128)(2,1)} %param.4), slice={[0:3], [123:256], [0:2048]} | slice | bytes 3268608 | tf_op jit(solution)/shard_map/slice | solution.py:122
  10.3 3.7 %collective-permute-start = (bf16[3,133,2048]{2,1,0:T(8,128)(2,1)}, bf16[3,133,2048]{2,1,0:T(8,128)(2,1)}, u32[]{:S(2)}, u32[]{:S(2)}) collective-permute-start(bf16[3,133,2048]{2,1,0:T(8,128)(2,1)} %slice.379), channel_id=1, source_target_pairs={{0,4},{4,8},{8,12},{12,16},{16,20},{20,24},{24,28},{1,5},{5,9},{9,... | collective-permute-start | bytes 4902920 | tf_op jit(solution)/shard_map/ppermute | solution.py:13
  14.3 5.7 %tile.4 = bf16[128,128,384]{2,1,0:T(8,128)(2,1)} broadcast(bf16[128,384]{1,0:T(8,128)(2,1)S(1)} %maximum_maximum_fusion), dimensions={0,2} | broadcast | bytes 12681216 | tf_op jit(solution)/shard_map/tile | solution.py:56
  19.9 12.5 %copy.47 = bf16[16,8,128,384]{3,1,2,0:T(8,128)(2,1)S(1)} copy(bf16[16,8,128,384]{3,2,1,0:T(8,128)(2,1)} %bitcast.139) | data formatting | bytes 25165824
  32.4 5.2 %slice.458 = bf16[128,49024]{1,0:T(8,128)(2,1)} slice(bf16[128,49152]{1,0:T(8,128)(2,1)S(1)} %bitcast.140), slice={[0:128], [0:49024]} | slice | bytes 25100288 | tf_op jit(solution)/shard_map/slice | solution.py:56
  37.6 31.0 %reshape.89 = bf16[128,128,383]{2,1,0:T(8,128)(2,1)} reshape(bf16[128,49024]{1,0:T(8,128)(2,1)} %slice.458) | data formatting | bytes 25100288 | tf_op jit(solution)/shard_map/reshape | solution.py:57
  68.6 0.1 fusion.99
  68.8 1.6 slice_bitcast_fusion.16
  70.3 0.9 slice_bitcast_fusion.21
  71.2 2.1 fusion.48
  73.3 0.7 copy.36
  74.0 3.5 %fusion.62 = f32[2,128,16,128]{3,2,0,1:T(8,128)S(1)} fusion(bf16[128,128,383]{2,1,0:T(8,128)(2,1)} %reshape.89, bf16[2,128,16,128]{3,2,1,0:T(8,128)(2,1)S(1)} %bitcast.141), kind=kOutput, calls=%fused_computation.166 | convolution fusion | flops 134217728 | bytes 7340032 | tf_op jit(solution)/shard_map/bgct,gts->bgcs/dot_general | solution.py:89
  77.5 3.4 %fusion.63 = f32[2,128,16,128]{3,2,0,1:T(8,128)S(1)} fusion(bf16[128,128,383]{2,1,0:T(8,128)(2,1)} %reshape.89, bf16[2,128,16,128]{3,2,1,0:T(8,128)(2,1)S(1)} %bitcast.142), kind=kOutput, calls=%fused_computation.167 | convolution fusion | flops 134217728 | bytes 7340032 | tf_op jit(solution)/shard_map/bgct,gts->bgcs/dot_general | solution.py:86
  80.9 0.4 pad_add_fusion
  81.3 1.9 copy.39
  83.2 3.7 %copy.40 = f32[3,128,2048]{2,1,0:T(8,128)} copy(f32[3,128,2048]{1,2,0:T(8,128)} %bitcast.151) | data formatting | bytes 6291456 | tf_op jit(solution)/shard_map/transpose | solution.py:69
  86.9 1.3 slice_bitcast_fusion.20
  88.2 9.5 %fusion.41 = (f32[2048]{0:T(1024)S(1)}, f32[2048]{0:T(1024)S(1)}, f32[2048]{0:T(1024)S(1)}, f32[2048]{0:T(1024)S(1)}, f32[2048]{0:T(1024)S(1)}, /*index=5*/f32[2...) fusion(bf16[256,2048]{1,0:T(8,128)(2,1)S(1)} %copy-done.5, ...), kind=kLoop, calls=%fused_computation.100 | loop fusion | flops 65873920 | bytes 12713984 | tf_op jit(solution)/shard_map/reduce_sum | solution.py:41
  97.8 7.4 %fusion.28 = (f32[2048]{0:T(1024)S(1)}, f32[2048]{0:T(1024)S(1)}, f32[2048]{0:T(1024)S(1)}, f32[2048]{0:T(1024)S(1)}, f32[2048]{0:T(1024)S(1)}, /*index=5*/f32[2...) fusion(bf16[256,2048]{1,0:T(8,128)(2,1)S(1)} %copy-done.4, ...), kind=kLoop, calls=%fused_computation.87 | loop fusion | flops 65873920 | bytes 12713984 | tf_op jit(solution)/shard_map/reduce_sum | solution.py:41
  105.2 0.7 multiply_convert_fusion
  105.8 0.4 concatenate.69
  106.2 1.3 fusion.98
  107.5 0.7 copy.32
  108.1 1.8 copy.30
  109.9 4.5 %fusion.13 = f32[128,128,2,16]{1,3,2,0:T(8,128)S(1)} fusion(bf16[128,128,383]{2,1,0:T(8,128)(2,1)} %reshape.89, bf16[2,128,16,128]{3,2,1,0:T(8,128)(2,1)S(1)} %bitcast.149), kind=kOutput, calls=%fused_computation.72 | convolution fusion | flops 134217728 | bytes 7340032 | tf_op jit(solution)/shard_map/bgcs,gts->bgct/dot_general | solution.py:75
  114.4 4.6 %add_bitcast_fusion = f32[2,128,16,128]{3,2,0,1:T(8,128)S(1)} fusion(f32[128,128,2,16]{1,3,2,0:T(8,128)S(1)} %fusion.13, bf16[128,128,383]{2,1,0:T(8,128)(2,1)} %reshape.89, bf16[2,128,16,128]{3,2,1,0:T(8,128)(2,1)S(1)} %bitcast.147), kind=kOutput, calls=%fused_computation.153 | convolution fusion | flops 134742016 | bytes 9437184 | tf_op jit(solution)/shard_map/bgcs,gts->bgct/dot_general | solution.py:78
  119.0 1.5 copy.34
  120.5 2.9 copy.35
  123.4 6.4 %fusion.61 = (f32[2048]{0:T(1024)S(1)}, f32[2048]{0:T(1024)S(1)}, f32[2048]{0:T(1024)S(1)}, f32[2048]{0:T(1024)S(1)}, f32[2048]{0:T(1024)S(1)}, /*index=5*/f32[2...) fusion(bf16[256,2048]{1,0:T(8,128)(2,1)} %copy-done.6, bf16[6,2048]{1,0:T(8,128)(2,1)S(1)} %slice_bitcast_fusion.21, ...), kind=kLoop, calls=%fused_computation.152 | loop fusion | flops 21481472 | bytes 7421952 | tf_op jit(solution)/shard_map/reduce_sum | solution.py:41
  129.9 0.2 pad_maximum_fusion.6
  130.1 2.8 fusion.92
  133.0 1.2 slice.494
  134.3 1.4 pad_maximum_fusion.2
  135.6 3.9 %fusion.94 = (bf16[389,2048]{1,0:T(8,128)(2,1)S(1)}, f32[389,2048]{1,0:T(8,128)}) fusion(f32[383,2048]{1,0:T(8,128)S(1)} %copy-done.1, f32[2048]{0:T(1024)S(1)} %bitcast.173, f32[395,2048]{1,0:T(8,128)S(1)} %get-tuple-element.70, f32[2048]{0:T(1024)S(1)} %bitcast.175, f32[2048]{0:T(1024)S(1)} %bitcast.177, f32[2048]{0:T(1024)S(1)} %bitcast.179, ...), kind=kLoop, calls=%fused_computation.220 | loop fusion | flops 11153408 | bytes 23908352 | tf_op jit(solution)/shard_map/convert.10
  139.5 1.0 slice.514
  140.5 3.9 %fusion.96 = (bf16[389,2048]{1,0:T(8,128)(2,1)S(1)}, f32[389,2048]{1,0:T(8,128)}) fusion(f32[383,2048]{1,0:T(8,128)S(1)} %copy-done, f32[2048]{0:T(1024)S(1)} %bitcast.161, f32[395,2048]{1,0:T(8,128)S(1)} %get-tuple-element.71, f32[2048]{0:T(1024)S(1)} %bitcast.163, f32[2048]{0:T(1024)S(1)} %bitcast.165, f32[2048]{0:T(1024)S(1)} %bitcast.167, ...), kind=kLoop, calls=%fused_computation.221 | loop fusion | flops 11153408 | bytes 23908352 | tf_op jit(solution)/shard_map/convert.18
  144.3 0.1 slice_bitcast_fusion.17
  144.5 0.9 slice.524
  145.4 1.3 convolution_bitcast_fusion
  146.7 1.3 convolution_bitcast_fusion.1
  148.0 1.3 collective-permute-start.1
  149.4 2.1 copy.41
  151.6 1.4 collective-permute-start.2
  153.0 6.2 %pad_maximum_fusion = f32[128,128,256]{1,2,0:T(8,128)} fusion(f32[128,128,128]{1,2,0:T(8,128)S(1)} %convolution_bitcast_fusion, f32[128,128,128]{1,2,0:T(8,128)S(1)} %convolution_bitcast_fusion.1), kind=kLoop, calls=%fused_computation | loop fusion | flops 4194304 | bytes 33554432 | tf_op jit(solution)/shard_map/concatenate | solution.py:102
  159.5 0.7 pad_maximum_fusion.11
  160.2 17.6 %copy.43 = f32[128,128,256]{0,2,1:T(8,128)} copy(f32[128,128,256]{1,2,0:T(8,128)} %pad_maximum_fusion) | data formatting | bytes 33554432 | tf_op jit(solution)/shard_map/concatenate | solution.py:102
  177.8 13.3 %concatenate.86 = f32[128,32896]{0,1:T(8,128)} pad(f32[128,32768]{0,1:T(8,128)} %bitcast.138, f32[]{:T(128)} %constant.5.clone.1), padding=0_0x0_128 | pad | bytes 33619972 | tf_op jit(solution)/shard_map/concatenate | solution.py:103
  191.1 17.5 %reshape.98 = f32[128,128,257]{0,2,1:T(8,128)} reshape(f32[128,32896]{0,1:T(8,128)} %concatenate.86) | data formatting | bytes 33685504 | tf_op jit(solution)/shard_map/reshape | solution.py:106
  208.6 6.8 %reduce_sum.238 = f32[128,257]{0,1:T(8,128)S(1)} reduce(f32[128,128,257]{0,2,1:T(8,128)} %reshape.98, f32[]{:T(128)} %constant.5.clone.1), dimensions={1}, to_apply=%region_23.0 | reduce | flops 4177792 | bytes 16974340 | tf_op jit(solution)/shard_map/reduce_sum | solution.py:107
  215.4 0.6 rev.7
  216.1 0.9 fusion.89
  216.9 59.0 %all-reduce.13.cloned.1.call-done = (f32[3,7,2048]{2,1,0:T(8,128)}, f32[128,128]{0,1:T(8,128)}) async-done(((f32[3,7,2048]{2,1,0:T(8,128)}, f32[128,128]{0,1:T(8,128)}), (f32[3,7,2048]{2,1,0:T(8,128)}, f32[128,128]{0,1:T(8,128)})) %all-reduce.13.cloned.1.call-update) | async-done | bytes 237584 | tf_op jit(solution)/shard_map/psum | solution.py:158
  275.9 1.5 multiply_reduce_fusion.1
  277.4 1.6 multiply_reduce_fusion
  280.3 0.1 maximum_bitcast_fusion
  280.4 10.3 %psum.23 = f32[]{:T(128)} all-reduce(f32[]{:T(128)S(6)} %add.200), channel_id=1, replica_groups=mesh['ctx'=8,'ch'=4] {'ch'}, use_global_device_ids=true, to_apply=%region_26.0 | all-reduce | flops 1 | bytes 8 | tf_op jit(solution)/shard_map/psum | solution.py:160
  291.4 0.8 broadcast_multiply_fusion.1
  292.3 0.7 copy.44
  293.0 1.6 broadcast_multiply_fusion
  294.6 0.4 copy_convert_fusion
  295.1 2.0 fusion.79
  297.0 0.2 maximum_bitcast_fusion.1
  297.2 0.2 maximum_bitcast_fusion.2
  297.4 2.0 pad_maximum_fusion.5
  (47 shorter events, 0.8 us)
Async XLA Ops:
  7.2 6.9 %copy-start.12 = (f32[128,128]{1,0:T(8,128)S(1)}, f32[128,128]{1,0:T(8,128)}, u32[]{:S(2)}) copy-start(f32[128,128]{1,0:T(8,128)} %param.6) | copy-start | bytes 196612
  7.2 268.7 %all-reduce.13.cloned.1.call-start = ((), (), s32[]{:S(2)}) async-start(), calls=%async_computation | async-start | bytes 524288 | tf_op jit(solution)/shard_map/psum | solution.py:158
  10.3 60.0 %collective-permute-start = (bf16[3,133,2048]{2,1,0:T(8,128)(2,1)}, bf16[3,133,2048]{2,1,0:T(8,128)(2,1)}, u32[]{:S(2)}, u32[]{:S(2)}) collective-permute-start(bf16[3,133,2048]{2,1,0:T(8,128)(2,1)} %slice.379), channel_id=1, source_target_pairs={{0,4},{4,8},{8,12},{12,16},{16,20},{20,24},{24,28},{1,5},{5,9},{9,... | collective-permute-start | bytes 4902920 | tf_op jit(solution)/shard_map/ppermute | solution.py:13
  37.6 31.0 %copy-start.11 = (f32[3,7,2048]{2,1,0:T(8,128)S(1)}, f32[3,7,2048]{2,1,0:T(8,128)}, u32[]{:S(2)}) copy-start(f32[3,7,2048]{2,1,0:T(8,128)} %param.5) | copy-start | bytes 516100
  37.6 31.1 %copy-start.3 = (bf16[3,256,2048]{2,1,0:T(8,128)(2,1)S(1)}, bf16[3,256,2048]{2,1,0:T(8,128)(2,1)}, u32[]{:S(2)}) copy-start(bf16[3,256,2048]{2,1,0:T(8,128)(2,1)} %param.4) | copy-start | bytes 9437188
  68.7 2.5 copy-start.7
  70.3 3.0 copy-start.6
  83.2 5.0 %copy-start.4 = (bf16[256,2048]{1,0:T(8,128)(2,1)S(1)}, bf16[256,2048]{1,0:T(8,128)(2,1)}, u32[]{:S(2)}) copy-start(bf16[256,2048]{1,0:T(8,128)(2,1)} %get-tuple-element.40) | copy-start | bytes 3145732
  83.2 5.0 %copy-start.5 = (bf16[256,2048]{1,0:T(8,128)(2,1)S(1)}, bf16[256,2048]{1,0:T(8,128)(2,1)}, u32[]{:S(2)}) copy-start(bf16[256,2048]{1,0:T(8,128)(2,1)} %get-tuple-element.42) | copy-start | bytes 3145732
  88.2 9.5 %copy-start.2 = (f32[3,128,2048]{2,1,0:T(8,128)S(1)}, f32[3,128,2048]{2,1,0:T(8,128)}, u32[]{:S(2)}) copy-start(f32[3,128,2048]{2,1,0:T(8,128)} %copy.40) | copy-start | bytes 9437188
  130.1 4.1 %copy-start = (f32[383,2048]{1,0:T(8,128)S(1)}, f32[383,2048]{1,0:T(8,128)}, u32[]{:S(2)}) copy-start(f32[383,2048]{1,0:T(8,128)} %get-tuple-element.32) | copy-start | bytes 9412612
  130.1 4.1 %copy-start.1 = (f32[383,2048]{1,0:T(8,128)S(1)}, f32[383,2048]{1,0:T(8,128)}, u32[]{:S(2)}) copy-start(f32[383,2048]{1,0:T(8,128)} %get-tuple-element.30) | copy-start | bytes 9412612
  148.0 68.1 %collective-permute-start.1 = (bf16[6,2048]{1,0:T(8,128)(2,1)S(1)}, bf16[6,2048]{1,0:T(8,128)(2,1)S(1)}, u32[]{:S(2)}, u32[]{:S(2)}) collective-permute-start(bf16[6,2048]{1,0:T(8,128)(2,1)S(1)} %slice.496), channel_id=1, source_target_pairs={{4,0},{8,4},{12,8},{16,12},{20,16},{24,20},{28,24},{5,1},{9,5},{13... | collective-permute-start | bytes 73736 | tf_op jit(solution)/shard_map/ppermute | solution.py:13
  151.5 7.8 %copy-start.13 = (f32[2048]{0:T(1024)S(1)}, f32[2048]{0:T(1024)}, u32[]{:S(2)}) copy-start(f32[2048]{0:T(1024)} %get-tuple-element.26) | copy-start | bytes 24580
  151.6 143.1 %collective-permute-start.2 = (bf16[2,133,2048]{2,0,1:T(2,128)(2,1)}, bf16[2,133,2048]{2,0,1:T(2,128)(2,1)S(1)}, u32[]{:S(2)}, u32[]{:S(2)}) collective-permute-start(bf16[2,133,2048]{2,0,1:T(2,128)(2,1)} %copy.41), channel_id=1, source_target_pairs={{4,0},{8,4},{12,8},{16,12},{20,16},{24,20},{28,24},{5,1},{9,5},{13... | collective-permute-start | bytes 3268616 | tf_op jit(solution)/shard_map/ppermute | solution.py:13
  208.6 71.7 %copy-start.8 = (bf16[250,2048]{1,0:T(8,128)(2,1)S(1)}, bf16[250,2048]{1,0:T(8,128)(2,1)}, u32[]{:S(2)}) copy-start(bf16[250,2048]{1,0:T(8,128)(2,1)} %slice.494) | copy-start | bytes 3072004
  295.0 2.0 copy-start.9
  295.1 2.2 copy-start.10
Sparse Core Ops, SparseCore 0:
  216.2 59.6 all-reduce.12
where the time goes:
time: 308 us; the launch traced here: 306 us
  local copies, waits for them, and re-layouts  132 us (43%)
  other arithmetic  63.8 us (21%)
  waiting for transfers between devices  59 us (19%)
  matrix products  18.6 us (6%)
  between operations  16.4 us (5%)
  blocking collectives  10.3 us (3%)
  starting transfers between devices  6.42 us (2%)
    psum x1, waiting for transfers between devices, on_device(): raw_short, raw_long = lax.psum((raw_short, raw_long), 'ctx')  59 us
    reshape x1, local copies, waits for them, and re-layouts, toeplitz(): return flat.reshape(groups, span, 3 * span - 1)[:, :, :2 * span]  31 us
    reduce_sum x3, other arithmetic, filter_grad(): jnp.sum(grad * extended[start:start + count].astype(jnp.float32), 0)  23.4 us
    concatenate x1, local copies, waits for them, and re-layouts, long_filter_grad(): inner = jnp.concatenate([lower, upper], 2)  17.6 us
    reshape x1, local copies, waits for them, and re-layouts, long_filter_grad(): skewed = flat.reshape(groups, span, 2 * span + 1)  17.5 us
    another operation x5, other arithmetic  13.4 us
    concatenate x1, local copies, waits for them, and re-layouts, long_filter_grad(): jnp.concatenate([inner.reshape(groups, span * 2 * span), jnp.zeros((group...  13.3 us
    unnamed x30, local copies, waits for them, and re-layouts  13.3 us
  transfers between devices with their start and end apart: 4, of which 1 were waited for; matrix products, arithmetic and copies ran while one was open for 42% of the time, Pallas kernels for 0%

commit v1 on v0

v1 whole, which is shorter than its diff:
```python
import functools

import jax
import jax.numpy as jnp
from jax import lax
from jax.experimental import pallas as pl
from jax.experimental.pallas import tpu as pltpu
from jax.sharding import PartitionSpec as P

D = 8192
G = 512
LANES = 128
EDGE = 8
F32 = jnp.float32
BF16 = jnp.bfloat16


def taps_of(filt, which, lanes):
    return [filt[which, pl.ds(j, 1), lanes] for j in range(filt.shape[1])]


def conv(source, taps, base, count):
    total = None
    for j, tap in enumerate(taps):
        term = tap * source[pl.ds(base - j, count), :]
        total = term if total is None else total + term
    return total


def chunks(count, size):
    return [(at, min(size, count - at)) for at in range(0, count, size)]


def edge_kernel(span, feat, cot, filt, ahead, back, qx, kx, vx):
    rows = feat.shape[1]
    width = feat.shape[2]
    reach = span + 2 * EDGE

    def tile(i, carry):
        lanes = pl.ds(pl.multiple_of(i * LANES, LANES), LANES)
        qx[...] = feat[0, 0:reach, lanes].astype(F32)
        kx[...] = feat[1, rows - reach : rows, lanes].astype(F32)
        vx[...] = feat[2, rows - reach : rows, lanes].astype(F32)
        fq, fk, fv = (taps_of(filt, a, lanes) for a in range(3))
        for at, size in chunks(span, 32):
            z = conv(kx, fk, at + 2 * EDGE, size) * conv(vx, fv, at + 2 * EDGE, size)
            ahead[at : at + size, lanes] = z.astype(BF16)
        q_tail = feat[0, rows - 2 * EDGE : rows, lanes].astype(F32)[EDGE:]
        tails = jnp.concatenate([q_tail, kx[reach - EDGE : reach, :]], 0)
        ahead[span : span + 2 * EDGE, lanes] = tails.astype(BF16)
        ahead[span + 2 * EDGE : span + 3 * EDGE, lanes] = vx[reach - EDGE : reach, :].astype(BF16)
        for at, size in chunks(span + EDGE, 32):
            low = max(at, EDGE)
            c = cot[at : at + max(size, 2 * EDGE), lanes].astype(F32)[low - at : size]
            dy = conv(qx, fq, low, at + size - low) * c
            if at == 0:
                dy = jnp.concatenate([qx[0:EDGE, :], dy], 0)
            back[at : at + size, lanes] = dy.astype(BF16)
        heads = [feat[a, 0 : 2 * EDGE, lanes].astype(F32)[:EDGE] for a in (1, 2)]
        heads.append(cot[0 : 2 * EDGE, lanes].astype(F32)[:EDGE])
        back[span + EDGE : span + 4 * EDGE, lanes] = jnp.concatenate(heads, 0).astype(BF16)
        return carry

    lax.fori_loop(0, width // LANES, tile, 0)


def edges(features, cotangent, short_filter, span):
    _, rows, width = features.shape
    taps = short_filter.shape[1]
    step = min(width, 1024)
    return pl.pallas_call(
        functools.partial(edge_kernel, span),
        grid=(width // step,),
        in_specs=[
            pl.BlockSpec((3, rows, step), lambda i: (0, 0, i)),
            pl.BlockSpec((rows, step), lambda i: (0, i)),
            pl.BlockSpec((3, taps, step), lambda i: (0, 0, i)),
        ],
        out_specs=[
            pl.BlockSpec((span + 3 * EDGE, step), lambda i: (0, i)),
            pl.BlockSpec((span + 4 * EDGE, step), lambda i: (0, i)),
        ],
        out_shape=[
            jax.ShapeDtypeStruct((span + 3 * EDGE, width), BF16),
            jax.ShapeDtypeStruct((span + 4 * EDGE, width), BF16),
        ],
        scratch_shapes=[pltpu.VMEM((span + 2 * EDGE, LANES), F32)] * 3,
        name="edges",
    )(features, cotangent, short_filter)


def dot(a, b, dims=((1,), (0,))):
    return lax.dot_general(a, b, (dims, ((), ())), preferred_element_type=F32)


def main_kernel(
    span, members,
    feat, cot, ahead, back, filt, lines,
    grads, sums,
    qx, kx, vx, ksx, vsx, zx, dyx, dqx, dkx, dvx, tst, ust, zm,
):
    rows = feat.shape[1]
    width = feat.shape[2]
    blocks = rows // span
    wide = rows + EDGE
    per = LANES // members

    @pl.when(pl.program_id(0) == 0)
    def _():
        zx[...] = jnp.zeros_like(zx)
        dyx[...] = jnp.zeros_like(dyx)

    def tile(i, carry):
        lanes = pl.ds(pl.multiple_of(i * LANES, LANES), LANES)
        fq, fk, fv = (taps_of(filt, a, lanes) for a in range(3))
        ends = ahead[span : span + 2 * EDGE, lanes].astype(F32)
        qx[0:EDGE, :] = ends[:EDGE]
        kx[0:EDGE, :] = ends[EDGE:]
        vx[0:EDGE, :] = ahead[span + 2 * EDGE : span + 3 * EDGE, lanes].astype(F32)
        for a, x in enumerate((qx, kx, vx)):
            for at, size in chunks(rows, 32):
                x[EDGE + at : EDGE + at + size, :] = feat[a, at : at + size, lanes].astype(F32)
        first = back[0 : 2 * EDGE, lanes].astype(F32)
        last = back[span + EDGE : span + 4 * EDGE, lanes].astype(F32)
        qx[EDGE + rows : EDGE + wide, :] = first[:EDGE]
        kx[EDGE + rows : EDGE + wide, :] = last[:EDGE]
        vx[EDGE + rows : EDGE + wide, :] = last[EDGE : 2 * EDGE]
        c_next = last[2 * EDGE :]

        zx[0:span, :] = ahead[0:span, lanes]
        for at, size in chunks(wide, 32):
            ks = conv(kx, fk, EDGE + at, size)
            vs = conv(vx, fv, EDGE + at, size)
            ksx[at : at + size, :] = ks
            vsx[at : at + size, :] = vs
            zx[span + at : span + at + size, :] = (ks * vs).astype(BF16)
        for at, size in chunks(rows, 32):
            c = cot[at : at + size, lanes].astype(F32)
            dyx[at : at + size, :] = (c * conv(qx, fq, EDGE + at, size)).astype(BF16)
        dy_next = c_next * conv(qx, fq, EDGE + rows, EDGE)
        dyx[rows : rows + 2 * EDGE, :] = jnp.concatenate([dy_next, first[EDGE:]], 0).astype(BF16)
        dyx[rows + 2 * EDGE : rows + span + EDGE, :] = back[2 * EDGE : span + EDGE, lanes]

        for g in range(per):
            for which, out in ((0, tst), (1, ust)):
                line = lines[which, pl.ds(i * per + g, 1), :]
                spread = jnp.broadcast_to(line, (span, 2 * span))
                turned = pltpu.roll(spread, 0, 1, stride=1, stride_axis=0)
                out[g * span : (g + 1) * span, :] = turned.astype(BF16)

        lane_group = lax.broadcasted_iota(jnp.int32, (1, LANES), 1) // members
        wide_group = jnp.concatenate([lane_group] * blocks, 1)

        def pick(stacked, size, owner):
            total = stacked[0:size]
            for g in range(1, per):
                total = jnp.where(owner == g, stacked[g * size : (g + 1) * size], total)
            return total

        def heads_of(matrix):
            return jnp.concatenate(
                [matrix[g * span : g * span + 2 * EDGE, :] for g in range(per)], 0
            )

        z_win = jnp.concatenate([zx[b * span : (b + 2) * span, :] for b in range(blocks)], 1)
        y = pick(dot(tst[...], z_win), span, wide_group)
        y_next = pick(dot(heads_of(tst), zx[rows : rows + 2 * span, :]), 2 * EDGE, lane_group)
        for b in range(blocks):
            for at, size in chunks(span, 32):
                t = b * span + at
                c = cot[t : t + size, lanes].astype(F32)
                dqx[t : t + size, :] = c * y[at : at + size, b * LANES : (b + 1) * LANES]
        dqx[rows:wide, :] = c_next * y_next[:EDGE]

        d_win = jnp.concatenate([dyx[b * span : (b + 2) * span, :] for b in range(blocks)], 1)
        dz = pick(dot(ust[...], d_win), span, wide_group)
        dz_next = pick(dot(heads_of(ust), dyx[rows : rows + 2 * span, :]), 2 * EDGE, lane_group)
        for b in range(blocks):
            for at, size in chunks(span, 32):
                t = b * span + at
                piece = dz[at : at + size, b * LANES : (b + 1) * LANES]
                dkx[t : t + size, :] = piece * vsx[t : t + size, :]
                dvx[t : t + size, :] = piece * ksx[t : t + size, :]
        dkx[rows:wide, :] = dz_next[:EDGE] * vsx[rows:wide, :]
        dvx[rows:wide, :] = dz_next[:EDGE] * ksx[rows:wide, :]

        r = lax.broadcasted_iota(jnp.int32, (span, span), 0)
        s = lax.broadcasted_iota(jnp.int32, (span, span), 1)
        flip = jnp.where(r + s == span - 1, 1.0, 0.0).astype(BF16)
        z_own = jnp.concatenate([zx[(b + 1) * span : (b + 2) * span, :] for b in range(blocks)], 1)
        z_back = dot(flip, z_own)
        for g in range(per):
            kept = jnp.where(wide_group == g, z_back, 0.0)
            zm[g * span : (g + 1) * span, :] = kept.astype(BF16)
        pairs = dot(zm[...], d_win, ((1,), (1,)))
        for g in range(per):
            part = pltpu.roll(
                pairs[g * span : (g + 1) * span, :], span + 1, 1, stride=1, stride_axis=0
            )
            sums[3 * EDGE + g : 3 * EDGE + g + 1, lanes] = jnp.sum(
                part[:, :span], 0, keepdims=True
            )

        for a, (x, dx, taps) in enumerate(((qx, dqx, fq), (kx, dkx, fk), (vx, dvx, fv))):
            parts = [None] * len(taps)
            for at, size in chunks(rows, 32):
                own = x[EDGE + at : EDGE + at + size, :]
                total = None
                for j, tap in enumerate(taps):
                    moved = dx[pl.ds(at + j, size), :]
                    term = tap * moved
                    total = term if total is None else total + term
                    prod = jnp.sum((own * moved).reshape(size // EDGE, EDGE, LANES), 0)
                    parts[j] = prod if parts[j] is None else parts[j] + prod
                grads[a, at : at + size, lanes] = total.astype(BF16)
            found = [jnp.sum(p, 0, keepdims=True) for p in parts]
            found.append(jnp.zeros((EDGE - len(taps), LANES), F32))
            sums[a * EDGE : (a + 1) * EDGE, lanes] = jnp.concatenate(found, 0)
        return carry

    lax.fori_loop(0, width // LANES, tile, 0)


def main(features, cotangent, ahead, back, short_filter, lines, span, members):
    _, rows, width = features.shape
    taps = short_filter.shape[1]
    step = min(width, 512)
    per = LANES // members
    blocks = rows // span
    wide = rows + EDGE
    tall = (blocks + 2) * span
    return pl.pallas_call(
        functools.partial(main_kernel, span, members),
        grid=(width // step,),
        in_specs=[
            pl.BlockSpec((3, rows, step), lambda i: (0, 0, i)),
            pl.BlockSpec((rows, step), lambda i: (0, i)),
            pl.BlockSpec((span + 3 * EDGE, step), lambda i: (0, i)),
            pl.BlockSpec((span + 4 * EDGE, step), lambda i: (0, i)),
            pl.BlockSpec((3, taps, step), lambda i: (0, 0, i)),
            pl.BlockSpec((2, step // members, 2 * span), lambda i: (0, i, 0)),
        ],
        out_specs=[
            pl.BlockSpec((3, rows, step), lambda i: (0, 0, i)),
            pl.BlockSpec((3 * EDGE + per, step), lambda i: (0, i)),
        ],
        out_shape=[
            jax.ShapeDtypeStruct((3, rows, width), BF16),
            jax.ShapeDtypeStruct((3 * EDGE + per, width), F32),
        ],
        scratch_shapes=[pltpu.VMEM((wide + EDGE, LANES), F32)] * 3
        + [pltpu.VMEM((wide, LANES), F32)] * 2
        + [pltpu.VMEM((tall, LANES), BF16)] * 2
        + [pltpu.VMEM((wide, LANES), F32)] * 3
        + [pltpu.VMEM((per * span, 2 * span), BF16)] * 2
        + [pltpu.VMEM((per * span, blocks * LANES), BF16)],
        compiler_params=pltpu.CompilerParams(vmem_limit_bytes=60 * 2**20),
        name="main",
    )(features, cotangent, ahead, back, short_filter, lines)


def factors_of(size):
    found = []
    factor = 2
    while size > 1:
        while size % factor == 0:
            found.append(factor)
            size //= factor
        factor += 1
    return found


def peers(value, axis, stride, factor):
    size = lax.axis_size(axis)
    got = []
    for turn in range(1, factor):
        route = []
        for i in range(size):
            digit = i // stride % factor
            route.append((i, i + ((digit + turn) % factor - digit) * stride))
        got.append(lax.ppermute(value, axis, route))
    return got


def add_in_order(value, got, axis, stride, factor):
    if factor == 2:
        return value.astype(F32) + got[0].astype(F32)
    digit = lax.axis_index(axis) // stride % factor
    every = jnp.stack([value] + got[::-1]).astype(F32)
    return jnp.sum(jnp.roll(every, digit, 0), 0)


def total_over(value, axis, stride, factors, kind):
    for factor in factors:
        value = value.astype(kind)
        value = add_in_order(value, peers(value, axis, stride, factor), axis, stride, factor)
        stride *= factor
    return value


def on_device(features, short_filter, long_filter, cotangent):
    _, rows, width = features.shape
    taps = short_filter.shape[1]
    groups, span = long_filter.shape
    members = width // groups
    per = LANES // members
    size = lax.axis_size("ctx")
    ahead, back = edges(features, cotangent, short_filter, span)
    ahead = lax.ppermute(ahead, "ctx", [(i, i + 1) for i in range(size - 1)])
    back = lax.ppermute(back, "ctx", [(i + 1, i) for i in range(size - 1)])
    rounded = long_filter.astype(BF16).astype(F32)
    lines = jnp.stack(
        [
            jnp.pad(rounded[:, ::-1], ((0, 0), (1, span - 1))),
            jnp.pad(rounded, ((0, 0), (0, span))),
        ]
    )
    grads, sums = main(features, cotangent, ahead, back, short_filter, lines, span, members)
    sums = total_over(sums, "ctx", 1, factors_of(size), BF16)
    square = jnp.sum(sums * sums)
    square = jnp.full((EDGE, LANES), square)
    square = total_over(square, "ch", 1, factors_of(lax.axis_size("ch")), F32)[:1, :1]
    factor = lax.rsqrt(square / (3 * taps * D + span * G) + 1e-06)
    scaled = sums * factor
    grad_short = scaled[: 3 * EDGE].reshape(3, EDGE, width)[:, :taps]
    grad_long = scaled[3 * EDGE :].reshape(per, width // LANES, span)
    return (grads, grad_short, grad_long.transpose(1, 0, 2).reshape(groups, span))


def solution(mesh):
    in_specs = (P(None, "ctx", "ch"), P(None, None, "ch"), P("ch", None), P("ctx", "ch"))
    out_specs = (P(None, "ctx", "ch"), P(None, None, "ch"), P("ch", None))
    return jax.shard_map(
        on_device, mesh=mesh, in_specs=in_specs, out_specs=out_specs, check_vma=False
    )
```

time: 308 us -> 82.6 us (0.27)
  local copies, waits for them, and re-layouts: 132 us -> 4.34 us
  other arithmetic: 63.8 us -> 4.71 us
  waiting for transfers between devices: 59 us -> 15.8 us
  Pallas kernels: 0 us -> 34.7 us
  matrix products: 18.6 us -> 0 us
  between operations: 16.4 us -> 1.42 us
  starting transfers between devices: 6.42 us -> 21.3 us
  blocking collectives: 10.3 us -> 0 us
    psum x1 -> x0, waiting for transfers between devices: 59 us -> none  [on_device(): raw_short, raw_long = lax.psum((raw_short, raw_long), 'ctx')]
    reshape x2, local copies, waits for them, and re-layouts: 48.5 us -> 1.32 us  [the longest x1 0.69 us: on_device(): grad_short = scaled[:3 * EDGE].reshape(3, EDGE, width)[:, :taps]]
    pallas_call x0 -> x2, Pallas kernels: none -> 34.7 us  [the longest x1 30 us: main(): pl.pallas_call(functools.partial(main_kernel, span, members), grid=(width...]
    reduce_sum x6 -> x1, other arithmetic: 33.2 us -> 0.67 us  [on_device(): square = jnp.sum(sums * sums)]
    concatenate x5 -> x0, local copies, waits for them, and re-layouts: 31.4 us -> none  [the longest x1 17.6 us: long_filter_grad(): inner = jnp.concatenate([lower, upper], 2)]
    dot_general x6 -> x0, matrix products: 18.6 us -> none  [the longest x1 4.57 us: long_forward(): jnp.einsum('bgcs,gts->bgct', blocks[1:], matrix[:, :, span:], preferred_e...]
    another operation x11 -> x1, other arithmetic: 16.6 us -> 0.73 us  [on_device(): jnp.stack([jnp.pad(rounded[:, ::-1], ((0, 0), (1, span - 1))), jnp.pad(ro...]
    ppermute x3 -> x7, waiting for transfers between devices: 0.01 us -> 15.8 us  [the longest x5 14.9 us: peers(): got.append(lax.ppermute(value, axis, route))]
  transfers between devices with their start and end apart: 4 -> 7, of which waited for: 1 -> 6; matrix products, arithmetic and copies ran while one was open for 42% -> 1% of each run, Pallas kernels for 0% -> 0%
where the time goes in v1:
time: 82.6 us; the launch traced here: 82.4 us
  Pallas kernels  34.7 us (42%)
  starting transfers between devices  21.3 us (26%)
  waiting for transfers between devices  15.8 us (19%)
  other arithmetic  4.71 us (6%)
  local copies, waits for them, and re-layouts  4.34 us (5%)
  between operations  1.42 us (2%)
    pallas_call x1, Pallas kernels, main(): pl.pallas_call(functools.partial(main_kernel, span, members), grid=(width...  30 us
    ppermute x5, starting transfers between devices, peers(): got.append(lax.ppermute(value, axis, route))  17 us
    ppermute x5, waiting for transfers between devices, peers(): got.append(lax.ppermute(value, axis, route))  14.9 us
    pallas_call x1, Pallas kernels, edges(): pl.pallas_call(functools.partial(edge_kernel, span), grid=(width // step,...  4.68 us
    ppermute x1, starting transfers between devices, on_device(): ahead = lax.ppermute(ahead, 'ctx', [(i, i + 1) for i in range(size - 1)])  3.07 us
    convert_element_type x3, other arithmetic, total_over(): value = value.astype(kind)  1.98 us
    unnamed x6, local copies, waits for them, and re-layouts  1.68 us
  transfers between devices with their start and end apart: 7, of which 6 were waited for; matrix products, arithmetic and copies ran while one was open for 1% of the time, Pallas kernels for 0%

profile of v1, /device:TPU:0, one launch (start us, length us, event | category | flops | bytes accessed | tf_op | source)
XLA Modules:
  0.0 82.4 jit_solution(8957139469671633820)
XLA Ops:
  0.6 0.0 copy-start.2
  0.6 4.7 %edges.1 = (bf16[152,2048]{1,0:T(8,128)(2,1)}, bf16[160,2048]{1,0:T(8,128)(2,1)}) custom-call(bf16[3,256,2048]{2,1,0:T(8,128)(2,1)} %feat.3, bf16[256,2048]{1,0:T(8,128)(2,1)} %cot.3, f32[3,7,2048]{2,1,0:T(8,128)} %filt.3), custom_call_target="tpu_custom_call" | custom-call | tf_op jit(solution)/shard_map/edges/pallas_call | solution.py:71
  5.3 1.3 %collective-permute-start.1 = (bf16[160,2048]{1,0:T(8,128)(2,1)}, bf16[160,2048]{1,0:T(8,128)(2,1)S(1)}, u32[]{:S(2)}, u32[]{:S(2)}) collective-permute-start(bf16[160,2048]{1,0:T(8,128)(2,1)} %get-tuple-element.8), channel_id=1, source_target_pairs={{4,0},{8,4},{12,8},{16,12},{20,16},{24,20},{28,24},{5,1},{9,5},{13... | collective-permute-start | bytes 1966088 | tf_op jit(solution)/shard_map/ppermute | solution.py:310
  6.6 3.1 %collective-permute-start = (bf16[152,2048]{1,0:T(8,128)(2,1)}, bf16[152,2048]{1,0:T(8,128)(2,1)S(1)}, u32[]{:S(2)}, u32[]{:S(2)}) collective-permute-start(bf16[152,2048]{1,0:T(8,128)(2,1)} %get-tuple-element.7), channel_id=1, source_target_pairs={{0,4},{4,8},{8,12},{12,16},{16,20},{20,24},{24,28},{1,5},{5,9},{9,... | collective-permute-start | bytes 1867784 | tf_op jit(solution)/shard_map/ppermute | solution.py:309
  9.7 0.0 copy-done.2
  9.7 0.1 rev.3
  9.8 0.1 pad_bitcast_fusion
  9.9 0.7 pad_maximum_fusion.lines
  10.6 0.9 %collective-permute-done.ahead = bf16[152,2048]{1,0:T(8,128)(2,1)S(1)} collective-permute-done((bf16[152,2048]{1,0:T(8,128)(2,1)}, bf16[152,2048]{1,0:T(8,128)(2,1)S(1)}, u32[]{:S(2)}, u32[]{:S(2)}) %collective-permute-start) | collective-permute-done | bytes 622624 | tf_op jit(solution)/shard_map/ppermute | solution.py:309
  11.5 0.0 copy-start.1
  11.5 0.0 collective-permute-done.1.back
  11.5 0.8 %copy-done.1 = bf16[152,2048]{1,0:T(8,128)(2,1)} copy-done((bf16[152,2048]{1,0:T(8,128)(2,1)}, bf16[152,2048]{1,0:T(8,128)(2,1)S(1)}, u32[]{:S(2)}) %copy-start.1) | copy-done | bytes 622616
  12.4 0.0 copy-start
  12.4 0.8 %copy-done = bf16[160,2048]{1,0:T(8,128)(2,1)} copy-done((bf16[160,2048]{1,0:T(8,128)(2,1)}, bf16[160,2048]{1,0:T(8,128)(2,1)S(1)}, u32[]{:S(2)}) %copy-start) | copy-done | bytes 655384
  13.2 30.0 %main.1 = (bf16[3,256,2048]{2,1,0:T(8,128)(2,1)}, f32[32,2048]{1,0:T(8,128)}) custom-call(bf16[3,256,2048]{2,1,0:T(8,128)(2,1)} %feat.3, bf16[256,2048]{1,0:T(8,128)(2,1)} %cot.3, bf16[152,2048]{1,0:T(8,128)(2,1)} %copy-done.1, bf16[160,2048]{1,0:T(8,128)(2,1)} %copy-done, f32[3,7,2048]{2,1,0:T(8,128)} %filt.3, f32[2,128,256]{2,1,0:T(8,128)} %pad_maximum_fusion.lines), custom_call_target="tpu_custom_call" | custom-call | tf_op jit(solution)/shard_map/main/pallas_call | solution.py:232
  43.2 1.0 %convert_element_type.39 = bf16[32,2048]{1,0:T(8,128)(2,1)S(1)} convert(f32[32,2048]{1,0:T(8,128)} %get-tuple-element.10) | non-fusion elementwise | flops 65536 | bytes 393216 | tf_op jit(solution)/shard_map/convert_element_type | solution.py:295
  44.2 8.3 %collective-permute-start.2 = (bf16[32,2048]{1,0:T(8,128)(2,1)S(1)}, bf16[32,2048]{1,0:T(8,128)(2,1)S(1)}, u32[]{:S(2)}, u32[]{:S(2)}) collective-permute-start(bf16[32,2048]{1,0:T(8,128)(2,1)S(1)} %convert_element_type.39), channel_id=1, source_target_pairs={{0,4},{4,0},{8,12},{12,8},{16,20},{20,16},{24,28},{28,24},{1,5},{5... | collective-permute-start | bytes 393224 | tf_op jit(solution)/shard_map/ppermute | solution.py:281
  52.6 1.0 %collective-permute-done.2 = bf16[32,2048]{1,0:T(8,128)(2,1)S(1)} collective-permute-done((bf16[32,2048]{1,0:T(8,128)(2,1)S(1)}, bf16[32,2048]{1,0:T(8,128)(2,1)S(1)}, u32[]{:S(2)}, u32[]{:S(2)}) %collective-permute-start.2) | collective-permute-done | bytes 131104 | tf_op jit(solution)/shard_map/ppermute | solution.py:281
  53.5 1.0 %add_convert_fusion.1 = bf16[32,2048]{1,0:T(8,128)(2,1)S(1)} fusion(bf16[32,2048]{1,0:T(8,128)(2,1)S(1)} %collective-permute-done.2, f32[32,2048]{1,0:T(8,128)} %get-tuple-element.10), kind=kLoop, calls=%fused_computation.4 | loop fusion | flops 327680 | bytes 524288 | tf_op jit(solution)/shard_map/convert_element_type | solution.py:295
  54.5 2.7 %collective-permute-start.3 = (bf16[32,2048]{1,0:T(8,128)(2,1)S(1)}, bf16[32,2048]{1,0:T(8,128)(2,1)S(1)}, u32[]{:S(2)}, u32[]{:S(2)}) collective-permute-start(bf16[32,2048]{1,0:T(8,128)(2,1)S(1)} %add_convert_fusion.1), channel_id=1, source_target_pairs={{0,8},{4,12},{8,0},{12,4},{16,24},{20,28},{24,16},{28,20},{1,9},{5... | collective-permute-start | bytes 393224 | tf_op jit(solution)/shard_map/ppermute | solution.py:281
  57.2 3.8 %collective-permute-done.3 = bf16[32,2048]{1,0:T(8,128)(2,1)S(1)} collective-permute-done((bf16[32,2048]{1,0:T(8,128)(2,1)S(1)}, bf16[32,2048]{1,0:T(8,128)(2,1)S(1)}, u32[]{:S(2)}, u32[]{:S(2)}) %collective-permute-start.3) | collective-permute-done | bytes 131104 | tf_op jit(solution)/shard_map/ppermute | solution.py:281
  61.1 2.8 %collective-permute-start.4 = (bf16[32,2048]{1,0:T(8,128)(2,1)S(1)}, bf16[32,2048]{1,0:T(8,128)(2,1)S(1)}, u32[]{:S(2)}, u32[]{:S(2)}) collective-permute-start(bf16[32,2048]{1,0:T(8,128)(2,1)S(1)} %add_convert_fusion), channel_id=1, source_target_pairs={{0,16},{4,20},{8,24},{12,28},{16,0},{20,4},{24,8},{28,12},{1,17},{... | collective-permute-start | bytes 393224 | tf_op jit(solution)/shard_map/ppermute | solution.py:281
  63.9 5.9 %collective-permute-done.4 = bf16[32,2048]{1,0:T(8,128)(2,1)S(1)} collective-permute-done((bf16[32,2048]{1,0:T(8,128)(2,1)S(1)}, bf16[32,2048]{1,0:T(8,128)(2,1)S(1)}, u32[]{:S(2)}, u32[]{:S(2)}) %collective-permute-start.4) | collective-permute-done | bytes 131104 | tf_op jit(solution)/shard_map/ppermute | solution.py:281
  69.8 0.7 multiply_reduce_fusion
  70.5 0.6 broadcast_in_dim.3
  71.1 1.6 %collective-permute-start.5 = (f32[8,128]{1,0:T(8,128)S(1)}, f32[8,128]{1,0:T(8,128)S(1)}, u32[]{:S(2)}, u32[]{:S(2)}) collective-permute-start(f32[8,128]{1,0:T(8,128)S(1)} %broadcast_in_dim.3), channel_id=1, source_target_pairs={{0,1},{1,0},{2,3},{3,2},{4,5},{5,4},{6,7},{7,6},{8,9},{9,8},{10,11... | collective-permute-start | bytes 12296 | tf_op jit(solution)/shard_map/ppermute | solution.py:281
  72.7 2.1 %collective-permute-done.5 = f32[8,128]{1,0:T(8,128)S(1)} collective-permute-done((f32[8,128]{1,0:T(8,128)S(1)}, f32[8,128]{1,0:T(8,128)S(1)}, u32[]{:S(2)}, u32[]{:S(2)}) %collective-permute-start.5) | collective-permute-done | bytes 4128 | tf_op jit(solution)/shard_map/ppermute | solution.py:281
  74.8 0.6 broadcast_add_fusion
  75.5 1.6 %collective-permute-start.6 = (f32[8,128]{1,0:T(8,128)S(1)}, f32[8,128]{1,0:T(8,128)S(1)}, u32[]{:S(2)}, u32[]{:S(2)}) collective-permute-start(f32[8,128]{1,0:T(8,128)S(1)} %broadcast_add_fusion), channel_id=1, source_target_pairs={{0,2},{1,3},{2,0},{3,1},{4,6},{5,7},{6,4},{7,5},{8,10},{9,11},{10,... | collective-permute-start | bytes 12296 | tf_op jit(solution)/shard_map/ppermute | solution.py:281
  77.0 2.1 %collective-permute-done.6 = f32[8,128]{1,0:T(8,128)S(1)} collective-permute-done((f32[8,128]{1,0:T(8,128)S(1)}, f32[8,128]{1,0:T(8,128)S(1)}, u32[]{:S(2)}, u32[]{:S(2)}) %collective-permute-start.6) | collective-permute-done | bytes 4128 | tf_op jit(solution)/shard_map/ppermute | solution.py:281
  79.1 0.6 fusion.1
  79.8 0.5 slice.12
  81.0 0.6 slice_bitcast_fusion.1
  81.7 0.7 slice_bitcast_fusion
  (3 shorter events, 0.1 us)
Async XLA Ops:
  0.6 9.1 %copy-start.2 = (f32[128,128]{1,0:T(8,128)S(1)}, f32[128,128]{1,0:T(8,128)}, u32[]{:S(2)}) copy-start(f32[128,128]{1,0:T(8,128)} %param.6) | copy-start | bytes 196612
  5.3 6.2 %collective-permute-start.1 = (bf16[160,2048]{1,0:T(8,128)(2,1)}, bf16[160,2048]{1,0:T(8,128)(2,1)S(1)}, u32[]{:S(2)}, u32[]{:S(2)}) collective-permute-start(bf16[160,2048]{1,0:T(8,128)(2,1)} %get-tuple-element.8), channel_id=1, source_target_pairs={{4,0},{8,4},{12,8},{16,12},{20,16},{24,20},{28,24},{5,1},{9,5},{13... | collective-permute-start | bytes 1966088 | tf_op jit(solution)/shard_map/ppermute | solution.py:310
  6.6 4.9 %collective-permute-start = (bf16[152,2048]{1,0:T(8,128)(2,1)}, bf16[152,2048]{1,0:T(8,128)(2,1)S(1)}, u32[]{:S(2)}, u32[]{:S(2)}) collective-permute-start(bf16[152,2048]{1,0:T(8,128)(2,1)} %get-tuple-element.7), channel_id=1, source_target_pairs={{0,4},{4,8},{8,12},{12,16},{16,20},{20,24},{24,28},{1,5},{5,9},{9,... | collective-permute-start | bytes 1867784 | tf_op jit(solution)/shard_map/ppermute | solution.py:309
  11.5 0.8 %copy-start.1 = (bf16[152,2048]{1,0:T(8,128)(2,1)}, bf16[152,2048]{1,0:T(8,128)(2,1)S(1)}, u32[]{:S(2)}) copy-start(bf16[152,2048]{1,0:T(8,128)(2,1)S(1)} %collective-permute-done.ahead) | copy-start | bytes 1867780
  12.4 0.8 %copy-start = (bf16[160,2048]{1,0:T(8,128)(2,1)}, bf16[160,2048]{1,0:T(8,128)(2,1)S(1)}, u32[]{:S(2)}) copy-start(bf16[160,2048]{1,0:T(8,128)(2,1)S(1)} %collective-permute-done.1.back) | copy-start | bytes 1966084
  44.2 9.3 %collective-permute-start.2 = (bf16[32,2048]{1,0:T(8,128)(2,1)S(1)}, bf16[32,2048]{1,0:T(8,128)(2,1)S(1)}, u32[]{:S(2)}, u32[]{:S(2)}) collective-permute-start(bf16[32,2048]{1,0:T(8,128)(2,1)S(1)} %convert_element_type.39), channel_id=1, source_target_pairs={{0,4},{4,0},{8,12},{12,8},{16,20},{20,16},{24,28},{28,24},{1,5},{5... | collective-permute-start | bytes 393224 | tf_op jit(solution)/shard_map/ppermute | solution.py:281
  54.5 6.5 %collective-permute-start.3 = (bf16[32,2048]{1,0:T(8,128)(2,1)S(1)}, bf16[32,2048]{1,0:T(8,128)(2,1)S(1)}, u32[]{:S(2)}, u32[]{:S(2)}) collective-permute-start(bf16[32,2048]{1,0:T(8,128)(2,1)S(1)} %add_convert_fusion.1), channel_id=1, source_target_pairs={{0,8},{4,12},{8,0},{12,4},{16,24},{20,28},{24,16},{28,20},{1,9},{5... | collective-permute-start | bytes 393224 | tf_op jit(solution)/shard_map/ppermute | solution.py:281
  61.1 8.7 %collective-permute-start.4 = (bf16[32,2048]{1,0:T(8,128)(2,1)S(1)}, bf16[32,2048]{1,0:T(8,128)(2,1)S(1)}, u32[]{:S(2)}, u32[]{:S(2)}) collective-permute-start(bf16[32,2048]{1,0:T(8,128)(2,1)S(1)} %add_convert_fusion), channel_id=1, source_target_pairs={{0,16},{4,20},{8,24},{12,28},{16,0},{20,4},{24,8},{28,12},{1,17},{... | collective-permute-start | bytes 393224 | tf_op jit(solution)/shard_map/ppermute | solution.py:281
  71.1 3.7 %collective-permute-start.5 = (f32[8,128]{1,0:T(8,128)S(1)}, f32[8,128]{1,0:T(8,128)S(1)}, u32[]{:S(2)}, u32[]{:S(2)}) collective-permute-start(f32[8,128]{1,0:T(8,128)S(1)} %broadcast_in_dim.3), channel_id=1, source_target_pairs={{0,1},{1,0},{2,3},{3,2},{4,5},{5,4},{6,7},{7,6},{8,9},{9,8},{10,11... | collective-permute-start | bytes 12296 | tf_op jit(solution)/shard_map/ppermute | solution.py:281
  75.5 3.7 %collective-permute-start.6 = (f32[8,128]{1,0:T(8,128)S(1)}, f32[8,128]{1,0:T(8,128)S(1)}, u32[]{:S(2)}, u32[]{:S(2)}) collective-permute-start(f32[8,128]{1,0:T(8,128)S(1)} %broadcast_add_fusion), channel_id=1, source_target_pairs={{0,2},{1,3},{2,0},{3,1},{4,6},{5,7},{6,4},{7,5},{8,10},{9,11},{10,... | collective-permute-start | bytes 12296 | tf_op jit(solution)/shard_map/ppermute | solution.py:281

commit v2 on v1

v2 whole, which is shorter than its diff:
```python
import functools

import jax
import jax.numpy as jnp
from jax import lax
from jax.experimental import pallas as pl
from jax.experimental.pallas import tpu as pltpu
from jax.sharding import PartitionSpec as P

D = 8192
G = 512
LANES = 128
EDGE = 8
F32 = jnp.float32
BF16 = jnp.bfloat16


def taps_of(filt, which, lanes):
    return [filt[which, pl.ds(j, 1), lanes] for j in range(filt.shape[1])]


def conv(source, taps, base, count):
    total = None
    for j, tap in enumerate(taps):
        term = tap * source[pl.ds(base - j, count), :]
        total = term if total is None else total + term
    return total


def chunks(count, size):
    return [(at, min(size, count - at)) for at in range(0, count, size)]


def odd_place():
    return lax.rem(lax.axis_index("ctx"), 2)


def edge_kernel(span, feat, cot, filt, near, far, qx, kx, vx):
    rows = feat.shape[1]
    width = feat.shape[2]
    reach = span + 2 * EDGE

    def run(ahead, back):
        def tile(i, carry):
            lanes = pl.ds(pl.multiple_of(i * LANES, LANES), LANES)
            qx[...] = feat[0, 0:reach, lanes].astype(F32)
            kx[...] = feat[1, rows - reach : rows, lanes].astype(F32)
            vx[...] = feat[2, rows - reach : rows, lanes].astype(F32)
            fq, fk, fv = (taps_of(filt, a, lanes) for a in range(3))
            for at, size in chunks(span, 32):
                z = conv(kx, fk, at + 2 * EDGE, size) * conv(vx, fv, at + 2 * EDGE, size)
                ahead[at : at + size, lanes] = z.astype(BF16)
            q_tail = feat[0, rows - 2 * EDGE : rows, lanes].astype(F32)[EDGE:]
            k_tail = kx[reach - EDGE : reach, :]
            v_tail = vx[reach - EDGE : reach, :]
            tails = jnp.concatenate([q_tail, k_tail, v_tail, v_tail], 0)
            ahead[span : span + 4 * EDGE, lanes] = tails.astype(BF16)
            for at, size in chunks(span + EDGE, 32):
                low = max(at, EDGE)
                c = cot[at : at + max(size, 2 * EDGE), lanes].astype(F32)[low - at : size]
                dy = conv(qx, fq, low, at + size - low) * c
                if at == 0:
                    dy = jnp.concatenate([qx[0:EDGE, :], dy], 0)
                back[at : at + size, lanes] = dy.astype(BF16)
            heads = [feat[a, 0 : 2 * EDGE, lanes].astype(F32)[:EDGE] for a in (1, 2)]
            heads.append(cot[0 : 2 * EDGE, lanes].astype(F32)[:EDGE])
            back[span + EDGE : span + 4 * EDGE, lanes] = jnp.concatenate(heads, 0).astype(BF16)
            return carry

        lax.fori_loop(0, width // LANES, tile, 0)

    odd = odd_place()

    @pl.when(odd == 0)
    def _():
        run(near, far)

    @pl.when(odd == 1)
    def _():
        run(far, near)


def edges(features, cotangent, short_filter, span):
    _, rows, width = features.shape
    taps = short_filter.shape[1]
    step = min(width, 1024)
    return pl.pallas_call(
        functools.partial(edge_kernel, span),
        grid=(width // step,),
        in_specs=[
            pl.BlockSpec((3, rows, step), lambda i: (0, 0, i)),
            pl.BlockSpec((rows, step), lambda i: (0, i)),
            pl.BlockSpec((3, taps, step), lambda i: (0, 0, i)),
        ],
        out_specs=[pl.BlockSpec((span + 4 * EDGE, step), lambda i: (0, i))] * 2,
        out_shape=[jax.ShapeDtypeStruct((span + 4 * EDGE, width), BF16)] * 2,
        scratch_shapes=[pltpu.VMEM((span + 2 * EDGE, LANES), F32)] * 3,
        name="edges",
    )(features, cotangent, short_filter)


def band_kernel(span, lines, bands):
    for which in range(2):
        for g in range(lines.shape[1]):
            spread = jnp.broadcast_to(lines[which, g : g + 1, :], (span, 2 * span))
            turned = pltpu.roll(spread, 0, 1, stride=1, stride_axis=0)
            bands[which, g * span : (g + 1) * span, :] = turned.astype(BF16)


def toeplitz(lines, span):
    groups = lines.shape[1]
    step = min(groups, 16)
    return pl.pallas_call(
        functools.partial(band_kernel, span),
        grid=(groups // step,),
        in_specs=[pl.BlockSpec((2, step, 2 * span), lambda i: (0, i, 0))],
        out_specs=pl.BlockSpec((2, step * span, 2 * span), lambda i: (0, i, 0)),
        out_shape=jax.ShapeDtypeStruct((2, groups * span, 2 * span), BF16),
        cost_estimate=pl.CostEstimate(
            flops=0, bytes_accessed=8 * groups * span * span, transcendentals=0
        ),
        name="bands",
    )(lines)


def dot(a, b, dims=((1,), (0,))):
    return lax.dot_general(a, b, (dims, ((), ())), preferred_element_type=F32)


def main_kernel(
    span, members,
    feat, cot, near, far, filt, bands,
    grads, keep, send,
    qx, kx, vx, ksx, vsx, zx, dyx, dqx, dkx, dvx, zm, sums,
):
    rows = feat.shape[1]
    width = feat.shape[2]
    blocks = rows // span
    wide = rows + EDGE
    per = LANES // members
    small = span // 2
    pieces = rows // small
    odd = odd_place()

    @pl.when(pl.program_id(0) == 0)
    def _():
        zx[...] = jnp.zeros_like(zx)
        dyx[...] = jnp.zeros_like(dyx)

    def tile(i, carry):
        lanes = pl.ds(pl.multiple_of(i * LANES, LANES), LANES)
        fq, fk, fv = (taps_of(filt, a, lanes) for a in range(3))

        def ahead(low, high):
            return jnp.where(odd == 1, near[low:high, lanes], far[low:high, lanes])

        def back(low, high):
            return jnp.where(odd == 1, far[low:high, lanes], near[low:high, lanes])

        ends = ahead(span, span + 4 * EDGE).astype(F32)
        first = back(0, 2 * EDGE).astype(F32)
        last = back(span + EDGE, span + 4 * EDGE).astype(F32)
        for a, x in enumerate((qx, kx, vx)):
            x[0:EDGE, :] = ends[a * EDGE : (a + 1) * EDGE]
            for at, size in chunks(rows, 32):
                x[EDGE + at : EDGE + at + size, :] = feat[a, at : at + size, lanes].astype(F32)
        qx[EDGE + rows : EDGE + wide, :] = first[:EDGE]
        kx[EDGE + rows : EDGE + wide, :] = last[:EDGE]
        vx[EDGE + rows : EDGE + wide, :] = last[EDGE : 2 * EDGE]
        c_next = last[2 * EDGE :]

        for at, size in chunks(rows, 32):
            c = cot[at : at + size, lanes].astype(F32)
            dyx[at : at + size, :] = (c * conv(qx, fq, EDGE + at, size)).astype(BF16)
        dy_next = c_next * conv(qx, fq, EDGE + rows, EDGE)
        dyx[rows : rows + 2 * EDGE, :] = jnp.concatenate([dy_next, first[EDGE:]], 0).astype(BF16)
        dyx[rows + 2 * EDGE : rows + span + EDGE, :] = back(2 * EDGE, span + EDGE)
        zx[0:span, :] = ahead(0, span)
        for at, size in chunks(wide, 32):
            ks = conv(kx, fk, EDGE + at, size)
            vs = conv(vx, fv, EDGE + at, size)
            ksx[at : at + size, :] = ks
            vsx[at : at + size, :] = vs
            zx[span + at : span + at + size, :] = (ks * vs).astype(BF16)

        lane_group = lax.broadcasted_iota(jnp.int32, (1, LANES), 1) // members
        wide_group = jnp.concatenate([lane_group] * blocks, 1)

        def pick(stacked, size, owner):
            total = stacked[0:size]
            for g in range(1, per):
                total = jnp.where(owner == g, stacked[g * size : (g + 1) * size], total)
            return total

        def band(which):
            return bands[which, pl.ds(pl.multiple_of(i * per * span, span), per * span), :]

        def heads_of(which):
            return jnp.concatenate(
                [
                    bands[which, pl.ds(pl.multiple_of((i * per + g) * span, span), 2 * EDGE), :]
                    for g in range(per)
                ],
                0,
            )

        d_win = jnp.concatenate([dyx[b * span : (b + 2) * span, :] for b in range(blocks)], 1)
        dz = pick(dot(band(1), d_win), span, wide_group)
        dz_next = pick(dot(heads_of(1), dyx[rows : rows + 2 * span, :]), 2 * EDGE, lane_group)
        z_win = jnp.concatenate([zx[b * span : (b + 2) * span, :] for b in range(blocks)], 1)
        y = pick(dot(band(0), z_win), span, wide_group)
        y_next = pick(dot(heads_of(0), zx[rows : rows + 2 * span, :]), 2 * EDGE, lane_group)

        r = lax.broadcasted_iota(jnp.int32, (small, small), 0)
        s = lax.broadcasted_iota(jnp.int32, (small, small), 1)
        flip = jnp.where(r + s == small - 1, 1.0, 0.0).astype(BF16)
        z_own = jnp.concatenate(
            [zx[span + b * small : span + (b + 1) * small, :] for b in range(pieces)], 1
        )
        z_back = dot(flip, z_own).astype(BF16)
        piece_group = jnp.concatenate([lane_group] * pieces, 1)
        for g in range(per):
            kept = jnp.where(piece_group == g, z_back, jnp.zeros_like(z_back))
            zm[g * small : (g + 1) * small, :] = kept
        d_near = jnp.concatenate(
            [dyx[b * small : b * small + 2 * span, :] for b in range(pieces)], 1
        )
        pairs = dot(zm[...], d_near, ((1,), (1,)))

        def long_sum(g):
            part = pltpu.roll(
                pairs[g * small : (g + 1) * small, :],
                2 * span + 1 - small, 1, stride=1, stride_axis=0,
            )
            sums[1, EDGE + g : EDGE + g + 1, lanes] = jnp.sum(part[:, :span], 0, keepdims=True)

        for b in range(blocks):
            for at, size in chunks(span, 32):
                t = b * span + at
                piece = dz[at : at + size, b * LANES : (b + 1) * LANES]
                dkx[t : t + size, :] = piece * vsx[t : t + size, :]
                dvx[t : t + size, :] = piece * ksx[t : t + size, :]
        dkx[rows:wide, :] = dz_next[:EDGE] * vsx[rows:wide, :]
        dvx[rows:wide, :] = dz_next[:EDGE] * ksx[rows:wide, :]
        for b in range(blocks):
            for at, size in chunks(span, 32):
                t = b * span + at
                c = cot[t : t + size, lanes].astype(F32)
                dqx[t : t + size, :] = c * y[at : at + size, b * LANES : (b + 1) * LANES]
        dqx[rows:wide, :] = c_next * y_next[:EDGE]

        done = 0
        for a, (x, dx, taps) in enumerate(((qx, dqx, fq), (kx, dkx, fk), (vx, dvx, fv))):
            parts = [None] * len(taps)
            for at, size in chunks(rows, 32):
                own = x[EDGE + at : EDGE + at + size, :]
                total = None
                for j, tap in enumerate(taps):
                    moved = dx[pl.ds(at + j, size), :]
                    term = tap * moved
                    total = term if total is None else total + term
                    prod = jnp.sum((own * moved).reshape(size // EDGE, EDGE, LANES), 0)
                    parts[j] = prod if parts[j] is None else parts[j] + prod
                grads[a, at : at + size, lanes] = total.astype(BF16)
                if done < per:
                    long_sum(done)
                    done += 1
            found = [jnp.sum(p, 0, keepdims=True) for p in parts]
            found.append(jnp.zeros((EDGE - len(taps), LANES), F32))
            sums[a // 2, a % 2 * EDGE : (a % 2 + 1) * EDGE, lanes] = jnp.concatenate(found, 0)
        for g in range(done, per):
            long_sum(g)
        return carry

    lax.fori_loop(0, width // LANES, tile, 0)
    keep[...] = sums[odd].astype(BF16)
    send[...] = sums[1 - odd].astype(BF16)


def main(features, cotangent, near, far, short_filter, bands, span, members):
    _, rows, width = features.shape
    taps = short_filter.shape[1]
    step = min(width, 512)
    per = LANES // members
    wide = rows + EDGE
    tall = rows + 2 * span
    half = (3 * EDGE + per) // 2
    return pl.pallas_call(
        functools.partial(main_kernel, span, members),
        grid=(width // step,),
        in_specs=[
            pl.BlockSpec((3, rows, step), lambda i: (0, 0, i)),
            pl.BlockSpec((rows, step), lambda i: (0, i)),
            pl.BlockSpec((span + 4 * EDGE, step), lambda i: (0, i)),
            pl.BlockSpec((span + 4 * EDGE, step), lambda i: (0, i)),
            pl.BlockSpec((3, taps, step), lambda i: (0, 0, i)),
            pl.BlockSpec((2, step // members * span, 2 * span), lambda i: (0, i, 0)),
        ],
        out_specs=[
            pl.BlockSpec((3, rows, step), lambda i: (0, 0, i)),
            pl.BlockSpec((half, step), lambda i: (0, i)),
            pl.BlockSpec((half, step), lambda i: (0, i)),
        ],
        out_shape=[
            jax.ShapeDtypeStruct((3, rows, width), BF16),
            jax.ShapeDtypeStruct((half, width), BF16),
            jax.ShapeDtypeStruct((half, width), BF16),
        ],
        scratch_shapes=[pltpu.VMEM((wide + EDGE, LANES), F32)] * 3
        + [pltpu.VMEM((wide, LANES), F32)] * 2
        + [pltpu.VMEM((tall, LANES), BF16)] * 2
        + [pltpu.VMEM((wide, LANES), F32)] * 3
        + [pltpu.VMEM((per * span // 2, 2 * rows // span * LANES), BF16)]
        + [pltpu.VMEM((2, half, step), F32)],
        compiler_params=pltpu.CompilerParams(vmem_limit_bytes=67043328),
        name="main",
    )(features, cotangent, near, far, short_filter, bands)


def finish_kernel(count, span, own, other, squares, grad_short, grad_long):
    odd = odd_place()
    taps = grad_short.shape[1]
    width = own.shape[1]
    per = own.shape[0] - EDGE
    total = jnp.sum(jnp.sum(squares[...], 0, keepdims=True), 1, keepdims=True)
    factor = lax.rsqrt(total / count + 1e-06)

    def put(low, high):
        grad_short[0] = low[0:taps, :] * factor
        grad_short[1] = low[EDGE : EDGE + taps, :] * factor
        grad_short[2] = high[0:taps, :] * factor
        for i in range(width // LANES):
            grad_long[i * per : (i + 1) * per, :] = (
                high[EDGE : EDGE + per, i * LANES : (i + 1) * LANES] * factor
            )

    @pl.when(odd == 0)
    def _():
        put(own, other)

    @pl.when(odd == 1)
    def _():
        put(other, own)


def finish(own, other, squares, taps, groups, span, count):
    width = own.shape[1]
    return pl.pallas_call(
        functools.partial(finish_kernel, count, span),
        out_shape=[
            jax.ShapeDtypeStruct((3, taps, width), F32),
            jax.ShapeDtypeStruct((groups, span), F32),
        ],
        name="finish",
    )(own, other, squares)


def square_kernel(own, other, out):
    total = None
    for x in (own, other):
        for at in range(0, x.shape[1], LANES):
            piece = x[:, at : at + LANES]
            square = jnp.sum((piece * piece).reshape(-1, EDGE, LANES), 0)
            total = square if total is None else total + square
    out[...] = total


def squares_of(own, other):
    return pl.pallas_call(
        square_kernel, out_shape=jax.ShapeDtypeStruct((EDGE, LANES), F32), name="squares"
    )(own, other)


def factors_of(size):
    found = []
    factor = 4
    while size > 1:
        while size % factor == 0:
            found.append(factor)
            size //= factor
        factor = 2 if factor == 4 else factor + 1
    return found


def swap(value, axis, stride, factor, turn):
    route = []
    for i in range(lax.axis_size(axis)):
        digit = i // stride % factor
        other = digit ^ turn if factor in (2, 4) else (digit + turn) % factor
        route.append((i, i + (other - digit) * stride))
    return lax.ppermute(value, axis, route)


def total_over(value, axis, stride, size, kind):
    value = value.astype(F32)
    for factor in factors_of(size):
        sent = value.astype(kind)
        got = [sent] + [swap(sent, axis, stride, factor, turn) for turn in range(1, factor)]
        got = [part.astype(F32) for part in got]
        if factor == 2:
            value = got[0] + got[1]
        elif factor == 4:
            value = (got[0] + got[1]) + (got[2] + got[3])
        else:
            digit = lax.axis_index(axis) // stride % factor
            every = jnp.stack(got[:1] + got[:0:-1])
            ordered = jnp.roll(every, -((factor - digit) % factor), 0)
            value = ordered[0]
            for part in ordered[1:]:
                value = value + part
        stride *= factor
    return value


def on_device(features, short_filter, long_filter, cotangent):
    _, rows, width = features.shape
    taps = short_filter.shape[1]
    groups, span = long_filter.shape
    members = width // groups
    size = lax.axis_size("ctx")
    near, far = edges(features, cotangent, short_filter, span)
    near = lax.ppermute(near, "ctx", [(i, i ^ 1) for i in range(size)])
    far = lax.ppermute(far, "ctx", [(i, (i + 1 ^ 1) - 1) for i in range(1, size - 1)])
    rounded = long_filter.astype(BF16).astype(F32)
    lines = jnp.stack(
        [
            jnp.pad(rounded[:, ::-1], ((0, 0), (1, span - 1))),
            jnp.pad(rounded, ((0, 0), (0, span))),
        ]
    )
    bands = toeplitz(lines, span)
    grads, keep, send = main(
        features, cotangent, near, far, short_filter, bands, span, members
    )
    own = keep.astype(F32) + swap(send, "ctx", 1, 2, 1).astype(F32)
    own = total_over(own, "ctx", 2, size // 2, BF16)
    other = swap(own, "ctx", 1, 2, 1)
    squares = total_over(squares_of(own, other), "ch", 1, lax.axis_size("ch"), F32)
    count = 3 * taps * D + span * G
    grad_short, grad_long = finish(own, other, squares, taps, groups, span, count)
    return (grads, grad_short, grad_long)


def solution(mesh):
    in_specs = (P(None, "ctx", "ch"), P(None, None, "ch"), P("ch", None), P("ctx", "ch"))
    out_specs = (P(None, "ctx", "ch"), P(None, None, "ch"), P("ch", None))
    return jax.shard_map(
        on_device, mesh=mesh, in_specs=in_specs, out_specs=out_specs, check_vma=False
    )
```

time: 82.6 us -> 74.2 us (0.90)
  Pallas kernels: 34.7 us -> 45.1 us
  starting transfers between devices: 21.3 us -> 13.2 us
  waiting for transfers between devices: 15.8 us -> 10.9 us
  local copies, waits for them, and re-layouts: 4.34 us -> 0.83 us
  other arithmetic: 4.71 us -> 2.9 us
    pallas_call x0 -> x3, Pallas kernels: none -> 12.7 us  [the longest x1 9.36 us: toeplitz(): pl.pallas_call(functools.partial(band_kernel, span), grid=(groups // step...]
    ppermute x7 -> x10, starting transfers between devices: 21.3 us -> 13.2 us  [the longest x8 11.2 us: swap(): return lax.ppermute(value, axis, route)]
    ppermute x7 -> x10, waiting for transfers between devices: 15.8 us -> 10.9 us  [the longest x8 10.9 us: swap(): return lax.ppermute(value, axis, route)]
    pallas_call x1, Pallas kernels: 30 us -> 27.6 us  [main(): pl.pallas_call(functools.partial(main_kernel, span, members), grid=(width...]
    reshape x2 -> x0, local copies, waits for them, and re-layouts: 1.32 us -> none  [the longest x1 0.69 us: on_device(): grad_short = scaled[:3 * EDGE].reshape(3, EDGE, width)[:, :taps]]
    convert_element_type x3 -> x1, other arithmetic: 1.98 us -> 0.86 us  [total_over(): sent = value.astype(kind)]
    unnamed x6, local copies, waits for them, and re-layouts: 1.68 us -> 0.65 us
  transfers between devices with their start and end apart: 7 -> 10, of which waited for: 6 -> 7; matrix products, arithmetic and copies ran while one was open for 1% -> 1% of each run, Pallas kernels for 0% -> 13%
where the time goes in v2:
time: 74.2 us; the launch traced here: 73.6 us
  Pallas kernels  45.1 us (61%)
  starting transfers between devices  13.2 us (18%)
  waiting for transfers between devices  10.9 us (15%)
  other arithmetic  2.9 us (4%)
  local copies, waits for them, and re-layouts  0.83 us (1%)
    pallas_call x1, Pallas kernels, main(): pl.pallas_call(functools.partial(main_kernel, span, members), grid=(width...  27.6 us
    ppermute x8, starting transfers between devices, swap(): return lax.ppermute(value, axis, route)  11.2 us
    ppermute x8, waiting for transfers between devices, swap(): return lax.ppermute(value, axis, route)  10.9 us
    pallas_call x1, Pallas kernels, toeplitz(): pl.pallas_call(functools.partial(band_kernel, span), grid=(groups // step...  9.36 us
    pallas_call x1, Pallas kernels, edges(): pl.pallas_call(functools.partial(edge_kernel, span), grid=(width // step,...  4.73 us
    pallas_call x1, Pallas kernels, finish(): pl.pallas_call(functools.partial(finish_kernel, count, span), out_shape=[...  1.77 us
    pallas_call x1, Pallas kernels, squares_of(): pl.pallas_call(square_kernel, out_shape=jax.ShapeDtypeStruct((EDGE, LANES...  1.6 us
    ppermute x1, starting transfers between devices, on_device(): lax.ppermute(far, 'ctx', [(i, (i + 1 ^ 1) - 1) for i in range(1, size - 1)])  1.52 us
  transfers between devices with their start and end apart: 10, of which 7 were waited for; matrix products, arithmetic and copies ran while one was open for 1% of the time, Pallas kernels for 13%

profile of v2, /device:TPU:0, one launch (start us, length us, event | category | flops | bytes accessed | tf_op | source)
XLA Modules:
  0.0 73.6 jit_solution(1687382071510484146)
XLA Ops:
  0.6 0.0 copy-start.2
  0.6 4.7 %edges.1 = (bf16[160,2048]{1,0:T(8,128)(2,1)}, bf16[160,2048]{1,0:T(8,128)(2,1)}) custom-call(bf16[3,256,2048]{2,1,0:T(8,128)(2,1)} %feat.3, bf16[256,2048]{1,0:T(8,128)(2,1)} %cot.3, f32[3,7,2048]{2,1,0:T(8,128)} %filt.3), custom_call_target="tpu_custom_call" | custom-call | tf_op jit(solution)/shard_map/edges/pallas_call | solution.py:87
  5.4 0.5 collective-permute-start
  5.9 1.5 %collective-permute-start.1 = (bf16[160,2048]{1,0:T(8,128)(2,1)}, bf16[160,2048]{1,0:T(8,128)(2,1)}, u32[]{:S(2)}, u32[]{:S(2)}) collective-permute-start(bf16[160,2048]{1,0:T(8,128)(2,1)} %get-tuple-element.11), channel_id=1, source_target_pairs={{4,8},{8,4},{12,16},{16,12},{20,24},{24,20},{5,9},{9,5},{13,17},{1... | collective-permute-start | bytes 1966088 | tf_op jit(solution)/shard_map/ppermute | solution.py:423
  7.4 0.0 copy-done.2
  7.4 0.1 rev.3
  7.5 0.1 pad_bitcast_fusion
  7.6 0.7 pad_maximum_fusion.lines
  8.3 9.4 %bands.1 = bf16[2,16384,256]{2,1,0:T(8,128)(2,1)} custom-call(f32[2,128,256]{2,1,0:T(8,128)} %pad_maximum_fusion.lines), custom_call_target="tpu_custom_call" | custom-call | bytes 16777216 | tf_op jit(solution)/shard_map/bands/pallas_call | solution.py:113
  17.7 0.0 collective-permute-done.near
  17.7 0.0 collective-permute-done.1.far
  17.7 27.6 %main.1 = (bf16[3,256,2048]{2,1,0:T(8,128)(2,1)}, bf16[16,2048]{1,0:T(8,128)(2,1)}, bf16[16,2048]{1,0:T(8,128)(2,1)}) custom-call(bf16[3,256,2048]{2,1,0:T(8,128)(2,1)} %feat.3, bf16[256,2048]{1,0:T(8,128)(2,1)} %cot.3, bf16[160,2048]{1,0:T(8,128)(2,1)} %collective-permute-done.near, bf16[160,2048]{1,0:T(8,128)(2,1)} %collective-permute-done.1.far, ...), custom_call_target="tpu_custom_call" | custom-call | tf_op jit(solution)/shard_map/main/pallas_call | solution.py:288
  45.3 3.1 %collective-permute-start.2 = (bf16[16,2048]{1,0:T(8,128)(2,1)}, bf16[16,2048]{1,0:T(8,128)(2,1)S(1)}, u32[]{:S(2)}, u32[]{:S(2)}) collective-permute-start(bf16[16,2048]{1,0:T(8,128)(2,1)} %get-tuple-element.14), channel_id=1, source_target_pairs={{0,4},{4,0},{8,12},{12,8},{16,20},{20,16},{24,28},{28,24},{1,5},{5... | collective-permute-start | bytes 196616 | tf_op jit(solution)/shard_map/ppermute | solution.py:391
  48.5 1.1 %collective-permute-done.2 = bf16[16,2048]{1,0:T(8,128)(2,1)S(1)} collective-permute-done((bf16[16,2048]{1,0:T(8,128)(2,1)}, bf16[16,2048]{1,0:T(8,128)(2,1)S(1)}, u32[]{:S(2)}, u32[]{:S(2)}) %collective-permute-start.2) | collective-permute-done | bytes 65568 | tf_op jit(solution)/shard_map/ppermute | solution.py:391
  49.6 0.9 %add_convert_fusion = bf16[16,2048]{1,0:T(8,128)(2,1)S(1)} fusion(bf16[16,2048]{1,0:T(8,128)(2,1)S(1)} %collective-permute-done.2, bf16[16,2048]{1,0:T(8,128)(2,1)} %get-tuple-element.13), kind=kLoop, calls=%fused_computation.2 | loop fusion | flops 131072 | bytes 196608 | tf_op jit(solution)/shard_map/convert_element_type | solution.py:397
  50.4 2.9 %collective-permute-start.5 = (bf16[16,2048]{1,0:T(8,128)(2,1)S(1)}, bf16[16,2048]{1,0:T(8,128)(2,1)S(1)}, u32[]{:S(2)}, u32[]{:S(2)}) collective-permute-start(bf16[16,2048]{1,0:T(8,128)(2,1)S(1)} %add_convert_fusion), channel_id=1, source_target_pairs={{0,24},{4,28},{8,16},{12,20},{16,8},{20,12},{24,0},{28,4},{1,25},{... | collective-permute-start | bytes 196616 | tf_op jit(solution)/shard_map/ppermute | solution.py:391
  53.3 0.2 collective-permute-start.4
  53.5 1.4 %collective-permute-start.3 = (bf16[16,2048]{1,0:T(8,128)(2,1)S(1)}, bf16[16,2048]{1,0:T(8,128)(2,1)S(1)}, u32[]{:S(2)}, u32[]{:S(2)}) collective-permute-start(bf16[16,2048]{1,0:T(8,128)(2,1)S(1)} %add_convert_fusion), channel_id=1, source_target_pairs={{0,8},{4,12},{8,0},{12,4},{16,24},{20,28},{24,16},{28,20},{1,9},{5... | collective-permute-start | bytes 196616 | tf_op jit(solution)/shard_map/ppermute | solution.py:391
  54.9 2.0 %collective-permute-done.5 = bf16[16,2048]{1,0:T(8,128)(2,1)S(1)} collective-permute-done((bf16[16,2048]{1,0:T(8,128)(2,1)S(1)}, bf16[16,2048]{1,0:T(8,128)(2,1)S(1)}, u32[]{:S(2)}, u32[]{:S(2)}) %collective-permute-start.5) | collective-permute-done | bytes 65568 | tf_op jit(solution)/shard_map/ppermute | solution.py:391
  56.8 3.2 %collective-permute-done.4 = bf16[16,2048]{1,0:T(8,128)(2,1)S(1)} collective-permute-done((bf16[16,2048]{1,0:T(8,128)(2,1)S(1)}, bf16[16,2048]{1,0:T(8,128)(2,1)S(1)}, u32[]{:S(2)}, u32[]{:S(2)}) %collective-permute-start.4) | collective-permute-done | bytes 65568 | tf_op jit(solution)/shard_map/ppermute | solution.py:391
  60.1 0.0 collective-permute-done.3
  60.1 0.0 copy-start
  60.1 0.1 collective-permute-start.6
  60.2 1.3 %collective-permute-done.6.other = f32[16,2048]{1,0:T(8,128)S(1)} collective-permute-done((f32[16,2048]{1,0:T(8,128)S(1)}, f32[16,2048]{1,0:T(8,128)S(1)}, u32[]{:S(2)}, u32[]{:S(2)}) %collective-permute-start.6) | collective-permute-done | bytes 131104 | tf_op jit(solution)/shard_map/ppermute | solution.py:391
  61.5 0.0 copy-done
  61.5 0.0 copy-start.1
  61.5 0.6 copy-done.1
  62.2 1.6 %squares.1 = f32[8,128]{1,0:T(8,128)} custom-call(f32[16,2048]{1,0:T(8,128)} %copy-done, f32[16,2048]{1,0:T(8,128)} %copy-done.1), custom_call_target="tpu_custom_call" | custom-call | tf_op jit(solution)/shard_map/squares/pallas_call | solution.py:369
  63.8 2.5 %collective-permute-start.9 = (f32[8,128]{1,0:T(8,128)}, f32[8,128]{1,0:T(8,128)S(1)}, u32[]{:S(2)}, u32[]{:S(2)}) collective-permute-start(f32[8,128]{1,0:T(8,128)} %squares.1), channel_id=1, source_target_pairs={{0,3},{1,2},{2,1},{3,0},{4,7},{5,6},{6,5},{7,4},{8,11},{9,10},{10,... | collective-permute-start | bytes 12296 | tf_op jit(solution)/shard_map/ppermute | solution.py:391
  66.2 0.5 collective-permute-start.8
  66.7 0.5 collective-permute-start.7
  67.3 1.2 %collective-permute-done.9 = f32[8,128]{1,0:T(8,128)S(1)} collective-permute-done((f32[8,128]{1,0:T(8,128)}, f32[8,128]{1,0:T(8,128)S(1)}, u32[]{:S(2)}, u32[]{:S(2)}) %collective-permute-start.9) | collective-permute-done | bytes 4128 | tf_op jit(solution)/shard_map/ppermute | solution.py:391
  68.5 1.6 %collective-permute-done.8 = f32[8,128]{1,0:T(8,128)S(1)} collective-permute-done((f32[8,128]{1,0:T(8,128)}, f32[8,128]{1,0:T(8,128)S(1)}, u32[]{:S(2)}, u32[]{:S(2)}) %collective-permute-start.8) | collective-permute-done | bytes 4128 | tf_op jit(solution)/shard_map/ppermute | solution.py:391
  70.0 0.5 collective-permute-done.7
  70.6 1.3 %add_add_fusion.1.squares = f32[8,128]{1,0:T(8,128)} fusion(f32[8,128]{1,0:T(8,128)S(1)} %collective-permute-done.8, f32[8,128]{1,0:T(8,128)S(1)} %collective-permute-done.9, f32[8,128]{1,0:T(8,128)} %squares.1, f32[8,128]{1,0:T(8,128)S(1)} %collective-permute-done.7), kind=kLoop, calls=%fused_computation.6 | loop fusion | flops 3072 | bytes 20480 | tf_op jit(solution)/shard_map/add | solution.py:403
  71.8 1.8 %finish.1 = (f32[3,7,2048]{2,1,0:T(8,128)}, f32[128,128]{1,0:T(8,128)}) custom-call(f32[16,2048]{1,0:T(8,128)} %copy-done, f32[16,2048]{1,0:T(8,128)} %copy-done.1, f32[8,128]{1,0:T(8,128)} %add_add_fusion.1.squares), custom_call_target="tpu_custom_call" | custom-call | tf_op jit(solution)/shard_map/finish/pallas_call | solution.py:348
  (2 shorter events, 0.0 us)
Async XLA Ops:
  0.6 6.7 %copy-start.2 = (f32[128,128]{1,0:T(8,128)S(1)}, f32[128,128]{1,0:T(8,128)}, u32[]{:S(2)}) copy-start(f32[128,128]{1,0:T(8,128)} %param.6) | copy-start | bytes 196612
  5.4 12.3 %collective-permute-start = (bf16[160,2048]{1,0:T(8,128)(2,1)}, bf16[160,2048]{1,0:T(8,128)(2,1)}, u32[]{:S(2)}, u32[]{:S(2)}) collective-permute-start(bf16[160,2048]{1,0:T(8,128)(2,1)} %get-tuple-element.10), channel_id=1, source_target_pairs={{0,4},{4,0},{8,12},{12,8},{16,20},{20,16},{24,28},{28,24},{1,5},{5... | collective-permute-start | bytes 1966088 | tf_op jit(solution)/shard_map/ppermute | solution.py:422
  5.9 11.8 %collective-permute-start.1 = (bf16[160,2048]{1,0:T(8,128)(2,1)}, bf16[160,2048]{1,0:T(8,128)(2,1)}, u32[]{:S(2)}, u32[]{:S(2)}) collective-permute-start(bf16[160,2048]{1,0:T(8,128)(2,1)} %get-tuple-element.11), channel_id=1, source_target_pairs={{4,8},{8,4},{12,16},{16,12},{20,24},{24,20},{5,9},{9,5},{13,17},{1... | collective-permute-start | bytes 1966088 | tf_op jit(solution)/shard_map/ppermute | solution.py:423
  45.3 4.3 %collective-permute-start.2 = (bf16[16,2048]{1,0:T(8,128)(2,1)}, bf16[16,2048]{1,0:T(8,128)(2,1)S(1)}, u32[]{:S(2)}, u32[]{:S(2)}) collective-permute-start(bf16[16,2048]{1,0:T(8,128)(2,1)} %get-tuple-element.14), channel_id=1, source_target_pairs={{0,4},{4,0},{8,12},{12,8},{16,20},{20,16},{24,28},{28,24},{1,5},{5... | collective-permute-start | bytes 196616 | tf_op jit(solution)/shard_map/ppermute | solution.py:391
  50.4 6.4 %collective-permute-start.5 = (bf16[16,2048]{1,0:T(8,128)(2,1)S(1)}, bf16[16,2048]{1,0:T(8,128)(2,1)S(1)}, u32[]{:S(2)}, u32[]{:S(2)}) collective-permute-start(bf16[16,2048]{1,0:T(8,128)(2,1)S(1)} %add_convert_fusion), channel_id=1, source_target_pairs={{0,24},{4,28},{8,16},{12,20},{16,8},{20,12},{24,0},{28,4},{1,25},{... | collective-permute-start | bytes 196616 | tf_op jit(solution)/shard_map/ppermute | solution.py:391
  53.3 6.8 %collective-permute-start.4 = (bf16[16,2048]{1,0:T(8,128)(2,1)S(1)}, bf16[16,2048]{1,0:T(8,128)(2,1)S(1)}, u32[]{:S(2)}, u32[]{:S(2)}) collective-permute-start(bf16[16,2048]{1,0:T(8,128)(2,1)S(1)} %add_convert_fusion), channel_id=1, source_target_pairs={{0,16},{4,20},{8,24},{12,28},{16,0},{20,4},{24,8},{28,12},{1,17},{... | collective-permute-start | bytes 196616 | tf_op jit(solution)/shard_map/ppermute | solution.py:391
  53.5 6.5 %collective-permute-start.3 = (bf16[16,2048]{1,0:T(8,128)(2,1)S(1)}, bf16[16,2048]{1,0:T(8,128)(2,1)S(1)}, u32[]{:S(2)}, u32[]{:S(2)}) collective-permute-start(bf16[16,2048]{1,0:T(8,128)(2,1)S(1)} %add_convert_fusion), channel_id=1, source_target_pairs={{0,8},{4,12},{8,0},{12,4},{16,24},{20,28},{24,16},{28,20},{1,9},{5... | collective-permute-start | bytes 196616 | tf_op jit(solution)/shard_map/ppermute | solution.py:391
  60.1 1.4 %copy-start = (f32[16,2048]{1,0:T(8,128)}, f32[16,2048]{1,0:T(8,128)S(1)}, u32[]{:S(2)}) copy-start(f32[16,2048]{1,0:T(8,128)S(1)} %add_add_fusion.own) | copy-start | bytes 393220
  60.1 1.4 %collective-permute-start.6 = (f32[16,2048]{1,0:T(8,128)S(1)}, f32[16,2048]{1,0:T(8,128)S(1)}, u32[]{:S(2)}, u32[]{:S(2)}) collective-permute-start(f32[16,2048]{1,0:T(8,128)S(1)} %add_add_fusion.own), channel_id=1, source_target_pairs={{0,4},{4,0},{8,12},{12,8},{16,20},{20,16},{24,28},{28,24},{1,5},{5... | collective-permute-start | bytes 393224 | tf_op jit(solution)/shard_map/ppermute | solution.py:391
  61.5 0.6 copy-start.1
  63.8 4.7 %collective-permute-start.9 = (f32[8,128]{1,0:T(8,128)}, f32[8,128]{1,0:T(8,128)S(1)}, u32[]{:S(2)}, u32[]{:S(2)}) collective-permute-start(f32[8,128]{1,0:T(8,128)} %squares.1), channel_id=1, source_target_pairs={{0,3},{1,2},{2,1},{3,0},{4,7},{5,6},{6,5},{7,4},{8,11},{9,10},{10,... | collective-permute-start | bytes 12296 | tf_op jit(solution)/shard_map/ppermute | solution.py:391
  66.2 3.8 %collective-permute-start.8 = (f32[8,128]{1,0:T(8,128)}, f32[8,128]{1,0:T(8,128)S(1)}, u32[]{:S(2)}, u32[]{:S(2)}) collective-permute-start(f32[8,128]{1,0:T(8,128)} %squares.1), channel_id=1, source_target_pairs={{0,2},{1,3},{2,0},{3,1},{4,6},{5,7},{6,4},{7,5},{8,10},{9,11},{10,... | collective-permute-start | bytes 12296 | tf_op jit(solution)/shard_map/ppermute | solution.py:391
  66.7 3.8 %collective-permute-start.7 = (f32[8,128]{1,0:T(8,128)}, f32[8,128]{1,0:T(8,128)S(1)}, u32[]{:S(2)}, u32[]{:S(2)}) collective-permute-start(f32[8,128]{1,0:T(8,128)} %squares.1), channel_id=1, source_target_pairs={{0,1},{1,0},{2,3},{3,2},{4,5},{5,4},{6,7},{7,6},{8,9},{9,8},{10,11... | collective-permute-start | bytes 12296 | tf_op jit(solution)/shard_map/ppermute | solution.py:391

commit v3 on v2

v3 whole, which is shorter than its diff:
```python
import functools

import jax
import jax.numpy as jnp
from jax import lax
from jax.experimental import pallas as pl
from jax.experimental.pallas import tpu as pltpu
from jax.sharding import PartitionSpec as P

D = 8192
G = 512
LANES = 128
EDGE = 8
F32 = jnp.float32
BF16 = jnp.bfloat16


def taps_of(filt, which, lanes):
    return [filt[which, pl.ds(j, 1), lanes] for j in range(filt.shape[1])]


def conv(source, taps, base, count):
    total = None
    for j, tap in enumerate(taps):
        term = tap * source[pl.ds(base - j, count), :]
        total = term if total is None else total + term
    return total


def chunks(count, size):
    return [(at, min(size, count - at)) for at in range(0, count, size)]


def odd_place():
    return lax.rem(lax.axis_index("ctx"), 2)


def edge_kernel(span, feat, cot, filt, near, far, qx, kx, vx):
    rows = feat.shape[1]
    width = feat.shape[2]
    reach = span + 2 * EDGE

    def run(ahead, back):
        def tile(i, carry):
            lanes = pl.ds(pl.multiple_of(i * LANES, LANES), LANES)
            qx[...] = feat[0, 0:reach, lanes].astype(F32)
            kx[...] = feat[1, rows - reach : rows, lanes].astype(F32)
            vx[...] = feat[2, rows - reach : rows, lanes].astype(F32)
            fq, fk, fv = (taps_of(filt, a, lanes) for a in range(3))
            for at, size in chunks(span, 32):
                z = conv(kx, fk, at + 2 * EDGE, size) * conv(vx, fv, at + 2 * EDGE, size)
                ahead[at : at + size, lanes] = z.astype(BF16)
            q_tail = feat[0, rows - 2 * EDGE : rows, lanes].astype(F32)[EDGE:]
            k_tail = kx[reach - EDGE : reach, :]
            v_tail = vx[reach - EDGE : reach, :]
            tails = jnp.concatenate([q_tail, k_tail, v_tail, v_tail], 0)
            ahead[span : span + 4 * EDGE, lanes] = tails.astype(BF16)
            for at, size in chunks(span + EDGE, 32):
                low = max(at, EDGE)
                c = cot[at : at + max(size, 2 * EDGE), lanes].astype(F32)[low - at : size]
                dy = conv(qx, fq, low, at + size - low) * c
                if at == 0:
                    dy = jnp.concatenate([qx[0:EDGE, :], dy], 0)
                back[at : at + size, lanes] = dy.astype(BF16)
            heads = [feat[a, 0 : 2 * EDGE, lanes].astype(F32)[:EDGE] for a in (1, 2)]
            heads.append(cot[0 : 2 * EDGE, lanes].astype(F32)[:EDGE])
            back[span + EDGE : span + 4 * EDGE, lanes] = jnp.concatenate(heads, 0).astype(BF16)
            return carry

        lax.fori_loop(0, width // LANES, tile, 0)

    odd = odd_place()

    @pl.when(odd == 0)
    def _():
        run(near, far)

    @pl.when(odd == 1)
    def _():
        run(far, near)


def edges(features, cotangent, short_filter, span):
    _, rows, width = features.shape
    taps = short_filter.shape[1]
    step = min(width, 1024)
    return pl.pallas_call(
        functools.partial(edge_kernel, span),
        grid=(width // step,),
        in_specs=[
            pl.BlockSpec((3, rows, step), lambda i: (0, 0, i)),
            pl.BlockSpec((rows, step), lambda i: (0, i)),
            pl.BlockSpec((3, taps, step), lambda i: (0, 0, i)),
        ],
        out_specs=[pl.BlockSpec((span + 4 * EDGE, step), lambda i: (0, i))] * 2,
        out_shape=[jax.ShapeDtypeStruct((span + 4 * EDGE, width), BF16)] * 2,
        scratch_shapes=[pltpu.VMEM((span + 2 * EDGE, LANES), F32)] * 3,
        name="edges",
    )(features, cotangent, short_filter)


def dot(a, b, dims=((1,), (0,))):
    return lax.dot_general(a, b, (dims, ((), ())), preferred_element_type=F32)


def owners(members, count):
    lane = lax.broadcasted_iota(jnp.int32, (1, LANES), 1) // members
    return jnp.concatenate([lane] * count, 1) if count > 1 else lane


def pick(stacked, size, owner, per):
    total = stacked[0:size]
    for g in range(1, per):
        total = jnp.where(owner == g, stacked[g * size : (g + 1) * size], total)
    return total


def strip(filters, g, shift):
    row = filters[g : g + 1, :]
    spread = jnp.concatenate([row, jnp.zeros_like(row)], 1)
    spread = jnp.broadcast_to(spread, (2 * EDGE, spread.shape[1]))
    return pltpu.roll(spread, shift, 1, stride=1, stride_axis=0).astype(BF16)


def reversing(size):
    r = lax.broadcasted_iota(jnp.int32, (size, size), 0)
    s = lax.broadcasted_iota(jnp.int32, (size, size), 1)
    return jnp.where(r + s == size - 1, 1.0, 0.0).astype(BF16)


def fill_band(out, g, base, span, per):
    rows = 2 * EDGE
    for at in range(0, span, rows):
        moved = base if at == 0 else pltpu.roll(base, at, 1)
        start = at * per + g * rows
        out[start : start + rows, :] = moved


def flipped(pieces, small):
    return dot(reversing(small), jnp.concatenate(pieces, 1)).astype(BF16)


def diagonal_sum(pairs, g, small, span):
    part = pltpu.roll(
        pairs[g * small : (g + 1) * small, :], 2 * span + 1 - small, 1, stride=1, stride_axis=0
    )
    return jnp.sum(part[:, :span], 0, keepdims=True)


def woven(first, second):
    live = [first, second]
    while live:
        for job in list(live):
            if next(job, True):
                live.remove(job)


def own_kernel(span, feat, cot, filt, ks_out, vs_out, z_out, dy_out, qx, kx, vx):
    rows = feat.shape[1]
    width = feat.shape[2]

    def tile(i, carry):
        lanes = pl.ds(pl.multiple_of(i * LANES, LANES), LANES)
        fq, fk, fv = (taps_of(filt, a, lanes) for a in range(3))
        for a, x in enumerate((qx, kx, vx)):
            for at, size in chunks(rows, 32):
                x[at : at + size, :] = feat[a, at : at + size, lanes].astype(F32)
        hole = jnp.zeros((EDGE, LANES), F32)
        for at, size in chunks(rows, 32):
            low = max(at, EDGE)
            c = cot[at : at + size, lanes].astype(F32)[low - at :]
            dy = c * conv(qx, fq, low, at + size - low)
            ks = conv(kx, fk, low, at + size - low)
            vs = conv(vx, fv, low, at + size - low)
            z = ks * vs
            ks_out[low : at + size, lanes] = ks
            vs_out[low : at + size, lanes] = vs
            if at == 0:
                z, dy = (jnp.concatenate([hole, x], 0) for x in (z, dy))
            z_out[at : at + size, lanes] = z.astype(BF16)
            dy_out[at : at + size, lanes] = dy.astype(BF16)
        return carry

    @pl.when(pl.program_id(0) >= 0)
    def _():
        ks_out[0:EDGE, :] = jnp.zeros((EDGE, width), F32)
        vs_out[0:EDGE, :] = jnp.zeros((EDGE, width), F32)

    lax.fori_loop(0, width // LANES, tile, 0)


def column_spec(step, *shape):
    return pl.BlockSpec(shape + (step,), lambda i: (0,) * len(shape) + (i,))


def own_part(features, cotangent, short_filter, span):
    _, rows, width = features.shape
    taps = short_filter.shape[1]
    step = min(width, 512)
    column = functools.partial(column_spec, step)
    kinds = [F32, F32, BF16, BF16]
    return pl.pallas_call(
        functools.partial(own_kernel, span),
        grid=(width // step,),
        in_specs=[column(3, rows), column(rows), column(3, taps)],
        out_specs=[column(rows)] * 4,
        out_shape=[jax.ShapeDtypeStruct((rows, width), kind) for kind in kinds],
        scratch_shapes=[pltpu.VMEM((rows, LANES), F32)] * 3,
        compiler_params=pltpu.CompilerParams(vmem_limit_bytes=67043328),
        cost_estimate=pl.CostEstimate(
            flops=40 * rows * width, bytes_accessed=20 * rows * width, transcendentals=0
        ),
        name="own",
    )(features, cotangent, short_filter)


def join_kernel(
    span, members,
    feat, cot, near, far, filt, lines, ks_in, vs_in, z_in, dy_in,
    grads, keep, send, sums, *scratch,
):
    rows = feat.shape[1]
    width = feat.shape[2]
    per = LANES // members
    blocks = rows // span
    small = span // 2
    wide = rows + EDGE
    odd = odd_place()
    count = len(scratch) // 2
    sets = (scratch[:count], scratch[count:])

    @pl.when(pl.program_id(0) == 0)
    def _():
        for bufs in sets:
            for ref in bufs[3:5]:
                ref[...] = jnp.zeros_like(ref)

    hole = jnp.zeros((EDGE, LANES), F32)

    def halves(low, high):
        return jnp.concatenate([low, high], 0).astype(BF16)

    def column(i):
        return pl.ds(i * LANES, LANES)

    def first_stage(i, bufs):
        qx, kx, vx, zx, dyx, dqx, dkx, dvx, tst, ust, zm, pairs = bufs
        lanes = column(i)
        fq, fk, fv = (taps_of(filt, a, lanes) for a in range(3))

        def ahead(low, high):
            return jnp.where(odd == 1, near[low:high, lanes], far[low:high, lanes])

        def back(low, high):
            return jnp.where(odd == 1, far[low:high, lanes], near[low:high, lanes])

        ends = ahead(span, span + 4 * EDGE).astype(F32)
        first = back(0, 2 * EDGE).astype(F32)
        last = back(span + EDGE, span + 4 * EDGE).astype(F32)
        nexts = (first[:EDGE], last[:EDGE], last[EDGE : 2 * EDGE])
        c_next = last[2 * EDGE :]
        c_first = cot[0 : 2 * EDGE, lanes].astype(F32)[:EDGE]
        for a, x in enumerate((qx, kx, vx)):
            x[0:EDGE, :] = ends[a * EDGE : (a + 1) * EDGE]
            x[EDGE : 2 * EDGE, :] = feat[a, 0 : 2 * EDGE, lanes].astype(F32)[:EDGE]
            x[2 * EDGE : 3 * EDGE, :] = feat[a, rows - 2 * EDGE : rows, lanes].astype(F32)[EDGE:]
            x[3 * EDGE : 4 * EDGE, :] = nexts[a]
        dy_first = c_first * conv(qx, fq, EDGE, EDGE)
        dy_next = c_next * conv(qx, fq, 3 * EDGE, EDGE)
        ks_first, vs_first = conv(kx, fk, EDGE, EDGE), conv(vx, fv, EDGE, EDGE)
        ks_next, vs_next = conv(kx, fk, 3 * EDGE, EDGE), conv(vx, fv, 3 * EDGE, EDGE)
        top = slice(0, 2 * EDGE)
        dyx[0 : 2 * EDGE, :] = halves(dy_first, dy_in[top, lanes].astype(F32)[EDGE:])
        dyx[2 * EDGE : rows, :] = dy_in[2 * EDGE : rows, lanes]
        dyx[rows : rows + 2 * EDGE, :] = halves(dy_next, first[EDGE:])
        dyx[rows + 2 * EDGE : rows + span + EDGE, :] = back(2 * EDGE, span + EDGE)
        zx[0:span, :] = ahead(0, span)
        z_top = halves(ks_first * vs_first, z_in[top, lanes].astype(F32)[EDGE:])
        zx[span : span + 2 * EDGE, :] = z_top
        zx[span + 2 * EDGE : span + rows, :] = z_in[2 * EDGE : rows, lanes]
        zx[span + rows : span + rows + 2 * EDGE, :] = halves(ks_next * vs_next, hole)

        owner = owners(members, blocks)
        one = owners(members, 1)
        rows16 = 2 * EDGE

        def windows(ref):
            return jnp.concatenate([ref[b * span : (b + 2) * span, :] for b in range(blocks)], 1)

        def chunk_of(stacked, at, who):
            start = at * per
            return pick(stacked[start : start + rows16 * per], rows16, who, per)

        filters = lines[i * per : (i + 1) * per, :].astype(BF16)
        turned = dot(filters, reversing(span))
        filters = filters.astype(F32)
        for g in range(per):
            fill_band(ust, g, strip(filters, g, 0), span, per)
            yield False
        dz = dot(ust[...], windows(dyx))
        dz_next = chunk_of(dot(ust[0 : rows16 * per, :], dyx[rows : rows + 2 * span, :]), 0, one)
        dkx[rows:wide, :] = dz_next[:EDGE] * vs_next
        dvx[rows:wide, :] = dz_next[:EDGE] * ks_next
        left = list(range(per))
        for at in range(0, span, rows16):
            piece = chunk_of(dz, at, owner)
            for b in range(blocks):
                t = b * span + at
                part = piece[:, b * LANES : (b + 1) * LANES]
                vs, ks = vs_in[t : t + rows16, lanes], ks_in[t : t + rows16, lanes]
                if t == 0:
                    vs = jnp.concatenate([vs_first, vs[EDGE:]], 0)
                    ks = jnp.concatenate([ks_first, ks[EDGE:]], 0)
                dkx[t : t + rows16, :] = part * vs
                dvx[t : t + rows16, :] = part * ks
            if left:
                g = left.pop(0)
                fill_band(tst, g, strip(turned, g, 1), span, per)
            yield False
        for g in left:
            fill_band(tst, g, strip(turned, g, 1), span, per)
        y = dot(tst[...], windows(zx))
        y_next = chunk_of(dot(tst[0 : rows16 * per, :], zx[rows : rows + 2 * span, :]), 0, one)
        dqx[rows:wide, :] = c_next * y_next[:EDGE]
        starts = range(0, rows, small)
        z_back = flipped([zx[span + t : span + t + small, :] for t in starts], small)
        who = owners(members, len(starts))
        left = list(range(per))

        def mask(g):
            kept = jnp.where(who == g, 1.0, 0.0).astype(BF16)
            zm[g * small : (g + 1) * small, :] = z_back * kept

        for at in range(0, span, rows16):
            piece = chunk_of(y, at, owner)
            for b in range(blocks):
                t = b * span + at
                c = cot[t : t + rows16, lanes].astype(F32)
                dqx[t : t + rows16, :] = c * piece[:, b * LANES : (b + 1) * LANES]
            if left:
                mask(left.pop(0))
            yield False
        for g in left:
            mask(g)
        near_rows = jnp.concatenate([dyx[t : t + 2 * span, :] for t in starts], 1)
        pairs[...] = dot(zm[...], near_rows, ((1,), (1,)))

    def second_stage(i, bufs):
        qx, kx, vx, zx, dyx, dqx, dkx, dvx, tst, ust, zm, pairs = bufs
        lanes = column(i)
        left = list(range(per))

        def diagonal(g):
            sums[1, EDGE + g : EDGE + g + 1, lanes] = diagonal_sum(pairs, g, small, span)

        for a, dx in zip((1, 2, 0), (dkx, dvx, dqx)):
            taps = taps_of(filt, a, lanes)
            parts = [None] * len(taps)
            for at, size in chunks(rows, 32):
                own = feat[a, at : at + size, lanes].astype(F32)
                total = None
                for j, tap in enumerate(taps):
                    moved = dx[pl.ds(at + j, size), :]
                    term = tap * moved
                    total = term if total is None else total + term
                    prod = jnp.sum((own * moved).reshape(size // EDGE, EDGE, LANES), 0)
                    parts[j] = prod if parts[j] is None else parts[j] + prod
                grads[a, at : at + size, lanes] = total.astype(BF16)
                if left:
                    diagonal(left.pop(0))
                yield False
            found = [jnp.sum(p, 0, keepdims=True) for p in parts]
            found.append(jnp.zeros((EDGE - len(taps), LANES), F32))
            sums[a // 2, a % 2 * EDGE : (a % 2 + 1) * EDGE, lanes] = jnp.concatenate(found, 0)
        for g in left:
            diagonal(g)

    tiles = width // LANES
    woven(first_stage(0, sets[0]), iter(()))

    for i in range(tiles):
        after = first_stage(i + 1, sets[(i + 1) % 2]) if i + 1 < tiles else iter(())
        woven(after, second_stage(i, sets[i % 2]))
    keep[...] = sums[odd].astype(BF16)
    send[...] = sums[1 - odd].astype(BF16)


def join(features, cotangent, got, short_filter, long_filter, parts, span, members):
    _, rows, width = features.shape
    taps = short_filter.shape[1]
    step = min(width, 1024)
    per = LANES // members
    wide = rows + EDGE
    tall = rows + 2 * span
    half = (3 * EDGE + per) // 2
    column = functools.partial(column_spec, step)
    buffers = (
        [pltpu.VMEM((4 * EDGE, LANES), F32)] * 3
        + [pltpu.VMEM((tall, LANES), BF16)] * 2
        + [pltpu.VMEM((wide, LANES), F32)] * 3
        + [pltpu.VMEM((per * span, 2 * span), BF16)] * 2
        + [pltpu.VMEM((per * span // 2, 2 * rows // span * LANES), BF16)]
        + [pltpu.VMEM((per * span // 2, 2 * span), F32)]
    )
    return pl.pallas_call(
        functools.partial(join_kernel, span, members),
        grid=(width // step,),
        in_specs=[
            column(3, rows),
            column(rows),
            column(span + 4 * EDGE),
            column(span + 4 * EDGE),
            column(3, taps),
            pl.BlockSpec((step // members, span), lambda i: (i, 0)),
            *[column(rows)] * 4,
        ],
        out_specs=[column(3, rows), column(half), column(half)],
        out_shape=[
            jax.ShapeDtypeStruct((3, rows, width), BF16),
            jax.ShapeDtypeStruct((half, width), BF16),
            jax.ShapeDtypeStruct((half, width), BF16),
        ],
        scratch_shapes=[pltpu.VMEM((2, half, step), F32)] + buffers * 2,
        compiler_params=pltpu.CompilerParams(vmem_limit_bytes=67043328),
        name="join",
    )(features, cotangent, *got, short_filter, long_filter, *parts)


def finish_kernel(count, own, other, *refs):
    *squares, grad_short, grad_long = refs
    odd = odd_place()
    taps = grad_short.shape[1]
    width = own.shape[1]
    per = own.shape[0] - EDGE
    found = [ref[...] for ref in squares]
    while len(found) > 1:
        found = [sum(found[at : at + 2]) for at in range(0, len(found), 2)]
    total = jnp.sum(jnp.sum(found[0], 0, keepdims=True), 1, keepdims=True)
    factor = lax.rsqrt(total / count + 1e-06)

    def put(low, high):
        grad_short[0] = low[0:taps, :] * factor
        grad_short[1] = low[EDGE : EDGE + taps, :] * factor
        grad_short[2] = high[0:taps, :] * factor
        for i in range(width // LANES):
            grad_long[i * per : (i + 1) * per, :] = (
                high[EDGE : EDGE + per, i * LANES : (i + 1) * LANES] * factor
            )

    @pl.when(odd == 0)
    def _():
        put(own, other)

    @pl.when(odd == 1)
    def _():
        put(other, own)


def finish(own, other, squares, taps, groups, span, count):
    width = own.shape[1]
    return pl.pallas_call(
        functools.partial(finish_kernel, count),
        out_shape=[
            jax.ShapeDtypeStruct((3, taps, width), F32),
            jax.ShapeDtypeStruct((groups, span), F32),
        ],
        name="finish",
    )(own, other, *squares)


def square_kernel(own, other, out):
    total = None
    for x in (own, other):
        for at in range(0, x.shape[1], LANES):
            piece = x[:, at : at + LANES]
            square = jnp.sum((piece * piece).reshape(-1, EDGE, LANES), 0)
            total = square if total is None else total + square
    out[...] = total


def squares_of(own, other):
    return pl.pallas_call(
        square_kernel, out_shape=jax.ShapeDtypeStruct((EDGE, LANES), F32), name="squares"
    )(own, other)


def factors_of(size):
    found = []
    factor = 4
    while size > 1:
        while size % factor == 0:
            found.append(factor)
            size //= factor
        factor = 2 if factor == 4 else factor + 1
    return found


def swap(value, axis, stride, factor, turn):
    route = []
    for i in range(lax.axis_size(axis)):
        digit = i // stride % factor
        other = digit ^ turn if factor in (2, 4) else (digit + turn) % factor
        route.append((i, i + (other - digit) * stride))
    return lax.ppermute(value, axis, route)


def total_over(value, axis, stride, size, kind):
    value = value.astype(F32)
    for factor in factors_of(size):
        sent = value.astype(kind)
        got = [sent] + [swap(sent, axis, stride, factor, turn) for turn in range(1, factor)]
        got = [part.astype(F32) for part in got]
        if factor == 2:
            value = got[0] + got[1]
        elif factor == 4:
            value = (got[0] + got[1]) + (got[2] + got[3])
        else:
            digit = lax.axis_index(axis) // stride % factor
            every = jnp.stack(got[:1] + got[:0:-1])
            ordered = jnp.roll(every, -((factor - digit) % factor), 0)
            value = ordered[0]
            for part in ordered[1:]:
                value = value + part
        stride *= factor
    return value


def on_device(features, short_filter, long_filter, cotangent):
    _, rows, width = features.shape
    taps = short_filter.shape[1]
    groups, span = long_filter.shape
    members = width // groups
    size = lax.axis_size("ctx")
    near, far = edges(features, cotangent, short_filter, span)
    got = (
        lax.ppermute(near, "ctx", [(i, i ^ 1) for i in range(size)]),
        lax.ppermute(far, "ctx", [(i, (i + 1 ^ 1) - 1) for i in range(1, size - 1)]),
    )
    parts = own_part(features, cotangent, short_filter, span)
    grads, keep, send = join(
        features, cotangent, got, short_filter, long_filter, parts, span, members
    )
    own = keep.astype(F32) + swap(send, "ctx", 1, 2, 1).astype(F32)
    own = total_over(own, "ctx", 2, size // 2, BF16)
    other = swap(own, "ctx", 1, 2, 1)
    *early, late = factors_of(lax.axis_size("ch"))
    squares = squares_of(own, other)
    stride = 1
    for factor in early:
        squares = total_over(squares, "ch", stride, factor, F32)
        stride *= factor
    squares = [squares] + [swap(squares, "ch", stride, late, turn) for turn in range(1, late)]
    count = 3 * taps * D + span * G
    grad_short, grad_long = finish(own, other, squares, taps, groups, span, count)
    return (grads, grad_short, grad_long)


def solution(mesh):
    in_specs = (P(None, "ctx", "ch"), P(None, None, "ch"), P("ch", None), P("ctx", "ch"))
    out_specs = (P(None, "ctx", "ch"), P(None, None, "ch"), P("ch", None))
    return jax.shard_map(
        on_device, mesh=mesh, in_specs=in_specs, out_specs=out_specs, check_vma=False
    )
```

time: 74.2 us -> 63 us (0.85)
  Pallas kernels: 45.1 us -> 33.7 us
  other arithmetic: 2.9 us -> 0.89 us
  starting transfers between devices: 13.2 us -> 14.8 us
    pallas_call x3, Pallas kernels: 38.8 us -> 27.4 us  [the longest x1 18.5 us: join(): pl.pallas_call(functools.partial(join_kernel, span, members), grid=(width...]
    ppermute x8, starting transfers between devices: 11.2 us -> 12.8 us  [swap(): return lax.ppermute(value, axis, route)]
    add x2 -> x1, other arithmetic: 1.31 us -> 0.03 us  [total_over(): value = got[0] + got[1] + (got[2] + got[3])]
  transfers between devices with their start and end apart: 10 -> 10, of which waited for: 7 -> 7; matrix products, arithmetic and copies ran while one was open for 1% -> 0% of each run, Pallas kernels for 13% -> 11%
where the time goes in v3:
time: 63 us; the launch traced here: 62.7 us
  Pallas kernels  33.7 us (53%)
  starting transfers between devices  14.8 us (23%)
  waiting for transfers between devices  11.2 us (18%)
  local copies, waits for them, and re-layouts  1.34 us (2%)
  other arithmetic  0.89 us (1%)
  between operations  0.67 us (1%)
    pallas_call x1, Pallas kernels, join(): pl.pallas_call(functools.partial(join_kernel, span, members), grid=(width...  18.5 us
    ppermute x8, starting transfers between devices, swap(): return lax.ppermute(value, axis, route)  12.8 us
    ppermute x8, waiting for transfers between devices, swap(): return lax.ppermute(value, axis, route)  11.2 us
    pallas_call x1, Pallas kernels, own_part(): pl.pallas_call(functools.partial(own_kernel, span), grid=(width // step,)...  7.11 us
    pallas_call x1, Pallas kernels, edges(): pl.pallas_call(functools.partial(edge_kernel, span), grid=(width // step,...  4.75 us
    pallas_call x1, Pallas kernels, finish(): pl.pallas_call(functools.partial(finish_kernel, count), out_shape=[jax.Sh...  1.78 us
    pallas_call x1, Pallas kernels, squares_of(): pl.pallas_call(square_kernel, out_shape=jax.ShapeDtypeStruct((EDGE, LANES...  1.59 us
    ppermute x1, starting transfers between devices, on_device(): lax.ppermute(far, 'ctx', [(i, (i + 1 ^ 1) - 1) for i in range(1, size - 1)])  1.56 us
  transfers between devices with their start and end apart: 10, of which 7 were waited for; matrix products, arithmetic and copies ran while one was open for 0% of the time, Pallas kernels for 11%

profile of v3, /device:TPU:0, one launch (start us, length us, event | category | flops | bytes accessed | tf_op | source)
XLA Modules:
  0.0 62.7 jit_solution(5720942184556879806)
XLA Ops:
  0.6 4.8 %edges.1 = (bf16[160,2048]{1,0:T(8,128)(2,1)}, bf16[160,2048]{1,0:T(8,128)(2,1)}) custom-call(bf16[3,256,2048]{2,1,0:T(8,128)(2,1)} %feat.5, bf16[256,2048]{1,0:T(8,128)(2,1)} %cot.5, f32[3,7,2048]{2,1,0:T(8,128)} %filt.5), custom_call_target="tpu_custom_call" | custom-call | tf_op jit(solution)/shard_map/edges/pallas_call | solution.py:87
  5.4 0.5 collective-permute-start
  5.9 1.6 %collective-permute-start.1 = (bf16[160,2048]{1,0:T(8,128)(2,1)}, bf16[160,2048]{1,0:T(8,128)(2,1)}, u32[]{:S(2)}, u32[]{:S(2)}) collective-permute-start(bf16[160,2048]{1,0:T(8,128)(2,1)} %get-tuple-element.15), channel_id=1, source_target_pairs={{4,8},{8,4},{12,16},{16,12},{20,24},{24,20},{5,9},{9,5},{13,17},{1... | collective-permute-start | bytes 1966088 | tf_op jit(solution)/shard_map/ppermute | solution.py:537
  7.4 7.1 %own.1 = (f32[256,2048]{1,0:T(8,128)}, f32[256,2048]{1,0:T(8,128)}, bf16[256,2048]{1,0:T(8,128)(2,1)}, bf16[256,2048]{1,0:T(8,128)(2,1)}) custom-call(bf16[3,256,2048]{2,1,0:T(8,128)(2,1)} %feat.5, bf16[256,2048]{1,0:T(8,128)(2,1)} %cot.5, f32[3,7,2048]{2,1,0:T(8,128)} %filt.5), custom_call_target="tpu_custom_call" | custom-call | flops 20971520 | bytes 10485760 | tf_op jit(solution)/shard_map/own/pallas_call | solution.py:202
  14.5 0.0 collective-permute-done.near
  14.5 0.0 collective-permute-done.1.far
  14.6 18.5 %join.1 = (bf16[3,256,2048]{2,1,0:T(8,128)(2,1)}, bf16[16,2048]{1,0:T(8,128)(2,1)}, bf16[16,2048]{1,0:T(8,128)(2,1)}) custom-call(bf16[3,256,2048]{2,1,0:T(8,128)(2,1)} %feat.5, bf16[256,2048]{1,0:T(8,128)(2,1)} %cot.5, bf16[160,2048]{1,0:T(8,128)(2,1)} %collective-permute-done.near, bf16[160,2048]{1,0:T(8,128)(2,1)} %collective-permute-done.1.far, ...), custom_call_target="tpu_custom_call" | custom-call | tf_op jit(solution)/shard_map/join/pallas_call | solution.py:405
  33.0 4.5 %collective-permute-start.2 = (bf16[16,2048]{1,0:T(8,128)(2,1)}, bf16[16,2048]{1,0:T(8,128)(2,1)S(1)}, u32[]{:S(2)}, u32[]{:S(2)}) collective-permute-start(bf16[16,2048]{1,0:T(8,128)(2,1)} %get-tuple-element.22), channel_id=1, source_target_pairs={{0,4},{4,0},{8,12},{12,8},{16,20},{20,16},{24,28},{28,24},{1,5},{5... | collective-permute-start | bytes 196616 | tf_op jit(solution)/shard_map/ppermute | solution.py:504
  37.6 1.1 %collective-permute-done.2 = bf16[16,2048]{1,0:T(8,128)(2,1)S(1)} collective-permute-done((bf16[16,2048]{1,0:T(8,128)(2,1)}, bf16[16,2048]{1,0:T(8,128)(2,1)S(1)}, u32[]{:S(2)}, u32[]{:S(2)}) %collective-permute-start.2) | collective-permute-done | bytes 65568 | tf_op jit(solution)/shard_map/ppermute | solution.py:504
  38.7 0.9 %add_convert_fusion = bf16[16,2048]{1,0:T(8,128)(2,1)S(1)} fusion(bf16[16,2048]{1,0:T(8,128)(2,1)S(1)} %collective-permute-done.2, bf16[16,2048]{1,0:T(8,128)(2,1)} %get-tuple-element.21), kind=kLoop, calls=%fused_computation.1 | loop fusion | flops 131072 | bytes 196608 | tf_op jit(solution)/shard_map/convert_element_type | solution.py:510
  39.5 4.1 %collective-permute-start.5 = (bf16[16,2048]{1,0:T(8,128)(2,1)S(1)}, bf16[16,2048]{1,0:T(8,128)(2,1)S(1)}, u32[]{:S(2)}, u32[]{:S(2)}) collective-permute-start(bf16[16,2048]{1,0:T(8,128)(2,1)S(1)} %add_convert_fusion), channel_id=1, source_target_pairs={{0,24},{4,28},{8,16},{12,20},{16,8},{20,12},{24,0},{28,4},{1,25},{... | collective-permute-start | bytes 196616 | tf_op jit(solution)/shard_map/ppermute | solution.py:504
  43.6 0.0 collective-permute-start.4
  43.6 0.6 %collective-permute-start.3 = (bf16[16,2048]{1,0:T(8,128)(2,1)S(1)}, bf16[16,2048]{1,0:T(8,128)(2,1)S(1)}, u32[]{:S(2)}, u32[]{:S(2)}) collective-permute-start(bf16[16,2048]{1,0:T(8,128)(2,1)S(1)} %add_convert_fusion), channel_id=1, source_target_pairs={{0,8},{4,12},{8,0},{12,4},{16,24},{20,28},{24,16},{28,20},{1,9},{5... | collective-permute-start | bytes 196616 | tf_op jit(solution)/shard_map/ppermute | solution.py:504
  44.2 1.9 %collective-permute-done.5 = bf16[16,2048]{1,0:T(8,128)(2,1)S(1)} collective-permute-done((bf16[16,2048]{1,0:T(8,128)(2,1)S(1)}, bf16[16,2048]{1,0:T(8,128)(2,1)S(1)}, u32[]{:S(2)}, u32[]{:S(2)}) %collective-permute-start.5) | collective-permute-done | bytes 65568 | tf_op jit(solution)/shard_map/ppermute | solution.py:504
  46.1 3.6 %collective-permute-done.4 = bf16[16,2048]{1,0:T(8,128)(2,1)S(1)} collective-permute-done((bf16[16,2048]{1,0:T(8,128)(2,1)S(1)}, bf16[16,2048]{1,0:T(8,128)(2,1)S(1)}, u32[]{:S(2)}, u32[]{:S(2)}) %collective-permute-start.4) | collective-permute-done | bytes 65568 | tf_op jit(solution)/shard_map/ppermute | solution.py:504
  49.7 0.0 collective-permute-done.3
  49.8 0.0 copy-start
  49.8 0.1 collective-permute-start.6
  49.9 1.3 %collective-permute-done.6.other = f32[16,2048]{1,0:T(8,128)S(1)} collective-permute-done((f32[16,2048]{1,0:T(8,128)S(1)}, f32[16,2048]{1,0:T(8,128)S(1)}, u32[]{:S(2)}, u32[]{:S(2)}) %collective-permute-start.6) | collective-permute-done | bytes 131104 | tf_op jit(solution)/shard_map/ppermute | solution.py:504
  51.2 0.0 copy-done
  51.2 0.0 copy-start.1
  51.2 0.7 %copy-done.1 = f32[16,2048]{1,0:T(8,128)} copy-done((f32[16,2048]{1,0:T(8,128)}, f32[16,2048]{1,0:T(8,128)S(1)}, u32[]{:S(2)}) %copy-start.1) | copy-done | bytes 131096
  51.8 1.6 %squares.1.refs_0_ = f32[8,128]{1,0:T(8,128)} custom-call(f32[16,2048]{1,0:T(8,128)} %copy-done, f32[16,2048]{1,0:T(8,128)} %copy-done.1), custom_call_target="tpu_custom_call" | custom-call | tf_op jit(solution)/shard_map/squares/pallas_call | solution.py:482
  53.4 2.4 %collective-permute-start.9 = (f32[8,128]{1,0:T(8,128)}, f32[8,128]{1,0:T(8,128)S(1)}, u32[]{:S(2)}, u32[]{:S(2)}) collective-permute-start(f32[8,128]{1,0:T(8,128)} %squares.1.refs_0_), channel_id=1, source_target_pairs={{0,3},{1,2},{2,1},{3,0},{4,7},{5,6},{6,5},{7,4},{8,11},{9,10},{10,... | collective-permute-start | bytes 12296 | tf_op jit(solution)/shard_map/ppermute | solution.py:504
  55.9 0.5 collective-permute-start.8
  56.4 0.5 collective-permute-start.7
  56.9 1.2 %collective-permute-done.9.refs_3_ = f32[8,128]{1,0:T(8,128)S(1)} collective-permute-done((f32[8,128]{1,0:T(8,128)}, f32[8,128]{1,0:T(8,128)S(1)}, u32[]{:S(2)}, u32[]{:S(2)}) %collective-permute-start.9) | collective-permute-done | bytes 4128 | tf_op jit(solution)/shard_map/ppermute | solution.py:504
  58.2 0.0 copy-start.2
  58.2 1.5 %collective-permute-done.8.refs_2_ = f32[8,128]{1,0:T(8,128)S(1)} collective-permute-done((f32[8,128]{1,0:T(8,128)}, f32[8,128]{1,0:T(8,128)S(1)}, u32[]{:S(2)}, u32[]{:S(2)}) %collective-permute-start.8) | collective-permute-done | bytes 4128 | tf_op jit(solution)/shard_map/ppermute | solution.py:504
  59.7 0.0 copy-start.3
  59.7 0.5 collective-permute-done.7.refs_1_
  60.2 0.0 copy-done.2
  60.2 0.1 copy-done.3
  60.3 0.0 copy-start.4
  60.3 0.6 copy-done.4
  60.9 1.8 %finish.1 = (f32[3,7,2048]{2,1,0:T(8,128)}, f32[128,128]{1,0:T(8,128)}) custom-call(f32[16,2048]{1,0:T(8,128)} %copy-done, f32[16,2048]{1,0:T(8,128)} %copy-done.1, f32[8,128]{1,0:T(8,128)} %squares.1.refs_0_, f32[8,128]{1,0:T(8,128)} %copy-done.4, f32[8,128]{1,0:T(8,128)} %copy-done.3, f32[8,128]{1,0:T(8,128)} %copy-done.2), custom_call_target="tpu_custom_call" | custom-call | tf_op jit(solution)/shard_map/finish/pallas_call | solution.py:461
  (1 shorter events, 0.0 us)
Async XLA Ops:
  5.4 9.2 %collective-permute-start = (bf16[160,2048]{1,0:T(8,128)(2,1)}, bf16[160,2048]{1,0:T(8,128)(2,1)}, u32[]{:S(2)}, u32[]{:S(2)}) collective-permute-start(bf16[160,2048]{1,0:T(8,128)(2,1)} %get-tuple-element.14), channel_id=1, source_target_pairs={{0,4},{4,0},{8,12},{12,8},{16,20},{20,16},{24,28},{28,24},{1,5},{5... | collective-permute-start | bytes 1966088 | tf_op jit(solution)/shard_map/ppermute | solution.py:536
  5.9 8.7 %collective-permute-start.1 = (bf16[160,2048]{1,0:T(8,128)(2,1)}, bf16[160,2048]{1,0:T(8,128)(2,1)}, u32[]{:S(2)}, u32[]{:S(2)}) collective-permute-start(bf16[160,2048]{1,0:T(8,128)(2,1)} %get-tuple-element.15), channel_id=1, source_target_pairs={{4,8},{8,4},{12,16},{16,12},{20,24},{24,20},{5,9},{9,5},{13,17},{1... | collective-permute-start | bytes 1966088 | tf_op jit(solution)/shard_map/ppermute | solution.py:537
  33.0 5.6 %collective-permute-start.2 = (bf16[16,2048]{1,0:T(8,128)(2,1)}, bf16[16,2048]{1,0:T(8,128)(2,1)S(1)}, u32[]{:S(2)}, u32[]{:S(2)}) collective-permute-start(bf16[16,2048]{1,0:T(8,128)(2,1)} %get-tuple-element.22), channel_id=1, source_target_pairs={{0,4},{4,0},{8,12},{12,8},{16,20},{20,16},{24,28},{28,24},{1,5},{5... | collective-permute-start | bytes 196616 | tf_op jit(solution)/shard_map/ppermute | solution.py:504
  39.5 6.6 %collective-permute-start.5 = (bf16[16,2048]{1,0:T(8,128)(2,1)S(1)}, bf16[16,2048]{1,0:T(8,128)(2,1)S(1)}, u32[]{:S(2)}, u32[]{:S(2)}) collective-permute-start(bf16[16,2048]{1,0:T(8,128)(2,1)S(1)} %add_convert_fusion), channel_id=1, source_target_pairs={{0,24},{4,28},{8,16},{12,20},{16,8},{20,12},{24,0},{28,4},{1,25},{... | collective-permute-start | bytes 196616 | tf_op jit(solution)/shard_map/ppermute | solution.py:504
  43.6 6.1 %collective-permute-start.4 = (bf16[16,2048]{1,0:T(8,128)(2,1)S(1)}, bf16[16,2048]{1,0:T(8,128)(2,1)S(1)}, u32[]{:S(2)}, u32[]{:S(2)}) collective-permute-start(bf16[16,2048]{1,0:T(8,128)(2,1)S(1)} %add_convert_fusion), channel_id=1, source_target_pairs={{0,16},{4,20},{8,24},{12,28},{16,0},{20,4},{24,8},{28,12},{1,17},{... | collective-permute-start | bytes 196616 | tf_op jit(solution)/shard_map/ppermute | solution.py:504
  43.6 6.1 %collective-permute-start.3 = (bf16[16,2048]{1,0:T(8,128)(2,1)S(1)}, bf16[16,2048]{1,0:T(8,128)(2,1)S(1)}, u32[]{:S(2)}, u32[]{:S(2)}) collective-permute-start(bf16[16,2048]{1,0:T(8,128)(2,1)S(1)} %add_convert_fusion), channel_id=1, source_target_pairs={{0,8},{4,12},{8,0},{12,4},{16,24},{20,28},{24,16},{28,20},{1,9},{5... | collective-permute-start | bytes 196616 | tf_op jit(solution)/shard_map/ppermute | solution.py:504
  49.8 1.4 %copy-start = (f32[16,2048]{1,0:T(8,128)}, f32[16,2048]{1,0:T(8,128)S(1)}, u32[]{:S(2)}) copy-start(f32[16,2048]{1,0:T(8,128)S(1)} %add_add_fusion.own) | copy-start | bytes 393220
  49.8 1.4 %collective-permute-start.6 = (f32[16,2048]{1,0:T(8,128)S(1)}, f32[16,2048]{1,0:T(8,128)S(1)}, u32[]{:S(2)}, u32[]{:S(2)}) collective-permute-start(f32[16,2048]{1,0:T(8,128)S(1)} %add_add_fusion.own), channel_id=1, source_target_pairs={{0,4},{4,0},{8,12},{12,8},{16,20},{20,16},{24,28},{28,24},{1,5},{5... | collective-permute-start | bytes 393224 | tf_op jit(solution)/shard_map/ppermute | solution.py:504
  51.2 0.7 %copy-start.1 = (f32[16,2048]{1,0:T(8,128)}, f32[16,2048]{1,0:T(8,128)S(1)}, u32[]{:S(2)}) copy-start(f32[16,2048]{1,0:T(8,128)S(1)} %collective-permute-done.6.other) | copy-start | bytes 393220
  53.4 4.7 %collective-permute-start.9 = (f32[8,128]{1,0:T(8,128)}, f32[8,128]{1,0:T(8,128)S(1)}, u32[]{:S(2)}, u32[]{:S(2)}) collective-permute-start(f32[8,128]{1,0:T(8,128)} %squares.1.refs_0_), channel_id=1, source_target_pairs={{0,3},{1,2},{2,1},{3,0},{4,7},{5,6},{6,5},{7,4},{8,11},{9,10},{10,... | collective-permute-start | bytes 12296 | tf_op jit(solution)/shard_map/ppermute | solution.py:504
  55.9 3.8 %collective-permute-start.8 = (f32[8,128]{1,0:T(8,128)}, f32[8,128]{1,0:T(8,128)S(1)}, u32[]{:S(2)}, u32[]{:S(2)}) collective-permute-start(f32[8,128]{1,0:T(8,128)} %squares.1.refs_0_), channel_id=1, source_target_pairs={{0,2},{1,3},{2,0},{3,1},{4,6},{5,7},{6,4},{7,5},{8,10},{9,11},{10,... | collective-permute-start | bytes 12296 | tf_op jit(solution)/shard_map/ppermute | solution.py:504
  56.4 3.8 %collective-permute-start.7 = (f32[8,128]{1,0:T(8,128)}, f32[8,128]{1,0:T(8,128)S(1)}, u32[]{:S(2)}, u32[]{:S(2)}) collective-permute-start(f32[8,128]{1,0:T(8,128)} %squares.1.refs_0_), channel_id=1, source_target_pairs={{0,1},{1,0},{2,3},{3,2},{4,5},{5,4},{6,7},{7,6},{8,9},{9,8},{10,11... | collective-permute-start | bytes 12296 | tf_op jit(solution)/shard_map/ppermute | solution.py:504
  58.2 2.1 %copy-start.2 = (f32[8,128]{1,0:T(8,128)}, f32[8,128]{1,0:T(8,128)S(1)}, u32[]{:S(2)}) copy-start(f32[8,128]{1,0:T(8,128)S(1)} %collective-permute-done.9.refs_3_) | copy-start | bytes 12292
  59.7 0.6 copy-start.3
  60.3 0.6 copy-start.4

commit v4 on v3

--- a/solution.py
+++ b/solution.py
@@ -147,8 +147,8 @@
     return jnp.sum(part[:, :span], 0, keepdims=True)
 
 
-def woven(first, second):
-    live = [first, second]
+def woven(*jobs):
+    live = list(jobs)
     while live:
         for job in list(live):
             if next(job, True):
@@ -243,7 +243,7 @@
     def column(i):
         return pl.ds(i * LANES, LANES)
 
-    def first_stage(i, bufs):
+    def prepare(i, bufs, state):
         qx, kx, vx, zx, dyx, dqx, dkx, dvx, tst, ust, zm, pairs = bufs
         lanes = column(i)
         fq, fk, fv = (taps_of(filt, a, lanes) for a in range(3))
@@ -280,28 +280,37 @@
         zx[span + 2 * EDGE : span + rows, :] = z_in[2 * EDGE : rows, lanes]
         zx[span + rows : span + rows + 2 * EDGE, :] = halves(ks_next * vs_next, hole)
 
-        owner = owners(members, blocks)
-        one = owners(members, 1)
-        rows16 = 2 * EDGE
-
-        def windows(ref):
-            return jnp.concatenate([ref[b * span : (b + 2) * span, :] for b in range(blocks)], 1)
-
-        def chunk_of(stacked, at, who):
-            start = at * per
-            return pick(stacked[start : start + rows16 * per], rows16, who, per)
-
+        state[i] = (c_next, ks_first, vs_first, ks_next, vs_next)
+        yield False
         filters = lines[i * per : (i + 1) * per, :].astype(BF16)
         turned = dot(filters, reversing(span))
         filters = filters.astype(F32)
         for g in range(per):
             fill_band(ust, g, strip(filters, g, 0), span, per)
             yield False
+        for g in range(per):
+            fill_band(tst, g, strip(turned, g, 1), span, per)
+            yield False
+
+    def multiply(i, bufs, state):
+        qx, kx, vx, zx, dyx, dqx, dkx, dvx, tst, ust, zm, pairs = bufs
+        lanes = column(i)
+        c_next, ks_first, vs_first, ks_next, vs_next = state.pop(i)
+        owner = owners(members, blocks)
+        one = owners(members, 1)
+        rows16 = 2 * EDGE
+
+        def windows(ref):
+            return jnp.concatenate([ref[b * span : (b + 2) * span, :] for b in range(blocks)], 1)
+
+        def chunk_of(stacked, at, who):
+            start = at * per
+            return pick(stacked[start : start + rows16 * per], rows16, who, per)
+
         dz = dot(ust[...], windows(dyx))
         dz_next = chunk_of(dot(ust[0 : rows16 * per, :], dyx[rows : rows + 2 * span, :]), 0, one)
         dkx[rows:wide, :] = dz_next[:EDGE] * vs_next
         dvx[rows:wide, :] = dz_next[:EDGE] * ks_next
-        left = list(range(per))
         for at in range(0, span, rows16):
             piece = chunk_of(dz, at, owner)
             for b in range(blocks):
@@ -313,12 +322,7 @@
                     ks = jnp.concatenate([ks_first, ks[EDGE:]], 0)
                 dkx[t : t + rows16, :] = part * vs
                 dvx[t : t + rows16, :] = part * ks
-            if left:
-                g = left.pop(0)
-                fill_band(tst, g, strip(turned, g, 1), span, per)
             yield False
-        for g in left:
-            fill_band(tst, g, strip(turned, g, 1), span, per)
         y = dot(tst[...], windows(zx))
         y_next = chunk_of(dot(tst[0 : rows16 * per, :], zx[rows : rows + 2 * span, :]), 0, one)
         dqx[rows:wide, :] = c_next * y_next[:EDGE]
@@ -376,11 +380,16 @@
             diagonal(g)
 
     tiles = width // LANES
-    woven(first_stage(0, sets[0]), iter(()))
-
-    for i in range(tiles):
-        after = first_stage(i + 1, sets[(i + 1) % 2]) if i + 1 < tiles else iter(())
-        woven(after, second_stage(i, sets[i % 2]))
+    state = {}
+    for i in range(-2, tiles):
+        jobs = []
+        if i + 2 < tiles:
+            jobs.append(prepare(i + 2, sets[i % 2], state))
+        if 0 <= i + 1 < tiles:
+            jobs.append(multiply(i + 1, sets[(i + 1) % 2], state))
+        if i >= 0:
+            jobs.append(second_stage(i, sets[i % 2]))
+        woven(*jobs)
     keep[...] = sums[odd].astype(BF16)
     send[...] = sums[1 - odd].astype(BF16)
 
@@ -464,24 +473,9 @@
             jax.ShapeDtypeStruct((3, taps, width), F32),
             jax.ShapeDtypeStruct((groups, span), F32),
         ],
+        compiler_params=pltpu.CompilerParams(vmem_limit_bytes=67043328),
         name="finish",
     )(own, other, *squares)
-
-
-def square_kernel(own, other, out):
-    total = None
-    for x in (own, other):
-        for at in range(0, x.shape[1], LANES):
-            piece = x[:, at : at + LANES]
-            square = jnp.sum((piece * piece).reshape(-1, EDGE, LANES), 0)
-            total = square if total is None else total + square
-    out[...] = total
-
-
-def squares_of(own, other):
-    return pl.pallas_call(
-        square_kernel, out_shape=jax.ShapeDtypeStruct((EDGE, LANES), F32), name="squares"
-    )(own, other)
 
 
 def factors_of(size):
@@ -544,7 +538,7 @@
     own = total_over(own, "ctx", 2, size // 2, BF16)
     other = swap(own, "ctx", 1, 2, 1)
     *early, late = factors_of(lax.axis_size("ch"))
-    squares = squares_of(own, other)
+    squares = jnp.sum(own * own + other * other, 0, keepdims=True)
     stride = 1
     for factor in early:
         squares = total_over(squares, "ch", stride, factor, F32)

time: 63 us -> 60.1 us (0.954)
  Pallas kernels: 33.7 us -> 31.6 us
    pallas_call x1 -> x0, Pallas kernels: 1.59 us -> none  [squares_of(): pl.pallas_call(square_kernel, out_shape=jax.ShapeDtypeStruct((EDGE, LANES...]
    ppermute x8, waiting for transfers between devices: 11.2 us -> 10.6 us  [swap(): return lax.ppermute(value, axis, route)]
  transfers between devices with their start and end apart: 10 -> 10, of which waited for: 7 -> 6; matrix products, arithmetic and copies ran while one was open for 0% -> 0% of each run, Pallas kernels for 11% -> 12%
where the time goes in v4:
time: 60.1 us; the launch traced here: 59.8 us
  Pallas kernels  31.6 us (53%)
  starting transfers between devices  14.8 us (25%)
  waiting for transfers between devices  10.6 us (18%)
  local copies, waits for them, and re-layouts  1.2 us (2%)
  other arithmetic  0.94 us (2%)
  between operations  0.68 us (1%)
    pallas_call x1, Pallas kernels, join(): pl.pallas_call(functools.partial(join_kernel, span, members), grid=(width...  17.9 us
    ppermute x8, starting transfers between devices, swap(): return lax.ppermute(value, axis, route)  12.7 us
    ppermute x8, waiting for transfers between devices, swap(): return lax.ppermute(value, axis, route)  10.6 us
    pallas_call x1, Pallas kernels, own_part(): pl.pallas_call(functools.partial(own_kernel, span), grid=(width // step,)...  7.17 us
    pallas_call x1, Pallas kernels, edges(): pl.pallas_call(functools.partial(edge_kernel, span), grid=(width // step,...  4.75 us
    pallas_call x1, Pallas kernels, finish(): pl.pallas_call(functools.partial(finish_kernel, count), out_shape=[jax.Sh...  1.81 us
    ppermute x1, starting transfers between devices, on_device(): lax.ppermute(far, 'ctx', [(i, (i + 1 ^ 1) - 1) for i in range(1, size - 1)])  1.55 us
  transfers between devices with their start and end apart: 10, of which 6 were waited for; matrix products, arithmetic and copies ran while one was open for 0% of the time, Pallas kernels for 12%

profile of v4, /device:TPU:0, one launch (start us, length us, event | category | flops | bytes accessed | tf_op | source)
XLA Modules:
  0.0 59.8 jit_solution(8070487855125369693)
XLA Ops:
  0.6 4.7 %edges.1 = (bf16[160,2048]{1,0:T(8,128)(2,1)}, bf16[160,2048]{1,0:T(8,128)(2,1)}) custom-call(bf16[3,256,2048]{2,1,0:T(8,128)(2,1)} %feat.5, bf16[256,2048]{1,0:T(8,128)(2,1)} %cot.5, f32[3,7,2048]{2,1,0:T(8,128)} %filt.5), custom_call_target="tpu_custom_call" | custom-call | tf_op jit(solution)/shard_map/edges/pallas_call | solution.py:87
  5.4 0.5 collective-permute-start
  5.9 1.6 %collective-permute-start.1 = (bf16[160,2048]{1,0:T(8,128)(2,1)}, bf16[160,2048]{1,0:T(8,128)(2,1)}, u32[]{:S(2)}, u32[]{:S(2)}) collective-permute-start(bf16[160,2048]{1,0:T(8,128)(2,1)} %get-tuple-element.15), channel_id=1, source_target_pairs={{4,8},{8,4},{12,16},{16,12},{20,24},{24,20},{5,9},{9,5},{13,17},{1... | collective-permute-start | bytes 1966088 | tf_op jit(solution)/shard_map/ppermute | solution.py:531
  7.4 7.2 %own.1 = (f32[256,2048]{1,0:T(8,128)}, f32[256,2048]{1,0:T(8,128)}, bf16[256,2048]{1,0:T(8,128)(2,1)}, bf16[256,2048]{1,0:T(8,128)(2,1)}) custom-call(bf16[3,256,2048]{2,1,0:T(8,128)(2,1)} %feat.5, bf16[256,2048]{1,0:T(8,128)(2,1)} %cot.5, f32[3,7,2048]{2,1,0:T(8,128)} %filt.5), custom_call_target="tpu_custom_call" | custom-call | flops 20971520 | bytes 10485760 | tf_op jit(solution)/shard_map/own/pallas_call | solution.py:202
  14.6 0.0 collective-permute-done.near
  14.6 0.0 collective-permute-done.1.far
  14.6 17.9 %join.1 = (bf16[3,256,2048]{2,1,0:T(8,128)(2,1)}, bf16[16,2048]{1,0:T(8,128)(2,1)}, bf16[16,2048]{1,0:T(8,128)(2,1)}) custom-call(bf16[3,256,2048]{2,1,0:T(8,128)(2,1)} %feat.5, bf16[256,2048]{1,0:T(8,128)(2,1)} %cot.5, bf16[160,2048]{1,0:T(8,128)(2,1)} %collective-permute-done.near, bf16[160,2048]{1,0:T(8,128)(2,1)} %collective-permute-done.1.far, ...), custom_call_target="tpu_custom_call" | custom-call | tf_op jit(solution)/shard_map/join/pallas_call | solution.py:414
  32.5 4.5 %collective-permute-start.2 = (bf16[16,2048]{1,0:T(8,128)(2,1)}, bf16[16,2048]{1,0:T(8,128)(2,1)S(1)}, u32[]{:S(2)}, u32[]{:S(2)}) collective-permute-start(bf16[16,2048]{1,0:T(8,128)(2,1)} %get-tuple-element.22), channel_id=1, source_target_pairs={{0,4},{4,0},{8,12},{12,8},{16,20},{20,16},{24,28},{28,24},{1,5},{5... | collective-permute-start | bytes 196616 | tf_op jit(solution)/shard_map/ppermute | solution.py:498
  37.0 1.1 %collective-permute-done.2 = bf16[16,2048]{1,0:T(8,128)(2,1)S(1)} collective-permute-done((bf16[16,2048]{1,0:T(8,128)(2,1)}, bf16[16,2048]{1,0:T(8,128)(2,1)S(1)}, u32[]{:S(2)}, u32[]{:S(2)}) %collective-permute-start.2) | collective-permute-done | bytes 65568 | tf_op jit(solution)/shard_map/ppermute | solution.py:498
  38.1 0.9 %add_convert_fusion = bf16[16,2048]{1,0:T(8,128)(2,1)S(1)} fusion(bf16[16,2048]{1,0:T(8,128)(2,1)S(1)} %collective-permute-done.2, bf16[16,2048]{1,0:T(8,128)(2,1)} %get-tuple-element.21), kind=kLoop, calls=%fused_computation.2 | loop fusion | flops 131072 | bytes 196608 | tf_op jit(solution)/shard_map/convert_element_type | solution.py:504
  39.0 4.1 %collective-permute-start.5 = (bf16[16,2048]{1,0:T(8,128)(2,1)S(1)}, bf16[16,2048]{1,0:T(8,128)(2,1)S(1)}, u32[]{:S(2)}, u32[]{:S(2)}) collective-permute-start(bf16[16,2048]{1,0:T(8,128)(2,1)S(1)} %add_convert_fusion), channel_id=1, source_target_pairs={{0,24},{4,28},{8,16},{12,20},{16,8},{20,12},{24,0},{28,4},{1,25},{... | collective-permute-start | bytes 196616 | tf_op jit(solution)/shard_map/ppermute | solution.py:498
  43.0 0.0 collective-permute-start.4
  43.0 0.6 %collective-permute-start.3 = (bf16[16,2048]{1,0:T(8,128)(2,1)S(1)}, bf16[16,2048]{1,0:T(8,128)(2,1)S(1)}, u32[]{:S(2)}, u32[]{:S(2)}) collective-permute-start(bf16[16,2048]{1,0:T(8,128)(2,1)S(1)} %add_convert_fusion), channel_id=1, source_target_pairs={{0,8},{4,12},{8,0},{12,4},{16,24},{20,28},{24,16},{28,20},{1,9},{5... | collective-permute-start | bytes 196616 | tf_op jit(solution)/shard_map/ppermute | solution.py:498
  43.7 1.9 %collective-permute-done.5 = bf16[16,2048]{1,0:T(8,128)(2,1)S(1)} collective-permute-done((bf16[16,2048]{1,0:T(8,128)(2,1)S(1)}, bf16[16,2048]{1,0:T(8,128)(2,1)S(1)}, u32[]{:S(2)}, u32[]{:S(2)}) %collective-permute-start.5) | collective-permute-done | bytes 65568 | tf_op jit(solution)/shard_map/ppermute | solution.py:498
  45.5 3.6 %collective-permute-done.4 = bf16[16,2048]{1,0:T(8,128)(2,1)S(1)} collective-permute-done((bf16[16,2048]{1,0:T(8,128)(2,1)S(1)}, bf16[16,2048]{1,0:T(8,128)(2,1)S(1)}, u32[]{:S(2)}, u32[]{:S(2)}) %collective-permute-start.4) | collective-permute-done | bytes 65568 | tf_op jit(solution)/shard_map/ppermute | solution.py:498
  49.1 0.0 collective-permute-done.3
  49.2 0.0 copy-start
  49.2 0.1 collective-permute-start.6
  49.3 1.3 %collective-permute-done.6.other = f32[16,2048]{1,0:T(8,128)S(1)} collective-permute-done((f32[16,2048]{1,0:T(8,128)S(1)}, f32[16,2048]{1,0:T(8,128)S(1)}, u32[]{:S(2)}, u32[]{:S(2)}) %collective-permute-start.6) | collective-permute-done | bytes 131104 | tf_op jit(solution)/shard_map/ppermute | solution.py:498
  50.6 0.0 copy-done
  50.6 0.0 copy-start.1
  50.7 0.6 copy-done.1
  51.3 0.0 copy-start.2
  51.3 2.4 %collective-permute-start.9 = (f32[1,2048]{1,0:T(1,128)S(1)}, f32[1,2048]{1,0:T(1,128)S(1)}, u32[]{:S(2)}, u32[]{:S(2)}) collective-permute-start(f32[1,2048]{1,0:T(1,128)S(1)} %bitcast.1), channel_id=1, source_target_pairs={{0,3},{1,2},{2,1},{3,0},{4,7},{5,6},{6,5},{7,4},{8,11},{9,10},{10,... | collective-permute-start | bytes 24584 | tf_op jit(solution)/shard_map/ppermute | solution.py:498
  53.7 0.5 collective-permute-start.8
  54.2 0.0 copy-done.2
  54.2 0.5 collective-permute-start.7
  54.7 1.1 %collective-permute-done.9.refs_3_ = f32[1,2048]{1,0:T(1,128)S(1)} collective-permute-done((f32[1,2048]{1,0:T(1,128)S(1)}, f32[1,2048]{1,0:T(1,128)S(1)}, u32[]{:S(2)}, u32[]{:S(2)}) %collective-permute-start.9) | collective-permute-done | bytes 8224 | tf_op jit(solution)/shard_map/ppermute | solution.py:498
  55.8 0.0 copy-start.3
  55.8 1.5 %collective-permute-done.8.refs_2_ = f32[1,2048]{1,0:T(1,128)S(1)} collective-permute-done((f32[1,2048]{1,0:T(1,128)S(1)}, f32[1,2048]{1,0:T(1,128)S(1)}, u32[]{:S(2)}, u32[]{:S(2)}) %collective-permute-start.8) | collective-permute-done | bytes 8224 | tf_op jit(solution)/shard_map/ppermute | solution.py:498
  57.4 0.0 copy-done.3
  57.4 0.0 copy-start.4
  57.4 0.6 copy-done.4
  58.0 0.0 collective-permute-done.7.refs_1_
  58.0 1.8 %finish.1 = (f32[3,7,2048]{2,1,0:T(8,128)}, f32[128,128]{1,0:T(8,128)}) custom-call(f32[16,2048]{1,0:T(8,128)} %copy-done, f32[16,2048]{1,0:T(8,128)} %copy-done.1, f32[1,2048]{1,0:T(1,128)} %bitcast.4, f32[1,2048]{1,0:T(1,128)} %collective-permute-done.7.refs_1_, f32[1,2048]{1,0:T(1,128)} %copy-done.4, f32[1,2048]{1,0:T(1,128)} %copy-done.3), custom_call_target="tpu_custom_call" | custom-call | tf_op jit(solution)/shard_map/finish/pallas_call | solution.py:470
  (2 shorter events, 0.1 us)
Async XLA Ops:
  5.4 9.2 %collective-permute-start = (bf16[160,2048]{1,0:T(8,128)(2,1)}, bf16[160,2048]{1,0:T(8,128)(2,1)}, u32[]{:S(2)}, u32[]{:S(2)}) collective-permute-start(bf16[160,2048]{1,0:T(8,128)(2,1)} %get-tuple-element.14), channel_id=1, source_target_pairs={{0,4},{4,0},{8,12},{12,8},{16,20},{20,16},{24,28},{28,24},{1,5},{5... | collective-permute-start | bytes 1966088 | tf_op jit(solution)/shard_map/ppermute | solution.py:530
  5.9 8.7 %collective-permute-start.1 = (bf16[160,2048]{1,0:T(8,128)(2,1)}, bf16[160,2048]{1,0:T(8,128)(2,1)}, u32[]{:S(2)}, u32[]{:S(2)}) collective-permute-start(bf16[160,2048]{1,0:T(8,128)(2,1)} %get-tuple-element.15), channel_id=1, source_target_pairs={{4,8},{8,4},{12,16},{16,12},{20,24},{24,20},{5,9},{9,5},{13,17},{1... | collective-permute-start | bytes 1966088 | tf_op jit(solution)/shard_map/ppermute | solution.py:531
  32.5 5.6 %collective-permute-start.2 = (bf16[16,2048]{1,0:T(8,128)(2,1)}, bf16[16,2048]{1,0:T(8,128)(2,1)S(1)}, u32[]{:S(2)}, u32[]{:S(2)}) collective-permute-start(bf16[16,2048]{1,0:T(8,128)(2,1)} %get-tuple-element.22), channel_id=1, source_target_pairs={{0,4},{4,0},{8,12},{12,8},{16,20},{20,16},{24,28},{28,24},{1,5},{5... | collective-permute-start | bytes 196616 | tf_op jit(solution)/shard_map/ppermute | solution.py:498
  39.0 6.6 %collective-permute-start.5 = (bf16[16,2048]{1,0:T(8,128)(2,1)S(1)}, bf16[16,2048]{1,0:T(8,128)(2,1)S(1)}, u32[]{:S(2)}, u32[]{:S(2)}) collective-permute-start(bf16[16,2048]{1,0:T(8,128)(2,1)S(1)} %add_convert_fusion), channel_id=1, source_target_pairs={{0,24},{4,28},{8,16},{12,20},{16,8},{20,12},{24,0},{28,4},{1,25},{... | collective-permute-start | bytes 196616 | tf_op jit(solution)/shard_map/ppermute | solution.py:498
  43.0 6.1 %collective-permute-start.4 = (bf16[16,2048]{1,0:T(8,128)(2,1)S(1)}, bf16[16,2048]{1,0:T(8,128)(2,1)S(1)}, u32[]{:S(2)}, u32[]{:S(2)}) collective-permute-start(bf16[16,2048]{1,0:T(8,128)(2,1)S(1)} %add_convert_fusion), channel_id=1, source_target_pairs={{0,16},{4,20},{8,24},{12,28},{16,0},{20,4},{24,8},{28,12},{1,17},{... | collective-permute-start | bytes 196616 | tf_op jit(solution)/shard_map/ppermute | solution.py:498
  43.0 6.1 %collective-permute-start.3 = (bf16[16,2048]{1,0:T(8,128)(2,1)S(1)}, bf16[16,2048]{1,0:T(8,128)(2,1)S(1)}, u32[]{:S(2)}, u32[]{:S(2)}) collective-permute-start(bf16[16,2048]{1,0:T(8,128)(2,1)S(1)} %add_convert_fusion), channel_id=1, source_target_pairs={{0,8},{4,12},{8,0},{12,4},{16,24},{20,28},{24,16},{28,20},{1,9},{5... | collective-permute-start | bytes 196616 | tf_op jit(solution)/shard_map/ppermute | solution.py:498
  49.2 1.4 %copy-start = (f32[16,2048]{1,0:T(8,128)}, f32[16,2048]{1,0:T(8,128)S(1)}, u32[]{:S(2)}) copy-start(f32[16,2048]{1,0:T(8,128)S(1)} %add_add_fusion.own) | copy-start | bytes 393220
  49.2 1.4 %collective-permute-start.6 = (f32[16,2048]{1,0:T(8,128)S(1)}, f32[16,2048]{1,0:T(8,128)S(1)}, u32[]{:S(2)}, u32[]{:S(2)}) collective-permute-start(f32[16,2048]{1,0:T(8,128)S(1)} %add_add_fusion.own), channel_id=1, source_target_pairs={{0,4},{4,0},{8,12},{12,8},{16,20},{20,16},{24,28},{28,24},{1,5},{5... | collective-permute-start | bytes 393224 | tf_op jit(solution)/shard_map/ppermute | solution.py:498
  50.6 0.6 %copy-start.1 = (f32[16,2048]{1,0:T(8,128)}, f32[16,2048]{1,0:T(8,128)S(1)}, u32[]{:S(2)}) copy-start(f32[16,2048]{1,0:T(8,128)S(1)} %collective-permute-done.6.other) | copy-start | bytes 393220
  51.3 3.0 %copy-start.2 = (f32[2048]{0:T(1024)}, f32[2048]{0:T(1024)S(1)}, u32[]{:S(2)}) copy-start(f32[2048]{0:T(1024)S(1)} %add_reduce_fusion) | copy-start | bytes 24580
  51.3 4.5 %collective-permute-start.9 = (f32[1,2048]{1,0:T(1,128)S(1)}, f32[1,2048]{1,0:T(1,128)S(1)}, u32[]{:S(2)}, u32[]{:S(2)}) collective-permute-start(f32[1,2048]{1,0:T(1,128)S(1)} %bitcast.1), channel_id=1, source_target_pairs={{0,3},{1,2},{2,1},{3,0},{4,7},{5,6},{6,5},{7,4},{8,11},{9,10},{10,... | collective-permute-start | bytes 24584 | tf_op jit(solution)/shard_map/ppermute | solution.py:498
  53.7 3.7 %collective-permute-start.8 = (f32[1,2048]{1,0:T(1,128)S(1)}, f32[1,2048]{1,0:T(1,128)S(1)}, u32[]{:S(2)}, u32[]{:S(2)}) collective-permute-start(f32[1,2048]{1,0:T(1,128)S(1)} %bitcast.2), channel_id=1, source_target_pairs={{0,2},{1,3},{2,0},{3,1},{4,6},{5,7},{6,4},{7,5},{8,10},{9,11},{10,... | collective-permute-start | bytes 24584 | tf_op jit(solution)/shard_map/ppermute | solution.py:498
  54.2 3.8 %collective-permute-start.7 = (f32[1,2048]{1,0:T(1,128)S(1)}, f32[1,2048]{1,0:T(1,128)}, u32[]{:S(2)}, u32[]{:S(2)}) collective-permute-start(f32[1,2048]{1,0:T(1,128)S(1)} %bitcast.3), channel_id=1, source_target_pairs={{0,1},{1,0},{2,3},{3,2},{4,5},{5,4},{6,7},{7,6},{8,9},{9,8},{10,11... | collective-permute-start | bytes 24584 | tf_op jit(solution)/shard_map/ppermute | solution.py:498
  55.8 1.6 %copy-start.3 = (f32[1,2048]{1,0:T(1,128)}, f32[1,2048]{1,0:T(1,128)S(1)}, u32[]{:S(2)}) copy-start(f32[1,2048]{1,0:T(1,128)S(1)} %collective-permute-done.9.refs_3_) | copy-start | bytes 24580
  57.4 0.6 copy-start.4

commit v5 on v4

--- a/solution.py
+++ b/solution.py
@@ -206,12 +206,12 @@
         out_specs=[column(rows)] * 4,
         out_shape=[jax.ShapeDtypeStruct((rows, width), kind) for kind in kinds],
         scratch_shapes=[pltpu.VMEM((rows, LANES), F32)] * 3,
-        compiler_params=pltpu.CompilerParams(vmem_limit_bytes=67043328),
+        compiler_params=pltpu.CompilerParams(vmem_limit_bytes=30 * 2**20),
         cost_estimate=pl.CostEstimate(
             flops=40 * rows * width, bytes_accessed=20 * rows * width, transcendentals=0
         ),
         name="own",
-    )(features, cotangent, short_filter)
+    )(*[pltpu.with_memory_space_constraint(x, pltpu.HBM) for x in (features, cotangent, short_filter)])
 
 
 def join_kernel(
@@ -430,9 +430,9 @@
             jax.ShapeDtypeStruct((half, width), BF16),
         ],
         scratch_shapes=[pltpu.VMEM((2, half, step), F32)] + buffers * 2,
-        compiler_params=pltpu.CompilerParams(vmem_limit_bytes=67043328),
+        compiler_params=pltpu.CompilerParams(vmem_limit_bytes=44 * 2**20),
         name="join",
-    )(features, cotangent, *got, short_filter, long_filter, *parts)
+    )(*[pltpu.with_memory_space_constraint(x, pltpu.HBM) for x in (features, cotangent, *got, short_filter, long_filter)], *parts)
 
 
 def finish_kernel(count, own, other, *refs):
@@ -475,7 +475,7 @@
         ],
         compiler_params=pltpu.CompilerParams(vmem_limit_bytes=67043328),
         name="finish",
-    )(own, other, *squares)
+    )(*[pltpu.with_memory_space_constraint(x, pltpu.HBM) for x in (own, other, *squares)])
 
 
 def factors_of(size):

time: 60.1 us -> 59 us (0.982)
  Pallas kernels: 31.6 us -> 29.5 us
  local copies, waits for them, and re-layouts: 1.2 us -> 2.29 us
  starting transfers between devices: 14.8 us -> 15.8 us
  other arithmetic: 0.94 us -> 0.09 us
    ppermute x8, starting transfers between devices: 12.7 us -> 14.7 us  [swap(): return lax.ppermute(value, axis, route)]
    pallas_call x1, Pallas kernels: 7.17 us -> 5.69 us  [own_part(): pl.pallas_call(functools.partial(own_kernel, span), grid=(width // step,)...]
    unnamed x10 -> x14, local copies, waits for them, and re-layouts: 1.2 us -> 2.29 us
    ppermute x1, starting transfers between devices: 1.55 us -> 0.69 us  [on_device(): lax.ppermute(far, 'ctx', [(i, (i + 1 ^ 1) - 1) for i in range(1, size - 1)])]
    convert_element_type x1, other arithmetic: 0.86 us -> 0.02 us  [total_over(): sent = value.astype(kind)]
    pallas_call x1, Pallas kernels: 17.9 us -> 17.2 us  [join(): pl.pallas_call(functools.partial(join_kernel, span, members), grid=(width...]
  transfers between devices with their start and end apart: 10 -> 10, of which waited for: 6 -> 6; matrix products, arithmetic and copies ran while one was open for 0% -> 0% of each run, Pallas kernels for 12% -> 10%
where the time goes in v5:
time: 59 us; the launch traced here: 58.8 us
  Pallas kernels  29.5 us (50%)
  starting transfers between devices  15.8 us (27%)
  waiting for transfers between devices  10.4 us (18%)
  local copies, waits for them, and re-layouts  2.29 us (4%)
  between operations  0.72 us (1%)
    pallas_call x1, Pallas kernels, join(): pl.pallas_call(functools.partial(join_kernel, span, members), grid=(width...  17.2 us
    ppermute x8, starting transfers between devices, swap(): return lax.ppermute(value, axis, route)  14.7 us
    ppermute x8, waiting for transfers between devices, swap(): return lax.ppermute(value, axis, route)  10.3 us
    pallas_call x1, Pallas kernels, own_part(): pl.pallas_call(functools.partial(own_kernel, span), grid=(width // step,)...  5.69 us
    pallas_call x1, Pallas kernels, edges(): pl.pallas_call(functools.partial(edge_kernel, span), grid=(width // step,...  4.74 us
    unnamed x14, local copies, waits for them, and re-layouts  2.29 us
    pallas_call x1, Pallas kernels, finish(): pl.pallas_call(functools.partial(finish_kernel, count), out_shape=[jax.Sh...  1.81 us
  transfers between devices with their start and end apart: 10, of which 6 were waited for; matrix products, arithmetic and copies ran while one was open for 0% of the time, Pallas kernels for 10%

profile of v5, /device:TPU:0, one launch (start us, length us, event | category | flops | bytes accessed | tf_op | source)
XLA Modules:
  0.0 58.8 jit_solution(5618438075875502118)
XLA Ops:
  0.6 4.7 %edges.1 = (bf16[160,2048]{1,0:T(8,128)(2,1)}, bf16[160,2048]{1,0:T(8,128)(2,1)}) custom-call(bf16[3,256,2048]{2,1,0:T(8,128)(2,1)} %feat.5, bf16[256,2048]{1,0:T(8,128)(2,1)} %cot.5, f32[3,7,2048]{2,1,0:T(8,128)} %filt.5), custom_call_target="tpu_custom_call" | custom-call | tf_op jit(solution)/shard_map/edges/pallas_call | solution.py:87
  5.4 0.5 collective-permute-start
  5.9 0.7 %collective-permute-start.1 = (bf16[160,2048]{1,0:T(8,128)(2,1)}, bf16[160,2048]{1,0:T(8,128)(2,1)S(1)}, u32[]{:S(2)}, u32[]{:S(2)}) collective-permute-start(bf16[160,2048]{1,0:T(8,128)(2,1)} %get-tuple-element.15), channel_id=1, source_target_pairs={{4,8},{8,4},{12,16},{16,12},{20,24},{24,20},{5,9},{9,5},{13,17},{1... | collective-permute-start | bytes 1966088 | tf_op jit(solution)/shard_map/ppermute | solution.py:531
  6.6 5.7 %own.1 = (f32[256,2048]{1,0:T(8,128)S(1)}, f32[256,2048]{1,0:T(8,128)S(1)}, bf16[256,2048]{1,0:T(8,128)(2,1)S(1)}, bf16[256,2048]{1,0:T(8,128)(2,1)S(1)}) custom-call(bf16[3,256,2048]{2,1,0:T(8,128)(2,1)} %feat.5, bf16[256,2048]{1,0:T(8,128)(2,1)} %cot.5, f32[3,7,2048]{2,1,0:T(8,128)} %filt.5), custom_call_target="tpu_custom_call" | custom-call | flops 20971520 | bytes 10485760 | tf_op jit(solution)/shard_map/own/pallas_call | solution.py:202
  12.3 0.0 collective-permute-done.near
  12.3 0.0 copy-start.1
  12.3 0.0 collective-permute-done.1.far
  12.3 0.0 copy-start.2
  12.3 0.8 %copy-done.1 = bf16[160,2048]{1,0:T(8,128)(2,1)} copy-done((bf16[160,2048]{1,0:T(8,128)(2,1)}, bf16[160,2048]{1,0:T(8,128)(2,1)S(1)}, u32[]{:S(2)}) %copy-start.1) | copy-done | bytes 655384
  13.1 0.3 copy-done.2
  13.4 17.2 %join.1 = (bf16[3,256,2048]{2,1,0:T(8,128)(2,1)}, bf16[16,2048]{1,0:T(8,128)(2,1)S(1)}, bf16[16,2048]{1,0:T(8,128)(2,1)S(1)}) custom-call(bf16[3,256,2048]{2,1,0:T(8,128)(2,1)} %feat.5, bf16[256,2048]{1,0:T(8,128)(2,1)} %cot.5, bf16[160,2048]{1,0:T(8,128)(2,1)} %copy-done.1, bf16[160,2048]{1,0:T(8,128)(2,1)} %copy-done.2, f32[3,7,2048]{2,1,0:T(8,128)} %filt.5, ...), custom_call_target="tpu_custom_call" | custom-call | tf_op jit(solution)/shard_map/join/pallas_call | solution.py:414
  30.6 6.4 %collective-permute-start.2 = (bf16[16,2048]{1,0:T(8,128)(2,1)S(1)}, bf16[16,2048]{1,0:T(8,128)(2,1)S(1)}, u32[]{:S(2)}, u32[]{:S(2)}) collective-permute-start(bf16[16,2048]{1,0:T(8,128)(2,1)S(1)} %get-tuple-element.22), channel_id=1, source_target_pairs={{0,4},{4,0},{8,12},{12,8},{16,20},{20,16},{24,28},{28,24},{1,5},{5... | collective-permute-start | bytes 196616 | tf_op jit(solution)/shard_map/ppermute | solution.py:498
  37.0 0.9 %collective-permute-done.2 = bf16[16,2048]{1,0:T(8,128)(2,1)S(1)} collective-permute-done((bf16[16,2048]{1,0:T(8,128)(2,1)S(1)}, bf16[16,2048]{1,0:T(8,128)(2,1)S(1)}, u32[]{:S(2)}, u32[]{:S(2)}) %collective-permute-start.2) | collective-permute-done | bytes 65568 | tf_op jit(solution)/shard_map/ppermute | solution.py:498
  37.9 4.1 %collective-permute-start.5 = (bf16[16,2048]{1,0:T(8,128)(2,1)S(1)}, bf16[16,2048]{1,0:T(8,128)(2,1)S(1)}, u32[]{:S(2)}, u32[]{:S(2)}) collective-permute-start(bf16[16,2048]{1,0:T(8,128)(2,1)S(1)} %add_convert_fusion), channel_id=1, source_target_pairs={{0,24},{4,28},{8,16},{12,20},{16,8},{20,12},{24,0},{28,4},{1,25},{... | collective-permute-start | bytes 196616 | tf_op jit(solution)/shard_map/ppermute | solution.py:498
  42.0 0.0 collective-permute-start.4
  42.0 0.6 %collective-permute-start.3 = (bf16[16,2048]{1,0:T(8,128)(2,1)S(1)}, bf16[16,2048]{1,0:T(8,128)(2,1)S(1)}, u32[]{:S(2)}, u32[]{:S(2)}) collective-permute-start(bf16[16,2048]{1,0:T(8,128)(2,1)S(1)} %add_convert_fusion), channel_id=1, source_target_pairs={{0,8},{4,12},{8,0},{12,4},{16,24},{20,28},{24,16},{28,20},{1,9},{5... | collective-permute-start | bytes 196616 | tf_op jit(solution)/shard_map/ppermute | solution.py:498
  42.6 1.9 %collective-permute-done.5 = bf16[16,2048]{1,0:T(8,128)(2,1)S(1)} collective-permute-done((bf16[16,2048]{1,0:T(8,128)(2,1)S(1)}, bf16[16,2048]{1,0:T(8,128)(2,1)S(1)}, u32[]{:S(2)}, u32[]{:S(2)}) %collective-permute-start.5) | collective-permute-done | bytes 65568 | tf_op jit(solution)/shard_map/ppermute | solution.py:498
  44.5 3.6 %collective-permute-done.4 = bf16[16,2048]{1,0:T(8,128)(2,1)S(1)} collective-permute-done((bf16[16,2048]{1,0:T(8,128)(2,1)S(1)}, bf16[16,2048]{1,0:T(8,128)(2,1)S(1)}, u32[]{:S(2)}, u32[]{:S(2)}) %collective-permute-start.4) | collective-permute-done | bytes 65568 | tf_op jit(solution)/shard_map/ppermute | solution.py:498
  48.1 0.0 collective-permute-done.3
  48.1 0.0 copy-start
  48.2 0.1 collective-permute-start.6
  48.2 1.3 %collective-permute-done.6.other = f32[16,2048]{1,0:T(8,128)S(1)} collective-permute-done((f32[16,2048]{1,0:T(8,128)S(1)}, f32[16,2048]{1,0:T(8,128)S(1)}, u32[]{:S(2)}, u32[]{:S(2)}) %collective-permute-start.6) | collective-permute-done | bytes 131104 | tf_op jit(solution)/shard_map/ppermute | solution.py:498
  49.6 0.0 copy-done
  49.6 0.0 copy-start.3
  49.6 0.6 %copy-done.3 = f32[16,2048]{1,0:T(8,128)} copy-done((f32[16,2048]{1,0:T(8,128)}, f32[16,2048]{1,0:T(8,128)S(1)}, u32[]{:S(2)}) %copy-start.3) | copy-done | bytes 131096
  50.2 0.0 copy-start.4
  50.2 2.4 %collective-permute-start.9 = (f32[1,2048]{1,0:T(1,128)S(1)}, f32[1,2048]{1,0:T(1,128)S(1)}, u32[]{:S(2)}, u32[]{:S(2)}) collective-permute-start(f32[1,2048]{1,0:T(1,128)S(1)} %bitcast.1), channel_id=1, source_target_pairs={{0,3},{1,2},{2,1},{3,0},{4,7},{5,6},{6,5},{7,4},{8,11},{9,10},{10,... | collective-permute-start | bytes 24584 | tf_op jit(solution)/shard_map/ppermute | solution.py:498
  52.7 0.5 collective-permute-start.8
  53.2 0.0 copy-done.4
  53.2 0.5 collective-permute-start.7
  53.7 1.1 %collective-permute-done.9.refs_3_ = f32[1,2048]{1,0:T(1,128)S(1)} collective-permute-done((f32[1,2048]{1,0:T(1,128)S(1)}, f32[1,2048]{1,0:T(1,128)S(1)}, u32[]{:S(2)}, u32[]{:S(2)}) %collective-permute-start.9) | collective-permute-done | bytes 8224 | tf_op jit(solution)/shard_map/ppermute | solution.py:498
  54.8 0.0 copy-start.5
  54.8 1.5 %collective-permute-done.8.refs_2_ = f32[1,2048]{1,0:T(1,128)S(1)} collective-permute-done((f32[1,2048]{1,0:T(1,128)S(1)}, f32[1,2048]{1,0:T(1,128)S(1)}, u32[]{:S(2)}, u32[]{:S(2)}) %collective-permute-start.8) | collective-permute-done | bytes 8224 | tf_op jit(solution)/shard_map/ppermute | solution.py:498
  56.3 0.0 copy-done.5
  56.3 0.0 copy-start.6
  56.3 0.6 %copy-done.6 = f32[1,2048]{1,0:T(1,128)} copy-done((f32[1,2048]{1,0:T(1,128)}, f32[1,2048]{1,0:T(1,128)S(1)}, u32[]{:S(2)}) %copy-start.6) | copy-done | bytes 8216
  56.9 0.0 collective-permute-done.7.refs_1_
  56.9 1.8 %finish.1 = (f32[3,7,2048]{2,1,0:T(8,128)}, f32[128,128]{1,0:T(8,128)}) custom-call(f32[16,2048]{1,0:T(8,128)} %copy-done, f32[16,2048]{1,0:T(8,128)} %copy-done.3, f32[1,2048]{1,0:T(1,128)} %bitcast.4, f32[1,2048]{1,0:T(1,128)} %collective-permute-done.7.refs_1_, f32[1,2048]{1,0:T(1,128)} %copy-done.6, f32[1,2048]{1,0:T(1,128)} %copy-done.5), custom_call_target="tpu_custom_call" | custom-call | tf_op jit(solution)/shard_map/finish/pallas_call | solution.py:470
  (3 shorter events, 0.1 us)
Async XLA Ops:
  5.4 6.9 %collective-permute-start = (bf16[160,2048]{1,0:T(8,128)(2,1)}, bf16[160,2048]{1,0:T(8,128)(2,1)S(1)}, u32[]{:S(2)}, u32[]{:S(2)}) collective-permute-start(bf16[160,2048]{1,0:T(8,128)(2,1)} %get-tuple-element.14), channel_id=1, source_target_pairs={{0,4},{4,0},{8,12},{12,8},{16,20},{20,16},{24,28},{28,24},{1,5},{5... | collective-permute-start | bytes 1966088 | tf_op jit(solution)/shard_map/ppermute | solution.py:530
  5.9 6.4 %collective-permute-start.1 = (bf16[160,2048]{1,0:T(8,128)(2,1)}, bf16[160,2048]{1,0:T(8,128)(2,1)S(1)}, u32[]{:S(2)}, u32[]{:S(2)}) collective-permute-start(bf16[160,2048]{1,0:T(8,128)(2,1)} %get-tuple-element.15), channel_id=1, source_target_pairs={{4,8},{8,4},{12,16},{16,12},{20,24},{24,20},{5,9},{9,5},{13,17},{1... | collective-permute-start | bytes 1966088 | tf_op jit(solution)/shard_map/ppermute | solution.py:531
  12.3 0.8 %copy-start.1 = (bf16[160,2048]{1,0:T(8,128)(2,1)}, bf16[160,2048]{1,0:T(8,128)(2,1)S(1)}, u32[]{:S(2)}) copy-start(bf16[160,2048]{1,0:T(8,128)(2,1)S(1)} %collective-permute-done.near) | copy-start | bytes 1966084
  12.3 1.1 %copy-start.2 = (bf16[160,2048]{1,0:T(8,128)(2,1)}, bf16[160,2048]{1,0:T(8,128)(2,1)S(1)}, u32[]{:S(2)}) copy-start(bf16[160,2048]{1,0:T(8,128)(2,1)S(1)} %collective-permute-done.1.far) | copy-start | bytes 1966084
  30.6 7.3 %collective-permute-start.2 = (bf16[16,2048]{1,0:T(8,128)(2,1)S(1)}, bf16[16,2048]{1,0:T(8,128)(2,1)S(1)}, u32[]{:S(2)}, u32[]{:S(2)}) collective-permute-start(bf16[16,2048]{1,0:T(8,128)(2,1)S(1)} %get-tuple-element.22), channel_id=1, source_target_pairs={{0,4},{4,0},{8,12},{12,8},{16,20},{20,16},{24,28},{28,24},{1,5},{5... | collective-permute-start | bytes 196616 | tf_op jit(solution)/shard_map/ppermute | solution.py:498
  37.9 6.6 %collective-permute-start.5 = (bf16[16,2048]{1,0:T(8,128)(2,1)S(1)}, bf16[16,2048]{1,0:T(8,128)(2,1)S(1)}, u32[]{:S(2)}, u32[]{:S(2)}) collective-permute-start(bf16[16,2048]{1,0:T(8,128)(2,1)S(1)} %add_convert_fusion), channel_id=1, source_target_pairs={{0,24},{4,28},{8,16},{12,20},{16,8},{20,12},{24,0},{28,4},{1,25},{... | collective-permute-start | bytes 196616 | tf_op jit(solution)/shard_map/ppermute | solution.py:498
  42.0 6.1 %collective-permute-start.4 = (bf16[16,2048]{1,0:T(8,128)(2,1)S(1)}, bf16[16,2048]{1,0:T(8,128)(2,1)S(1)}, u32[]{:S(2)}, u32[]{:S(2)}) collective-permute-start(bf16[16,2048]{1,0:T(8,128)(2,1)S(1)} %add_convert_fusion), channel_id=1, source_target_pairs={{0,16},{4,20},{8,24},{12,28},{16,0},{20,4},{24,8},{28,12},{1,17},{... | collective-permute-start | bytes 196616 | tf_op jit(solution)/shard_map/ppermute | solution.py:498
  42.0 6.1 %collective-permute-start.3 = (bf16[16,2048]{1,0:T(8,128)(2,1)S(1)}, bf16[16,2048]{1,0:T(8,128)(2,1)S(1)}, u32[]{:S(2)}, u32[]{:S(2)}) collective-permute-start(bf16[16,2048]{1,0:T(8,128)(2,1)S(1)} %add_convert_fusion), channel_id=1, source_target_pairs={{0,8},{4,12},{8,0},{12,4},{16,24},{20,28},{24,16},{28,20},{1,9},{5... | collective-permute-start | bytes 196616 | tf_op jit(solution)/shard_map/ppermute | solution.py:498
  48.1 1.4 %copy-start = (f32[16,2048]{1,0:T(8,128)}, f32[16,2048]{1,0:T(8,128)S(1)}, u32[]{:S(2)}) copy-start(f32[16,2048]{1,0:T(8,128)S(1)} %add_add_fusion.own) | copy-start | bytes 393220
  48.2 1.4 %collective-permute-start.6 = (f32[16,2048]{1,0:T(8,128)S(1)}, f32[16,2048]{1,0:T(8,128)S(1)}, u32[]{:S(2)}, u32[]{:S(2)}) collective-permute-start(f32[16,2048]{1,0:T(8,128)S(1)} %add_add_fusion.own), channel_id=1, source_target_pairs={{0,4},{4,0},{8,12},{12,8},{16,20},{20,16},{24,28},{28,24},{1,5},{5... | collective-permute-start | bytes 393224 | tf_op jit(solution)/shard_map/ppermute | solution.py:498
  49.6 0.7 %copy-start.3 = (f32[16,2048]{1,0:T(8,128)}, f32[16,2048]{1,0:T(8,128)S(1)}, u32[]{:S(2)}) copy-start(f32[16,2048]{1,0:T(8,128)S(1)} %collective-permute-done.6.other) | copy-start | bytes 393220
  50.2 3.0 %copy-start.4 = (f32[2048]{0:T(1024)}, f32[2048]{0:T(1024)S(1)}, u32[]{:S(2)}) copy-start(f32[2048]{0:T(1024)S(1)} %add_reduce_fusion) | copy-start | bytes 24580
  50.2 4.5 %collective-permute-start.9 = (f32[1,2048]{1,0:T(1,128)S(1)}, f32[1,2048]{1,0:T(1,128)S(1)}, u32[]{:S(2)}, u32[]{:S(2)}) collective-permute-start(f32[1,2048]{1,0:T(1,128)S(1)} %bitcast.1), channel_id=1, source_target_pairs={{0,3},{1,2},{2,1},{3,0},{4,7},{5,6},{6,5},{7,4},{8,11},{9,10},{10,... | collective-permute-start | bytes 24584 | tf_op jit(solution)/shard_map/ppermute | solution.py:498
  52.7 3.7 %collective-permute-start.8 = (f32[1,2048]{1,0:T(1,128)S(1)}, f32[1,2048]{1,0:T(1,128)S(1)}, u32[]{:S(2)}, u32[]{:S(2)}) collective-permute-start(f32[1,2048]{1,0:T(1,128)S(1)} %bitcast.2), channel_id=1, source_target_pairs={{0,2},{1,3},{2,0},{3,1},{4,6},{5,7},{6,4},{7,5},{8,10},{9,11},{10,... | collective-permute-start | bytes 24584 | tf_op jit(solution)/shard_map/ppermute | solution.py:498
  53.2 3.8 %collective-permute-start.7 = (f32[1,2048]{1,0:T(1,128)S(1)}, f32[1,2048]{1,0:T(1,128)}, u32[]{:S(2)}, u32[]{:S(2)}) collective-permute-start(f32[1,2048]{1,0:T(1,128)S(1)} %bitcast.3), channel_id=1, source_target_pairs={{0,1},{1,0},{2,3},{3,2},{4,5},{5,4},{6,7},{7,6},{8,9},{9,8},{10,11... | collective-permute-start | bytes 24584 | tf_op jit(solution)/shard_map/ppermute | solution.py:498
  54.8 1.5 %copy-start.5 = (f32[1,2048]{1,0:T(1,128)}, f32[1,2048]{1,0:T(1,128)S(1)}, u32[]{:S(2)}) copy-start(f32[1,2048]{1,0:T(1,128)S(1)} %collective-permute-done.9.refs_3_) | copy-start | bytes 24580
  56.3 0.6 %copy-start.6 = (f32[1,2048]{1,0:T(1,128)}, f32[1,2048]{1,0:T(1,128)S(1)}, u32[]{:S(2)}) copy-start(f32[1,2048]{1,0:T(1,128)S(1)} %collective-permute-done.8.refs_2_) | copy-start | bytes 24580

commit v6 on v5

--- a/solution.py
+++ b/solution.py
@@ -6,6 +6,7 @@
 from jax.experimental import pallas as pl
 from jax.experimental.pallas import tpu as pltpu
 from jax.sharding import PartitionSpec as P
+
 
 D = 8192
 G = 512
@@ -155,7 +156,7 @@
                 live.remove(job)
 
 
-def own_kernel(span, feat, cot, filt, ks_out, vs_out, z_out, dy_out, qx, kx, vx):
+def own_kernel(feat, cot, filt, ks_out, vs_out, z_out, dy_out, qx, kx, vx):
     rows = feat.shape[1]
     width = feat.shape[2]
 
@@ -193,14 +194,14 @@
     return pl.BlockSpec(shape + (step,), lambda i: (0,) * len(shape) + (i,))
 
 
-def own_part(features, cotangent, short_filter, span):
+def own_part(features, cotangent, short_filter):
     _, rows, width = features.shape
     taps = short_filter.shape[1]
     step = min(width, 512)
     column = functools.partial(column_spec, step)
     kinds = [F32, F32, BF16, BF16]
     return pl.pallas_call(
-        functools.partial(own_kernel, span),
+        own_kernel,
         grid=(width // step,),
         in_specs=[column(3, rows), column(rows), column(3, taps)],
         out_specs=[column(rows)] * 4,
@@ -244,7 +245,7 @@
         return pl.ds(i * LANES, LANES)
 
     def prepare(i, bufs, state):
-        qx, kx, vx, zx, dyx, dqx, dkx, dvx, tst, ust, zm, pairs = bufs
+        qx, kx, vx, zx, dyx, _, _, _, tst, ust, _, _ = bufs
         lanes = column(i)
         fq, fk, fv = (taps_of(filt, a, lanes) for a in range(3))
 
@@ -293,7 +294,7 @@
             yield False
 
     def multiply(i, bufs, state):
-        qx, kx, vx, zx, dyx, dqx, dkx, dvx, tst, ust, zm, pairs = bufs
+        _, _, _, zx, dyx, dqx, dkx, dvx, tst, ust, zm, pairs = bufs
         lanes = column(i)
         c_next, ks_first, vs_first, ks_next, vs_next = state.pop(i)
         owner = owners(members, blocks)
@@ -350,7 +351,7 @@
         pairs[...] = dot(zm[...], near_rows, ((1,), (1,)))
 
     def second_stage(i, bufs):
-        qx, kx, vx, zx, dyx, dqx, dkx, dvx, tst, ust, zm, pairs = bufs
+        _, _, _, _, _, dqx, dkx, dvx, _, _, _, pairs = bufs
         lanes = column(i)
         left = list(range(per))
 
@@ -520,17 +521,16 @@
 
 
 def on_device(features, short_filter, long_filter, cotangent):
-    _, rows, width = features.shape
+    _, _, width = features.shape
     taps = short_filter.shape[1]
     groups, span = long_filter.shape
     members = width // groups
     size = lax.axis_size("ctx")
     near, far = edges(features, cotangent, short_filter, span)
-    got = (
-        lax.ppermute(near, "ctx", [(i, i ^ 1) for i in range(size)]),
-        lax.ppermute(far, "ctx", [(i, (i + 1 ^ 1) - 1) for i in range(1, size - 1)]),
-    )
-    parts = own_part(features, cotangent, short_filter, span)
+    far = lax.ppermute(far, "ctx", [(i, (i + 1 ^ 1) - 1) for i in range(1, size - 1)])
+    near = lax.ppermute(near, "ctx", [(i, i ^ 1) for i in range(size)])
+    got = (near, far)
+    parts = own_part(features, cotangent, short_filter)
     grads, keep, send = join(
         features, cotangent, got, short_filter, long_filter, parts, span, members
     )

time: 59 us -> 59 us (level)
  no operation moved by 1% of the time
where the time goes in v6:
time: 59 us; the launch traced here: 58.8 us
  Pallas kernels  29.5 us (50%)
  starting transfers between devices  15.8 us (27%)
  waiting for transfers between devices  10.4 us (18%)
  local copies, waits for them, and re-layouts  2.29 us (4%)
  between operations  0.72 us (1%)
    pallas_call x1, Pallas kernels, join(): pl.pallas_call(functools.partial(join_kernel, span, members), grid=(width...  17.2 us
    ppermute x8, starting transfers between devices, swap(): return lax.ppermute(value, axis, route)  14.7 us
    ppermute x8, waiting for transfers between devices, swap(): return lax.ppermute(value, axis, route)  10.3 us
    pallas_call x1, Pallas kernels, own_part(): pl.pallas_call(own_kernel, grid=(width // step,), in_specs=[column(3, row...  5.69 us
    pallas_call x1, Pallas kernels, edges(): pl.pallas_call(functools.partial(edge_kernel, span), grid=(width // step,...  4.74 us
    unnamed x14, local copies, waits for them, and re-layouts  2.29 us
    pallas_call x1, Pallas kernels, finish(): pl.pallas_call(functools.partial(finish_kernel, count), out_shape=[jax.Sh...  1.81 us
  transfers between devices with their start and end apart: 10, of which 6 were waited for; matrix products, arithmetic and copies ran while one was open for 0% of the time, Pallas kernels for 10%

profile of v6, /device:TPU:0, one launch (start us, length us, event | category | flops | bytes accessed | tf_op | source)
XLA Modules:
  0.0 58.8 jit_solution(5618438075875502118)
XLA Ops:
  0.6 4.7 %edges.1 = (bf16[160,2048]{1,0:T(8,128)(2,1)}, bf16[160,2048]{1,0:T(8,128)(2,1)}) custom-call(bf16[3,256,2048]{2,1,0:T(8,128)(2,1)} %feat.5, bf16[256,2048]{1,0:T(8,128)(2,1)} %cot.5, f32[3,7,2048]{2,1,0:T(8,128)} %filt.5), custom_call_target="tpu_custom_call" | custom-call | tf_op jit(solution)/shard_map/edges/pallas_call | solution.py:88
  5.4 0.5 collective-permute-start
  5.9 0.7 %collective-permute-start.1 = (bf16[160,2048]{1,0:T(8,128)(2,1)}, bf16[160,2048]{1,0:T(8,128)(2,1)S(1)}, u32[]{:S(2)}, u32[]{:S(2)}) collective-permute-start(bf16[160,2048]{1,0:T(8,128)(2,1)} %get-tuple-element.15), channel_id=1, source_target_pairs={{4,8},{8,4},{12,16},{16,12},{20,24},{24,20},{5,9},{9,5},{13,17},{1... | collective-permute-start | bytes 1966088 | tf_op jit(solution)/shard_map/ppermute | solution.py:530
  6.6 5.7 %own.1 = (f32[256,2048]{1,0:T(8,128)S(1)}, f32[256,2048]{1,0:T(8,128)S(1)}, bf16[256,2048]{1,0:T(8,128)(2,1)S(1)}, bf16[256,2048]{1,0:T(8,128)(2,1)S(1)}) custom-call(bf16[3,256,2048]{2,1,0:T(8,128)(2,1)} %feat.5, bf16[256,2048]{1,0:T(8,128)(2,1)} %cot.5, f32[3,7,2048]{2,1,0:T(8,128)} %filt.5), custom_call_target="tpu_custom_call" | custom-call | flops 20971520 | bytes 10485760 | tf_op jit(solution)/shard_map/own/pallas_call | solution.py:203
  12.3 0.0 collective-permute-done.near
  12.3 0.0 copy-start.1
  12.3 0.0 collective-permute-done.1.far
  12.3 0.0 copy-start.2
  12.3 0.8 %copy-done.1 = bf16[160,2048]{1,0:T(8,128)(2,1)} copy-done((bf16[160,2048]{1,0:T(8,128)(2,1)}, bf16[160,2048]{1,0:T(8,128)(2,1)S(1)}, u32[]{:S(2)}) %copy-start.1) | copy-done | bytes 655384
  13.1 0.3 copy-done.2
  13.4 17.2 %join.1 = (bf16[3,256,2048]{2,1,0:T(8,128)(2,1)}, bf16[16,2048]{1,0:T(8,128)(2,1)S(1)}, bf16[16,2048]{1,0:T(8,128)(2,1)S(1)}) custom-call(bf16[3,256,2048]{2,1,0:T(8,128)(2,1)} %feat.5, bf16[256,2048]{1,0:T(8,128)(2,1)} %cot.5, bf16[160,2048]{1,0:T(8,128)(2,1)} %copy-done.1, bf16[160,2048]{1,0:T(8,128)(2,1)} %copy-done.2, f32[3,7,2048]{2,1,0:T(8,128)} %filt.5, ...), custom_call_target="tpu_custom_call" | custom-call | tf_op jit(solution)/shard_map/join/pallas_call | solution.py:415
  30.6 6.4 %collective-permute-start.2 = (bf16[16,2048]{1,0:T(8,128)(2,1)S(1)}, bf16[16,2048]{1,0:T(8,128)(2,1)S(1)}, u32[]{:S(2)}, u32[]{:S(2)}) collective-permute-start(bf16[16,2048]{1,0:T(8,128)(2,1)S(1)} %get-tuple-element.22), channel_id=1, source_target_pairs={{0,4},{4,0},{8,12},{12,8},{16,20},{20,16},{24,28},{28,24},{1,5},{5... | collective-permute-start | bytes 196616 | tf_op jit(solution)/shard_map/ppermute | solution.py:499
  37.0 0.9 %collective-permute-done.2 = bf16[16,2048]{1,0:T(8,128)(2,1)S(1)} collective-permute-done((bf16[16,2048]{1,0:T(8,128)(2,1)S(1)}, bf16[16,2048]{1,0:T(8,128)(2,1)S(1)}, u32[]{:S(2)}, u32[]{:S(2)}) %collective-permute-start.2) | collective-permute-done | bytes 65568 | tf_op jit(solution)/shard_map/ppermute | solution.py:499
  37.9 4.1 %collective-permute-start.5 = (bf16[16,2048]{1,0:T(8,128)(2,1)S(1)}, bf16[16,2048]{1,0:T(8,128)(2,1)S(1)}, u32[]{:S(2)}, u32[]{:S(2)}) collective-permute-start(bf16[16,2048]{1,0:T(8,128)(2,1)S(1)} %add_convert_fusion), channel_id=1, source_target_pairs={{0,24},{4,28},{8,16},{12,20},{16,8},{20,12},{24,0},{28,4},{1,25},{... | collective-permute-start | bytes 196616 | tf_op jit(solution)/shard_map/ppermute | solution.py:499
  42.0 0.0 collective-permute-start.4
  42.0 0.6 %collective-permute-start.3 = (bf16[16,2048]{1,0:T(8,128)(2,1)S(1)}, bf16[16,2048]{1,0:T(8,128)(2,1)S(1)}, u32[]{:S(2)}, u32[]{:S(2)}) collective-permute-start(bf16[16,2048]{1,0:T(8,128)(2,1)S(1)} %add_convert_fusion), channel_id=1, source_target_pairs={{0,8},{4,12},{8,0},{12,4},{16,24},{20,28},{24,16},{28,20},{1,9},{5... | collective-permute-start | bytes 196616 | tf_op jit(solution)/shard_map/ppermute | solution.py:499
  42.6 1.9 %collective-permute-done.5 = bf16[16,2048]{1,0:T(8,128)(2,1)S(1)} collective-permute-done((bf16[16,2048]{1,0:T(8,128)(2,1)S(1)}, bf16[16,2048]{1,0:T(8,128)(2,1)S(1)}, u32[]{:S(2)}, u32[]{:S(2)}) %collective-permute-start.5) | collective-permute-done | bytes 65568 | tf_op jit(solution)/shard_map/ppermute | solution.py:499
  44.5 3.6 %collective-permute-done.4 = bf16[16,2048]{1,0:T(8,128)(2,1)S(1)} collective-permute-done((bf16[16,2048]{1,0:T(8,128)(2,1)S(1)}, bf16[16,2048]{1,0:T(8,128)(2,1)S(1)}, u32[]{:S(2)}, u32[]{:S(2)}) %collective-permute-start.4) | collective-permute-done | bytes 65568 | tf_op jit(solution)/shard_map/ppermute | solution.py:499
  48.1 0.0 collective-permute-done.3
  48.1 0.0 copy-start
  48.2 0.1 collective-permute-start.6
  48.2 1.3 %collective-permute-done.6.other = f32[16,2048]{1,0:T(8,128)S(1)} collective-permute-done((f32[16,2048]{1,0:T(8,128)S(1)}, f32[16,2048]{1,0:T(8,128)S(1)}, u32[]{:S(2)}, u32[]{:S(2)}) %collective-permute-start.6) | collective-permute-done | bytes 131104 | tf_op jit(solution)/shard_map/ppermute | solution.py:499
  49.6 0.0 copy-done
  49.6 0.0 copy-start.3
  49.6 0.6 %copy-done.3 = f32[16,2048]{1,0:T(8,128)} copy-done((f32[16,2048]{1,0:T(8,128)}, f32[16,2048]{1,0:T(8,128)S(1)}, u32[]{:S(2)}) %copy-start.3) | copy-done | bytes 131096
  50.2 0.0 copy-start.4
  50.2 2.4 %collective-permute-start.9 = (f32[1,2048]{1,0:T(1,128)S(1)}, f32[1,2048]{1,0:T(1,128)S(1)}, u32[]{:S(2)}, u32[]{:S(2)}) collective-permute-start(f32[1,2048]{1,0:T(1,128)S(1)} %bitcast.1), channel_id=1, source_target_pairs={{0,3},{1,2},{2,1},{3,0},{4,7},{5,6},{6,5},{7,4},{8,11},{9,10},{10,... | collective-permute-start | bytes 24584 | tf_op jit(solution)/shard_map/ppermute | solution.py:499
  52.7 0.5 collective-permute-start.8
  53.2 0.0 copy-done.4
  53.2 0.5 collective-permute-start.7
  53.7 1.1 %collective-permute-done.9.refs_3_ = f32[1,2048]{1,0:T(1,128)S(1)} collective-permute-done((f32[1,2048]{1,0:T(1,128)S(1)}, f32[1,2048]{1,0:T(1,128)S(1)}, u32[]{:S(2)}, u32[]{:S(2)}) %collective-permute-start.9) | collective-permute-done | bytes 8224 | tf_op jit(solution)/shard_map/ppermute | solution.py:499
  54.8 0.0 copy-start.5
  54.8 1.5 %collective-permute-done.8.refs_2_ = f32[1,2048]{1,0:T(1,128)S(1)} collective-permute-done((f32[1,2048]{1,0:T(1,128)S(1)}, f32[1,2048]{1,0:T(1,128)S(1)}, u32[]{:S(2)}, u32[]{:S(2)}) %collective-permute-start.8) | collective-permute-done | bytes 8224 | tf_op jit(solution)/shard_map/ppermute | solution.py:499
  56.3 0.0 copy-done.5
  56.3 0.0 copy-start.6
  56.3 0.6 %copy-done.6 = f32[1,2048]{1,0:T(1,128)} copy-done((f32[1,2048]{1,0:T(1,128)}, f32[1,2048]{1,0:T(1,128)S(1)}, u32[]{:S(2)}) %copy-start.6) | copy-done | bytes 8216
  56.9 0.0 collective-permute-done.7.refs_1_
  56.9 1.8 %finish.1 = (f32[3,7,2048]{2,1,0:T(8,128)}, f32[128,128]{1,0:T(8,128)}) custom-call(f32[16,2048]{1,0:T(8,128)} %copy-done, f32[16,2048]{1,0:T(8,128)} %copy-done.3, f32[1,2048]{1,0:T(1,128)} %bitcast.4, f32[1,2048]{1,0:T(1,128)} %collective-permute-done.7.refs_1_, f32[1,2048]{1,0:T(1,128)} %copy-done.6, f32[1,2048]{1,0:T(1,128)} %copy-done.5), custom_call_target="tpu_custom_call" | custom-call | tf_op jit(solution)/shard_map/finish/pallas_call | solution.py:471
  (3 shorter events, 0.1 us)
Async XLA Ops:
  5.4 6.9 %collective-permute-start = (bf16[160,2048]{1,0:T(8,128)(2,1)}, bf16[160,2048]{1,0:T(8,128)(2,1)S(1)}, u32[]{:S(2)}, u32[]{:S(2)}) collective-permute-start(bf16[160,2048]{1,0:T(8,128)(2,1)} %get-tuple-element.14), channel_id=1, source_target_pairs={{0,4},{4,0},{8,12},{12,8},{16,20},{20,16},{24,28},{28,24},{1,5},{5... | collective-permute-start | bytes 1966088 | tf_op jit(solution)/shard_map/ppermute | solution.py:531
  5.9 6.4 %collective-permute-start.1 = (bf16[160,2048]{1,0:T(8,128)(2,1)}, bf16[160,2048]{1,0:T(8,128)(2,1)S(1)}, u32[]{:S(2)}, u32[]{:S(2)}) collective-permute-start(bf16[160,2048]{1,0:T(8,128)(2,1)} %get-tuple-element.15), channel_id=1, source_target_pairs={{4,8},{8,4},{12,16},{16,12},{20,24},{24,20},{5,9},{9,5},{13,17},{1... | collective-permute-start | bytes 1966088 | tf_op jit(solution)/shard_map/ppermute | solution.py:530
  12.3 0.8 %copy-start.1 = (bf16[160,2048]{1,0:T(8,128)(2,1)}, bf16[160,2048]{1,0:T(8,128)(2,1)S(1)}, u32[]{:S(2)}) copy-start(bf16[160,2048]{1,0:T(8,128)(2,1)S(1)} %collective-permute-done.near) | copy-start | bytes 1966084
  12.3 1.1 %copy-start.2 = (bf16[160,2048]{1,0:T(8,128)(2,1)}, bf16[160,2048]{1,0:T(8,128)(2,1)S(1)}, u32[]{:S(2)}) copy-start(bf16[160,2048]{1,0:T(8,128)(2,1)S(1)} %collective-permute-done.1.far) | copy-start | bytes 1966084
  30.6 7.3 %collective-permute-start.2 = (bf16[16,2048]{1,0:T(8,128)(2,1)S(1)}, bf16[16,2048]{1,0:T(8,128)(2,1)S(1)}, u32[]{:S(2)}, u32[]{:S(2)}) collective-permute-start(bf16[16,2048]{1,0:T(8,128)(2,1)S(1)} %get-tuple-element.22), channel_id=1, source_target_pairs={{0,4},{4,0},{8,12},{12,8},{16,20},{20,16},{24,28},{28,24},{1,5},{5... | collective-permute-start | bytes 196616 | tf_op jit(solution)/shard_map/ppermute | solution.py:499
  37.9 6.6 %collective-permute-start.5 = (bf16[16,2048]{1,0:T(8,128)(2,1)S(1)}, bf16[16,2048]{1,0:T(8,128)(2,1)S(1)}, u32[]{:S(2)}, u32[]{:S(2)}) collective-permute-start(bf16[16,2048]{1,0:T(8,128)(2,1)S(1)} %add_convert_fusion), channel_id=1, source_target_pairs={{0,24},{4,28},{8,16},{12,20},{16,8},{20,12},{24,0},{28,4},{1,25},{... | collective-permute-start | bytes 196616 | tf_op jit(solution)/shard_map/ppermute | solution.py:499
  42.0 6.1 %collective-permute-start.4 = (bf16[16,2048]{1,0:T(8,128)(2,1)S(1)}, bf16[16,2048]{1,0:T(8,128)(2,1)S(1)}, u32[]{:S(2)}, u32[]{:S(2)}) collective-permute-start(bf16[16,2048]{1,0:T(8,128)(2,1)S(1)} %add_convert_fusion), channel_id=1, source_target_pairs={{0,16},{4,20},{8,24},{12,28},{16,0},{20,4},{24,8},{28,12},{1,17},{... | collective-permute-start | bytes 196616 | tf_op jit(solution)/shard_map/ppermute | solution.py:499
  42.0 6.1 %collective-permute-start.3 = (bf16[16,2048]{1,0:T(8,128)(2,1)S(1)}, bf16[16,2048]{1,0:T(8,128)(2,1)S(1)}, u32[]{:S(2)}, u32[]{:S(2)}) collective-permute-start(bf16[16,2048]{1,0:T(8,128)(2,1)S(1)} %add_convert_fusion), channel_id=1, source_target_pairs={{0,8},{4,12},{8,0},{12,4},{16,24},{20,28},{24,16},{28,20},{1,9},{5... | collective-permute-start | bytes 196616 | tf_op jit(solution)/shard_map/ppermute | solution.py:499
  48.1 1.4 %copy-start = (f32[16,2048]{1,0:T(8,128)}, f32[16,2048]{1,0:T(8,128)S(1)}, u32[]{:S(2)}) copy-start(f32[16,2048]{1,0:T(8,128)S(1)} %add_add_fusion.own) | copy-start | bytes 393220
  48.2 1.4 %collective-permute-start.6 = (f32[16,2048]{1,0:T(8,128)S(1)}, f32[16,2048]{1,0:T(8,128)S(1)}, u32[]{:S(2)}, u32[]{:S(2)}) collective-permute-start(f32[16,2048]{1,0:T(8,128)S(1)} %add_add_fusion.own), channel_id=1, source_target_pairs={{0,4},{4,0},{8,12},{12,8},{16,20},{20,16},{24,28},{28,24},{1,5},{5... | collective-permute-start | bytes 393224 | tf_op jit(solution)/shard_map/ppermute | solution.py:499
  49.6 0.7 %copy-start.3 = (f32[16,2048]{1,0:T(8,128)}, f32[16,2048]{1,0:T(8,128)S(1)}, u32[]{:S(2)}) copy-start(f32[16,2048]{1,0:T(8,128)S(1)} %collective-permute-done.6.other) | copy-start | bytes 393220
  50.2 3.0 %copy-start.4 = (f32[2048]{0:T(1024)}, f32[2048]{0:T(1024)S(1)}, u32[]{:S(2)}) copy-start(f32[2048]{0:T(1024)S(1)} %add_reduce_fusion) | copy-start | bytes 24580
  50.2 4.5 %collective-permute-start.9 = (f32[1,2048]{1,0:T(1,128)S(1)}, f32[1,2048]{1,0:T(1,128)S(1)}, u32[]{:S(2)}, u32[]{:S(2)}) collective-permute-start(f32[1,2048]{1,0:T(1,128)S(1)} %bitcast.1), channel_id=1, source_target_pairs={{0,3},{1,2},{2,1},{3,0},{4,7},{5,6},{6,5},{7,4},{8,11},{9,10},{10,... | collective-permute-start | bytes 24584 | tf_op jit(solution)/shard_map/ppermute | solution.py:499
  52.7 3.7 %collective-permute-start.8 = (f32[1,2048]{1,0:T(1,128)S(1)}, f32[1,2048]{1,0:T(1,128)S(1)}, u32[]{:S(2)}, u32[]{:S(2)}) collective-permute-start(f32[1,2048]{1,0:T(1,128)S(1)} %bitcast.2), channel_id=1, source_target_pairs={{0,2},{1,3},{2,0},{3,1},{4,6},{5,7},{6,4},{7,5},{8,10},{9,11},{10,... | collective-permute-start | bytes 24584 | tf_op jit(solution)/shard_map/ppermute | solution.py:499
  53.2 3.8 %collective-permute-start.7 = (f32[1,2048]{1,0:T(1,128)S(1)}, f32[1,2048]{1,0:T(1,128)}, u32[]{:S(2)}, u32[]{:S(2)}) collective-permute-start(f32[1,2048]{1,0:T(1,128)S(1)} %bitcast.3), channel_id=1, source_target_pairs={{0,1},{1,0},{2,3},{3,2},{4,5},{5,4},{6,7},{7,6},{8,9},{9,8},{10,11... | collective-permute-start | bytes 24584 | tf_op jit(solution)/shard_map/ppermute | solution.py:499
  54.8 1.5 %copy-start.5 = (f32[1,2048]{1,0:T(1,128)}, f32[1,2048]{1,0:T(1,128)S(1)}, u32[]{:S(2)}) copy-start(f32[1,2048]{1,0:T(1,128)S(1)} %collective-permute-done.9.refs_3_) | copy-start | bytes 24580
  56.3 0.6 %copy-start.6 = (f32[1,2048]{1,0:T(1,128)}, f32[1,2048]{1,0:T(1,128)S(1)}, u32[]{:S(2)}) copy-start(f32[1,2048]{1,0:T(1,128)S(1)} %collective-permute-done.8.refs_2_) | copy-start | bytes 24580
